TPU v7x, 32 devices: a whole 2x2x4 slice. The times are simulated.
32 devices in a mesh: rows: 8 (over z, y), sub: 4 (over x, core).
Axes of the slice: x: 2, y: 2, z: 4, core: 2. Of those that a mesh axis runs over, the one named last changes fastest.
Arguments:
- stiffness_tiles: bfloat16 [8, 4, 128, 128, 128], P('rows', 'sub'), may hold values from -0.5 to 0.5
- damping_tiles: bfloat16 [8, 4, 128, 128, 128], P('rows', 'sub'), may hold values from -0.5 to 0.5
- tile_map: int32 [8, 4, 2, 128], P('rows', 'sub'), may hold values from -1 to 767, as said below
- inv_mass: float32 [262144], P(('rows', 'sub')), may hold values from 0.5 to 2
- spectral_shift: float32 [], replicated, may hold values from 0.5 to 1.5
- basis: float32 [58, 262144], P(None, ('rows', 'sub')), may hold values from -20 to 20
- compact: float32 [2, 58, 57], replicated, may hold values from -0.54 to 0.54
Outputs:
- new_basis: float32 [2, 262144], P(None, ('rows', 'sub'))
- compact_out: float32 [2, 60, 59], replicated
- hessenberg: float32 [59, 2], replicated
Inputs may be any that keep to these rules, and one draw needn't show every extreme that they name: tile_map[r, s, 0, t] is the tile row of part r that slot t adds to, or -1 for an unused slot; the used slots of a device come first, and some device uses all 128. tile_map[r, s, 1, t] is the source column tile counted from the start of part r - 1.
All inputs are finite; a program needn't handle non-finite values.
Results may differ from a plain program's by a relative error of at most 0.0033.
Values may be sent and summed in bfloat16 or wider, within the bound.
No kernel may reach another device: no remote copies, remote signals or barrier semaphores. Data moves between devices by JAX's collectives and lax.ppermute only.
A program may use at most 64 MiB of HBM per device.

v0:
```python
import jax
import jax.numpy as jnp
from jax import lax
from jax.sharding import PartitionSpec as P

ITERS = 2


precise = lax.Precision.HIGHEST


def padded(array, sides, width):
    for axis, dim in sides:
        devices, length = (lax.axis_size(axis), array.shape[dim])
        up = [(i, (i + 1) % devices) for i in range(devices - 1)]
        down = [(j, i) for i, j in up]
        last = lax.slice_in_dim(array, length - width, length, axis=dim)
        initial = lax.slice_in_dim(array, 0, width, axis=dim)
        before = lax.ppermute(last, axis, up)
        after = lax.ppermute(initial, axis, down)
        array = jnp.concatenate([before, array, after], axis=dim)
    return array


def compact_update(upper_half, lower_half, coefficients, norm_value, lower_tail):
    columns = upper_half.shape[1]
    zero_row = jnp.zeros((1, columns), upper_half.dtype)
    upper_ext = jnp.concatenate([upper_half, zero_row], 0)
    lower_ext = jnp.concatenate([lower_half, zero_row], 0)
    upper_coeffs = jnp.concatenate([coefficients, norm_value[None]])
    lower_coeffs = jnp.concatenate([lower_tail, jnp.zeros((1,), lower_tail.dtype)])
    weights = jnp.zeros((columns,), upper_half.dtype)
    for repeat_index in range(2):
        projection = jnp.dot(upper_coeffs, upper_ext, precision=precise) + jnp.dot(
            lower_coeffs, lower_ext, precision=precise
        )
        upper_coeffs = upper_coeffs - jnp.dot(upper_ext, projection, precision=precise)
        lower_coeffs = lower_coeffs - jnp.dot(lower_ext, projection, precision=precise)
        weights = weights + projection
    beta_norm = jnp.sqrt(
        jnp.sum(upper_coeffs * upper_coeffs) + jnp.sum(lower_coeffs * lower_coeffs) + 1e-06
    )
    upper_new = jnp.concatenate([upper_ext, (upper_coeffs / beta_norm)[:, None]], 1)
    lower_new = jnp.concatenate([lower_ext, (lower_coeffs / beta_norm)[:, None]], 1)
    return (upper_new, lower_new, weights, beta_norm)


def tile_products(damping, stiffness, target, source, blocked, tile_rows):
    picked_damp = blocked[0][source]
    picked_stiff = blocked[1][source]
    product = jnp.einsum("sij,sj->si", damping, picked_damp, preferred_element_type=jnp.float32)
    product = product + jnp.einsum(
        "sij,sj->si", stiffness, picked_stiff, preferred_element_type=jnp.float32
    )
    selector = (target[None, :] == jnp.arange(tile_rows, dtype=jnp.int32)[:, None]).astype(
        jnp.float32
    )
    return jnp.dot(selector, product, precision=precise)


def on_device(stiffness_tiles, damping_tiles, tile_map, inv_mass, spectral_shift, basis, compact):
    rows_count = lax.axis_size("rows")
    sub_count = lax.axis_size("sub")
    tile_size = stiffness_tiles.shape[-1]
    local_rows = basis.shape[1]
    part_rows = sub_count * local_rows
    tile_rows = part_rows // tile_size
    unknowns = local_rows * rows_count * sub_count
    target = tile_map[0, 0, 0]
    source = tile_map[0, 0, 1]
    damping = damping_tiles[0, 0]
    stiffness = stiffness_tiles[0, 0]
    held = basis
    upper_half = compact[0]
    lower_half = compact[1]
    new_columns = []
    hess_columns = []
    for iteration in range(ITERS):
        upper_last = upper_half[:, -1]
        lower_last = lower_half[:, -1]
        upper_vec = jnp.dot(upper_last, held, precision=precise)
        lower_vec = jnp.dot(lower_last, held, precision=precise)
        vectors = jnp.stack([upper_vec, lower_vec]).astype(jnp.bfloat16)
        whole_part = lax.all_gather(vectors, "sub", axis=1, tiled=True)
        window = padded(whole_part, (("rows", 1),), part_rows)
        blocked = window.reshape(2, 3 * tile_rows, tile_size)
        summed = tile_products(damping, stiffness, target, source, blocked, tile_rows)
        partial_value = summed.reshape(-1)
        coupled = lax.psum_scatter(partial_value, "sub", scatter_dimension=0, tiled=True)
        image = spectral_shift * upper_vec - inv_mass * coupled
        image_inner, image_self, gram = lax.psum(
            (
                jnp.dot(held, image, precision=precise),
                jnp.sum(image * image),
                jnp.dot(held, held.T, precision=precise),
            ),
            ("rows", "sub"),
        )
        first_part = image_inner / unknowns
        gram = gram / unknowns
        second_part = first_part - jnp.dot(gram, first_part, precision=precise)
        coefficients = first_part + second_part
        residual_two = image - jnp.dot(coefficients, held, precision=precise)
        square_mean = (
            image_self / unknowns
            - 2.0 * jnp.dot(coefficients, first_part, precision=precise)
            + jnp.dot(
                coefficients, jnp.dot(gram, coefficients, precision=precise), precision=precise
            )
        )
        norm_value = jnp.sqrt(square_mean + 1e-06)
        column = residual_two / norm_value
        lower_tail = upper_last + spectral_shift * lower_last
        upper_half, lower_half, weights, beta_norm = compact_update(
            upper_half, lower_half, coefficients, norm_value, lower_tail
        )
        held = jnp.concatenate([held, column[None]], 0)
        new_columns.append(column)
        hess_columns.append(
            jnp.concatenate(
                [weights, beta_norm[None], jnp.zeros((ITERS - 1 - iteration,), weights.dtype)]
            )
        )
    return (
        jnp.stack(new_columns),
        jnp.stack([upper_half, lower_half]),
        jnp.stack(hess_columns, axis=1),
    )


def solution(mesh):
    in_specs = (
        P("rows", "sub", None, None, None),
        P("rows", "sub", None, None, None),
        P("rows", "sub", None, None),
        P(("rows", "sub")),
        P(),
        P(None, ("rows", "sub")),
        P(),
    )
    out_specs = (P(None, ("rows", "sub")), P(), P())
    return jax.shard_map(
        on_device, mesh=mesh, in_specs=in_specs, out_specs=out_specs, check_vma=False
    )
```

profile of v0, /device:TPU:0, one launch (start us, length us, event | category | flops | bytes accessed | tf_op | source)
XLA Modules:
  0.0 251.9 jit_solution(1315669255677280857)
XLA Ops:
  7.2 1.0 fusion.104
  8.7 2.7 %fusion.54 = f32[1,8192]{1,0:T(1,128)S(1)} fusion(f32[58,8192]{1,0:T(8,128)} %param.12, f32[58]{0:T(128)S(1)} %get-tuple-element.48), kind=kOutput, calls=%fused_computation.120 | convolution fusion | flops 5701632 | bytes 1933544 | tf_op jit(solution)/shard_map/dot_general | solution.py:81
  11.4 1.1 fusion.52
  12.6 6.5 %all_gather.6 = bf16[2,32768]{1,0:T(2,128)(2,1)S(1)} all-gather(bf16[2,8192]{1,0:T(2,128)(2,1)S(1)} %pad_maximum_fusion.8), channel_id=1, replica_groups=mesh['rows'=8,'sub'=4] {'sub'}, dimensions={1}, use_global_device_ids=true | all-gather | bytes 163840 | tf_op jit(solution)/shard_map/all_gather | solution.py:84
  19.1 3.9 %collective-permute-start = (bf16[2,32768]{1,0:T(2,128)(2,1)S(1)}, bf16[2,32768]{1,0:T(2,128)(2,1)S(1)}, u32[]{:S(2)}, u32[]{:S(2)}) collective-permute-start(bf16[2,32768]{1,0:T(2,128)(2,1)S(1)} %all_gather.6), channel_id=1, source_target_pairs={{0,4},{4,8},{8,12},{12,16},{16,20},{20,24},{24,28},{1,5},{5,9},{9,... | collective-permute-start | bytes 393224 | tf_op jit(solution)/shard_map/ppermute | solution.py:19
  23.1 1.3 collective-permute-start.1
  24.4 1.8 fusion.115
  27.1 3.4 %collective-permute-done.1 = bf16[2,32768]{1,0:T(2,128)(2,1)S(1)} collective-permute-done((bf16[2,32768]{1,0:T(2,128)(2,1)S(1)}, bf16[2,32768]{1,0:T(2,128)(2,1)S(1)}, u32[]{:S(2)}, u32[]{:S(2)}) %collective-permute-start.1) | collective-permute-done | bytes 131104 | tf_op jit(solution)/shard_map/ppermute | solution.py:20
  30.5 2.1 slice_reduce_fusion.2
  32.6 0.7 gather_fusion
  33.3 0.7 gather_fusion.1
  34.0 4.6 %fusion.6 = f32[128,1,128]{2,1,0:T(1,128)S(1)} fusion(bf16[1,1,128,128,128]{4,3,2,1,0:T(8,128)(2,1)} %param.8, bf16[128,128,1]{1,0,2:T(8,128)(2,1)S(1)} %bitcast.283), kind=kOutput, calls=%fused_computation.12 | convolution fusion | flops 4194304 | bytes 4292608 | tf_op jit(solution)/shard_map/sij,sj->si/dot_general | solution.py:51
  38.6 2.3 fusion.2
  40.9 0.9 convolution_bitcast_fusion.1
  41.9 0.6 dynamic-slice
  43.2 31.7 %all-reduce.11.cloned.1.call-done = f32[32768]{0:T(1024)} async-done(((f32[32768]{0:T(1024)}), f32[32768]{0:T(1024)}) %all-reduce.11.cloned.1.call-update) | async-done | bytes 131088
  74.9 1.4 multiply_reduce_fusion.1
  76.3 1.7 convolution_bitcast_fusion.23
  78.0 39.9 %all-reduce.7 = (f32[58,58]{1,0:T(8,128)S(1)}, f32[58]{0:T(128)S(1)}, f32[]{:T(128)}) all-reduce(f32[58,58]{1,0:T(8,128)S(1)} %fusion.115, f32[58]{0:T(128)S(1)} %convolution_bitcast_fusion.23, f32[]{:T(128)} %get-tuple-element.27), channel_id=1, replica_groups=mesh['rows'=8,'sub'=4] {'rows','sub'}, use_global_device_ids=true, to_apply=%region_2.0 | all-reduce | flops 3423 | bytes 27384 | tf_op jit(solution)/shard_map/psum | solution.py:91
  117.9 0.8 multiply_reduce_fusion.3
  118.7 0.8 fusion.26
  122.5 0.8 multiply_reduce_fusion.6
  123.3 0.8 multiply_reduce_fusion.7
  124.0 1.1 fusion.76
  126.5 1.1 fusion.31
  127.7 1.1 fusion.30
  129.0 5.8 %all_gather.7 = bf16[2,32768]{1,0:T(2,128)(2,1)S(1)} all-gather(bf16[2,8192]{1,0:T(2,128)(2,1)S(1)} %pad_maximum_fusion.9), channel_id=1, replica_groups=mesh['rows'=8,'sub'=4] {'sub'}, dimensions={1}, use_global_device_ids=true | all-gather | bytes 163840 | tf_op jit(solution)/shard_map/all_gather | solution.py:84
  134.8 3.8 %collective-permute-start.2 = (bf16[2,32768]{1,0:T(2,128)(2,1)S(1)}, bf16[2,32768]{1,0:T(2,128)(2,1)S(1)}, u32[]{:S(2)}, u32[]{:S(2)}) collective-permute-start(bf16[2,32768]{1,0:T(2,128)(2,1)S(1)} %all_gather.7), channel_id=1, source_target_pairs={{0,4},{4,8},{8,12},{12,16},{16,20},{20,24},{24,28},{1,5},{5,9},{9,... | collective-permute-start | bytes 393224 | tf_op jit(solution)/shard_map/ppermute | solution.py:19
  138.6 1.3 collective-permute-start.3
  139.9 1.8 fusion.29
  142.3 3.7 %collective-permute-done.3 = bf16[2,32768]{1,0:T(2,128)(2,1)S(1)} collective-permute-done((bf16[2,32768]{1,0:T(2,128)(2,1)S(1)}, bf16[2,32768]{1,0:T(2,128)(2,1)S(1)}, u32[]{:S(2)}, u32[]{:S(2)}) %collective-permute-start.3) | collective-permute-done | bytes 131104 | tf_op jit(solution)/shard_map/ppermute | solution.py:20
  146.0 2.1 slice_reduce_fusion
  148.1 0.7 gather_fusion.3
  148.8 4.4 %fusion = f32[128,1,128]{2,1,0:T(1,128)S(1)} fusion(bf16[1,1,128,128,128]{4,3,2,1,0:T(8,128)(2,1)} %param.7, bf16[128,128,1]{1,0,2:T(8,128)(2,1)S(1)} %bitcast.286), kind=kOutput, calls=%fused_computation.6 | convolution fusion | flops 4194304 | bytes 4292608 | tf_op jit(solution)/shard_map/sij,sj->si/dot_general | solution.py:52
  153.3 0.7 gather_fusion.2
  154.0 4.4 %fusion.4 = f32[128,1,128]{2,1,0:T(1,128)S(1)} fusion(bf16[1,1,128,128,128]{4,3,2,1,0:T(8,128)(2,1)} %param.8, bf16[128,128,1]{1,0,2:T(8,128)(2,1)S(1)} %bitcast.285), kind=kOutput, calls=%fused_computation.10 | convolution fusion | flops 4194304 | bytes 4292608 | tf_op jit(solution)/shard_map/sij,sj->si/dot_general | solution.py:51
  158.4 0.9 convolution_bitcast_fusion
  159.4 31.7 %all-reduce.13.cloned.1.call-done = f32[32768]{0:T(1024)} async-done(((f32[32768]{0:T(1024)}), f32[32768]{0:T(1024)}) %all-reduce.13.cloned.1.call-update) | async-done | bytes 131088
  191.1 1.4 multiply_reduce_fusion
  192.5 1.7 convolution_bitcast_fusion.22
  194.2 39.7 %all-reduce.6 = (f32[59,59]{1,0:T(8,128)S(1)}, f32[59]{0:T(128)S(1)}, f32[]{:T(128)}) all-reduce(f32[59,59]{1,0:T(8,128)S(1)} %fusion.29, f32[59]{0:T(128)S(1)} %convolution_bitcast_fusion.22, f32[]{:T(128)} %get-tuple-element.25), channel_id=1, replica_groups=mesh['rows'=8,'sub'=4] {'rows','sub'}, use_global_device_ids=true, to_apply=%region_9.0 | all-reduce | flops 3541 | bytes 28328 | tf_op jit(solution)/shard_map/psum | solution.py:91
  233.9 0.8 multiply_reduce_fusion.2
  234.7 0.8 fusion.27
  238.5 0.8 multiply_reduce_fusion.5
  239.3 0.8 multiply_reduce_fusion.4
  240.1 1.1 fusion.28
  243.0 0.7 copy.32
  243.7 0.7 pad_maximum_fusion.6
  (70 shorter events, 5.1 us)
Async XLA Ops:
  7.2 4.2 %copy-start = (f32[58,8192]{1,0:T(8,128)S(1)}, f32[58,8192]{1,0:T(8,128)}, u32[]{:S(2)}) copy-start(f32[58,8192]{1,0:T(8,128)} %param.12) | copy-start | bytes 5701636
  7.2 67.7 %all-reduce.11.cloned.1.call-start = ((), (), s32[]{:S(2)}) async-start(), calls=%async_computation | async-start | bytes 262144
  19.1 7.0 %copy-start.3 = (s32[1,1,2,128]{3,2,1,0:T(2,128)S(1)}, s32[1,1,2,128]{3,2,1,0:T(2,128)}, u32[]{:S(2)}) copy-start(s32[1,1,2,128]{3,2,1,0:T(2,128)} %param.9) | copy-start | bytes 3076
  19.1 7.7 %collective-permute-start = (bf16[2,32768]{1,0:T(2,128)(2,1)S(1)}, bf16[2,32768]{1,0:T(2,128)(2,1)S(1)}, u32[]{:S(2)}, u32[]{:S(2)}) collective-permute-start(bf16[2,32768]{1,0:T(2,128)(2,1)S(1)} %all_gather.6), channel_id=1, source_target_pairs={{0,4},{4,8},{8,12},{12,16},{16,20},{20,24},{24,28},{1,5},{5,9},{9,... | collective-permute-start | bytes 393224 | tf_op jit(solution)/shard_map/ppermute | solution.py:19
  23.1 7.4 %collective-permute-start.1 = (bf16[2,32768]{1,0:T(2,128)(2,1)S(1)}, bf16[2,32768]{1,0:T(2,128)(2,1)S(1)}, u32[]{:S(2)}, u32[]{:S(2)}) collective-permute-start(bf16[2,32768]{1,0:T(2,128)(2,1)S(1)} %all_gather.6), channel_id=1, source_target_pairs={{4,0},{8,4},{12,8},{16,12},{20,16},{24,20},{28,24},{5,1},{9,5},{13... | collective-permute-start | bytes 393224 | tf_op jit(solution)/shard_map/ppermute | solution.py:20
  34.0 4.6 %copy-start.1 = (bf16[1,1,128,128,128]{4,3,2,1,0:T(8,128)(2,1)S(1)}, bf16[1,1,128,128,128]{4,3,2,1,0:T(8,128)(2,1)}, u32[]{:S(2)}) copy-start(bf16[1,1,128,128,128]{4,3,2,1,0:T(8,128)(2,1)} %param.7) | copy-start | bytes 12582916
  38.6 3.3 %copy-start.4 = (u32[32]{0:T(128)S(1)}, u32[32]{0:T(128)}, u32[]{:S(2)}) copy-start(u32[32]{0:T(128)} %constant.43) | copy-start | bytes 388
  38.6 36.3 %copy-start.2 = (f32[8192]{0:T(1024)S(1)}, f32[8192]{0:T(1024)}, u32[]{:S(2)}) copy-start(f32[8192]{0:T(1024)} %param.10) | copy-start | bytes 98308
  41.8 149.3 %all-reduce.13.cloned.1.call-start = ((), (), s32[]{:S(2)}) async-start(), calls=%async_computation.1 | async-start | bytes 262144
  134.8 7.2 %collective-permute-start.2 = (bf16[2,32768]{1,0:T(2,128)(2,1)S(1)}, bf16[2,32768]{1,0:T(2,128)(2,1)S(1)}, u32[]{:S(2)}, u32[]{:S(2)}) collective-permute-start(bf16[2,32768]{1,0:T(2,128)(2,1)S(1)} %all_gather.7), channel_id=1, source_target_pairs={{0,4},{4,8},{8,12},{12,16},{16,20},{20,24},{24,28},{1,5},{5,9},{9,... | collective-permute-start | bytes 393224 | tf_op jit(solution)/shard_map/ppermute | solution.py:19
  138.6 7.4 %collective-permute-start.3 = (bf16[2,32768]{1,0:T(2,128)(2,1)S(1)}, bf16[2,32768]{1,0:T(2,128)(2,1)S(1)}, u32[]{:S(2)}, u32[]{:S(2)}) collective-permute-start(bf16[2,32768]{1,0:T(2,128)(2,1)S(1)} %all_gather.7), channel_id=1, source_target_pairs={{4,0},{8,4},{12,8},{16,12},{20,16},{24,20},{28,24},{5,1},{9,5},{13... | collective-permute-start | bytes 393224 | tf_op jit(solution)/shard_map/ppermute | solution.py:20
Sparse Core Ops, SparseCore 0:
  41.9 32.9 all-reduce.10
  159.5 31.6 all-reduce.12
where the time goes:
time: 253 us; the launch traced here: 252 us
  blocking collectives  91.9 us (36%)
  waiting for transfers between devices  70.5 us (28%)
  matrix products  41.1 us (16%)
  between operations  22.3 us (9%)
  local copies, waits for them, and re-layouts  10.9 us (4%)
  starting transfers between devices  10.4 us (4%)
  other arithmetic  4.73 us (2%)
    psum x2, blocking collectives, on_device(): lax.psum((jnp.dot(held, image, precision=precise), jnp.sum(image * image)...  79.6 us
    unnamed x4, waiting for transfers between devices  63.4 us
    all_gather x2, blocking collectives, on_device(): whole_part = lax.all_gather(vectors, 'sub', axis=1, tiled=True)  12.3 us
    dot_general x2, matrix products, tile_products(): jnp.einsum('sij,sj->si', damping, picked_damp, preferred_element_type=jnp...  9.01 us
    ppermute x2, starting transfers between devices, padded(): before = lax.ppermute(last, axis, up)  7.71 us
    ppermute x2, waiting for transfers between devices, padded(): after = lax.ppermute(initial, axis, down)  7.03 us
    dot_general x2, matrix products, tile_products(): jnp.einsum('sij,sj->si', stiffness, picked_stiff, preferred_element_type=...  6.71 us
  transfers between devices with their start and end apart: 6, of which 4 were waited for; matrix products, arithmetic and copies ran while one was open for 2% of the time, Pallas kernels for 0%

commit v1 on v0

v1 whole, which is shorter than its diff:
```python
import functools

import jax
import jax.numpy as jnp
from jax import lax
from jax.experimental import pallas as pl
from jax.experimental.pallas import tpu as pltpu
from jax.sharding import PartitionSpec as P

ITERS = 2
LANES = 128
SUBL = 8
F32 = jnp.float32
BF16 = jnp.bfloat16
VM = pltpu.VMEM
SM = pltpu.SMEM


def vmem():
    return pl.BlockSpec(memory_space=VM)


def smem():
    return pl.BlockSpec(memory_space=SM)


def iota(shape, axis):
    return lax.broadcasted_iota(jnp.int32, shape, axis)


def lane_sum(x):
    return jnp.sum(x, axis=1, keepdims=True)


def sub_sum(x):
    return jnp.sum(x, axis=0, keepdims=True)


def row_to_col(row, height):
    shape = (height, LANES)
    return lane_sum(jnp.where(iota(shape, 0) == iota(shape, 1), row, 0.0))


def col_to_row(col, height):
    shape = (height, LANES)
    return sub_sum(jnp.where(iota(shape, 0) == iota(shape, 1), col, 0.0))


def at_sublane(col, index):
    return jnp.sum(jnp.where(iota(col.shape, 0) == index, col, 0.0), axis=0, keepdims=True)


def gather_rows(parts):
    shift = 1
    while len(parts) > 1:
        low = (iota((SUBL, LANES), 0) // shift) % 2 == 0
        merged = []
        for a, b in zip(parts[0::2], parts[1::2]):
            moved = pltpu.roll(jnp.where(low, b, a), SUBL - shift, axis=0)
            merged.append(jnp.where(low, a, b) + moved)
        parts = merged
        shift *= 2
    return parts[0]


def block_rows(held_ref):
    n = held_ref.shape[0]
    return [(i, min(SUBL, n - i)) for i in range(0, n, SUBL)]


def combine(held_ref, cols, group):
    out = []
    totals = [[] for _ in cols]
    for k in range(SUBL):
        lanes = pl.ds((group * SUBL + k) * LANES, LANES)
        sums = [None] * len(cols)
        for start, size in block_rows(held_ref):
            block = held_ref[pl.ds(start, size), lanes]
            if size < SUBL:
                block = jnp.concatenate(
                    [block, jnp.zeros((SUBL - size, LANES), F32)], axis=0
                )
            for i, col in enumerate(cols):
                term = block * col[start : start + SUBL]
                sums[i] = term if sums[i] is None else sums[i] + term
        for i in range(len(cols)):
            totals[i].append(sums[i])
    for i in range(len(cols)):
        out.append(gather_rows(totals[i]))
    return out


def start_kernel(last_ref, held_ref, upper_ref, vec_ref):
    tiles = upper_ref.shape[0]
    n = held_ref.shape[0]
    height = -(-n // SUBL) * SUBL
    rows = jnp.pad(last_ref[...], ((0, 0), (0, LANES - n)))
    cols = [
        jnp.broadcast_to(row_to_col(rows[i : i + 1], height), (height, LANES)) for i in range(2)
    ]
    for group in range(tiles // SUBL):
        upper, lower = combine(held_ref, cols, group)
        at = group * SUBL
        upper_ref[at : at + SUBL] = upper
        vec_ref[at : at + SUBL] = upper.astype(BF16)
        vec_ref[tiles + at : tiles + at + SUBL] = lower.astype(BF16)


def tile_kernel(
    rows_count,
    sub_count,
    packed,
    map_ref,
    target_ref,
    pair_ref,
    mine_ref,
    other_ref,
    damping_ref,
    stiffness_ref,
    *rest,
):
    if packed:
        gram_ref, rest = rest[0], rest[1:]
    outs, rest = rest[:sub_count], rest[sub_count:]
    window_ref, picked_ref, product_ref = rest[:3]
    step = pl.program_id(0)
    r = lax.axis_index("rows")
    s = lax.axis_index("sub")
    tiles = pair_ref.shape[1] // 2
    slots = product_ref.shape[0]
    block = damping_ref.shape[0]
    part_tiles = sub_count * tiles

    @pl.when(step == 0)
    def _():
        def put(value, part, sub, scale):
            at = pl.multiple_of((part * sub_count + sub) * tiles, tiles)
            wide = value.astype(F32)
            if scale is not None:
                wide = wide * scale
            window_ref[0, pl.ds(at, tiles)] = wide[:tiles]
            window_ref[1, pl.ds(at, tiles)] = wide[tiles:]

        put(pair_ref[0], 1, s, None)
        put(pair_ref[1], 1, s ^ 1, None)
        towards = jnp.where((r + s) % 2 == 0, 1, -1)
        half = sub_count // 2
        for source_ref, base, rel in ((mine_ref, s, towards), (other_ref, s ^ 1, -towards)):
            for k in range(1, half):
                put(source_ref[k - 1], 1, base ^ (2 * k), None)
            inside = jnp.logical_and(r + rel >= 0, r + rel < rows_count)
            scale = jnp.where(inside, 1.0, 0.0)
            for k in range(half):
                for e in range(2):
                    put(
                        source_ref[half - 1 + 2 * k + e],
                        1 + rel,
                        base ^ (2 * k) ^ e,
                        scale,
                    )
        for t in range(slots):
            source = jnp.clip(map_ref[1, t], 0, 3 * part_tiles - 1)
            picked_ref[0, t : t + 1] = window_ref[0, pl.ds(source, 1)]
            picked_ref[1, t : t + 1] = window_ref[1, pl.ds(source, 1)]

    at = pl.ds(pl.multiple_of(step * block, block), block)
    dims = (((1,), (1,)), ((), ()))
    result = lax.dot_general(
        picked_ref[0, at].astype(BF16),
        damping_ref[...].reshape(block * LANES, LANES),
        dims,
        preferred_element_type=F32,
    ) + lax.dot_general(
        picked_ref[1, at].astype(BF16),
        stiffness_ref[...].reshape(block * LANES, LANES),
        dims,
        preferred_element_type=F32,
    )
    own = jnp.zeros((block, LANES), F32)
    for t in range(block):
        own = own + jnp.where(
            iota((block, LANES), 0) == t, result[:, t * LANES : (t + 1) * LANES], 0.0
        )
    product_ref[at] = own

    @pl.when(step == pl.num_programs(0) - 1)
    def _():
        target = target_ref[...]
        target = jnp.where(target >= 0, target ^ (s * tiles), -1)
        selector = jnp.where(iota((part_tiles, slots), 0) == target, 1.0, 0.0).astype(BF16)
        left = product_ref[...]
        summed = jnp.zeros((part_tiles, LANES), F32)
        for _ in range(3):
            piece = left.astype(BF16)
            summed = summed + jnp.dot(selector, piece, preferred_element_type=F32)
            left = left - piece.astype(F32)
        for k in range(sub_count):
            outs[k][:tiles] = summed[k * tiles : (k + 1) * tiles]
        if packed:
            square_ref = rest[3]
            n = gram_ref.shape[0]
            square_ref[...] = jnp.zeros(square_ref.shape, F32)
            square_ref[:n, :n] = gram_ref[...]
            share = square_ref.shape[0] // sub_count
            for k in range(sub_count):
                start = pl.multiple_of((s ^ k) * share, SUBL)
                low = square_ref[pl.ds(start, SUBL)]
                high = square_ref[pl.ds(start + SUBL, SUBL)]
                outs[k][tiles:] = low + pltpu.roll(high, LANES // 2, axis=1)


def inner_kernel(sub_count, packed, shift_ref, *refs):
    parts = refs[:sub_count]
    upper_ref, mass_ref, held_ref = refs[sub_count : sub_count + 3]
    refs = refs[sub_count + 3 :]
    if not packed:
        column_ref, refs = refs[0], refs[1:]
    image_ref, packet_ref = refs
    tiles = upper_ref.shape[0]
    n = held_ref.shape[0]
    total = parts[0][:tiles]
    for k in range(1, sub_count):
        total = total + parts[k][:tiles]
    image = shift_ref[0] * upper_ref[...] - mass_ref[...] * total
    image_ref[...] = image
    square = lane_sum(sub_sum(image * image))
    blocks = block_rows(held_ref)
    sums = [None] * len(blocks)
    for k in range(tiles):
        row = image_ref[k : k + 1]
        for i, (start, size) in enumerate(blocks):
            term = held_ref[pl.ds(start, size), pl.ds(k * LANES, LANES)] * row
            sums[i] = term if sums[i] is None else sums[i] + term
    cols = []
    for total_block, (start, size) in zip(sums, blocks):
        col = lane_sum(total_block)
        if size < SUBL:
            col = jnp.concatenate([col, jnp.zeros((SUBL - size, 1), F32)], axis=0)
        cols.append(col)
    lane = iota((SUBL, LANES), 1)
    if packed:
        packet = parts[0][tiles:]
        for k in range(1, sub_count):
            packet = packet + parts[k][tiles:]
        for i, col in enumerate(cols):
            spot = (i % 2) * (LANES // 2) + n + i // 2
            packet = jnp.where(lane == spot, col, packet)
        spot = n + (len(cols) + 1) // 2
        first = iota((SUBL, LANES), 0) == 0
        packet = jnp.where(jnp.logical_and(lane == spot, first), square, packet)
        packet_ref[...] = jnp.broadcast_to(packet[None], packet_ref.shape)
    else:
        height = SUBL * len(cols)
        row = col_to_row(jnp.concatenate(cols, axis=0), height)
        extra = lane_sum(sub_sum(image * column_ref[...]))
        row = jnp.where(lane[:1] == n, extra, row)
        row = jnp.where(lane[:1] == LANES - 1, square, row)
        packet_ref[...] = jnp.broadcast_to(row[None], packet_ref.shape)


def update_kernel(unknowns, sub_count, iteration, last, shift_ref, *refs):
    packet_ref, image_ref, held_ref, upper_half_ref, lower_half_ref = refs[:5]
    refs = refs[5:]
    n0 = held_ref.shape[0]
    n = n0 + iteration
    tiles = image_ref.shape[0]
    height = -(-n0 // (2 * SUBL)) * 2 * SUBL
    shape = (height, LANES)
    lane = iota(shape, 1)
    subl = iota(shape, 0)
    inverse = 1.0 / unknowns
    if iteration == 0:
        out_refs = refs
        count = packet_ref.shape[0] // sub_count
        blocks = []
        for s in range(sub_count):
            total = packet_ref[s]
            for r in range(1, count):
                total = total + packet_ref[r * sub_count + s]
            blocks.append(total)
        every = blocks[0]
        for s in range(1, sub_count):
            every = every + blocks[s]
        lane8 = iota((SUBL, LANES), 1)
        gram = []
        for total in blocks:
            gram.append(jnp.where(lane8 < n, total, 0.0))
            gram.append(jnp.where(lane8 < n, pltpu.roll(total, LANES // 2, axis=1), 0.0))
        gram = jnp.concatenate(gram, axis=0) * inverse
        pieces = -(-n0 // SUBL)
        cols = []
        for i in range(height // SUBL):
            spot = (i % 2) * (LANES // 2) + n + i // 2
            cols.append(lane_sum(jnp.where(lane8 == spot, every, 0.0)))
        first_col = jnp.concatenate(cols, axis=0) * inverse
        first_row = col_to_row(first_col, height)
        spot = n + (pieces + 1) // 2
        self_mean = sub_sum(lane_sum(jnp.where(lane8 == spot, every, 0.0))) * inverse
    else:
        gram_ref, column_ref, weights_ref = refs[:3]
        out_refs = refs[3:]
        total = packet_ref[0]
        for i in range(1, packet_ref.shape[0]):
            total = total + packet_ref[i]
        gram = gram_ref[...]
        first_row = jnp.where(lane[:1] < n, total, 0.0) * inverse
        first_col = row_to_col(first_row, height)
        self_mean = lane_sum(jnp.where(lane[:1] == LANES - 1, total, 0.0)) * inverse
    coef_col = first_col + (first_col - lane_sum(gram * first_row))
    coef_row = first_row + (first_row - sub_sum(gram * first_col))
    gram_coef = lane_sum(gram * coef_row)
    mean_square = self_mean - 2.0 * sub_sum(coef_col * first_col) + sub_sum(coef_col * gram_coef)
    norm = jnp.sqrt(mean_square + 1e-06)
    upper_half = upper_half_ref[...]
    lower_half = lower_half_ref[...]
    columns = n - 1
    shift = shift_ref[0]
    tail = lane_sum(jnp.where(lane == columns - 1, upper_half + shift * lower_half, 0.0))
    upper_coef = jnp.where(subl[:, :1] == n, norm, coef_col)
    lower_coef = tail
    weights = jnp.zeros((1, LANES), F32)
    for _ in range(2):
        projection = sub_sum(upper_half * upper_coef + lower_half * lower_coef)
        upper_coef = upper_coef - lane_sum(upper_half * projection)
        lower_coef = lower_coef - lane_sum(lower_half * projection)
        weights = weights + projection
    beta = jnp.sqrt(sub_sum(upper_coef * upper_coef + lower_coef * lower_coef) + 1e-06)
    upper_new = upper_coef / beta
    lower_new = lower_coef / beta
    upper_half = jnp.where(lane == columns, upper_new, upper_half)
    lower_half = jnp.where(lane == columns, lower_new, lower_half)
    weights = jnp.where(lane[:1] == columns, beta, weights)
    coef_wide = jnp.broadcast_to(coef_col, shape)
    if not last:
        column_ref, upper_ref, vec_ref, upper_half_out, lower_half_out, gram_out, weights_out = (
            out_refs
        )
        upper_half_out[...] = upper_half
        lower_half_out[...] = lower_half
        weights_out[...] = jnp.broadcast_to(weights, (SUBL, LANES))
        cross_col = (first_col - gram_coef) / norm
        cross_row = (first_row - sub_sum(gram * coef_col)) / norm
        gram = jnp.where(lane == n, cross_col, gram)
        gram = jnp.where(subl == n, cross_row, gram)
        corner = jnp.logical_and(lane == n, subl == n)
        gram_out[...] = jnp.where(corner, mean_square / (norm * norm), gram)
        upper_wide = jnp.broadcast_to(upper_new, shape)
        lower_wide = jnp.broadcast_to(lower_new, shape)
        upper_last = at_sublane(upper_new, n)
        lower_last = at_sublane(lower_new, n)
        for group in range(tiles // SUBL):
            at = group * SUBL
            along, upper, lower = combine(held_ref, [coef_wide, upper_wide, lower_wide], group)
            column = (image_ref[at : at + SUBL] - along) / norm
            upper = upper + column * upper_last
            lower = lower + column * lower_last
            column_ref[at : at + SUBL] = column
            upper_ref[at : at + SUBL] = upper
            vec_ref[at : at + SUBL] = upper.astype(BF16)
            vec_ref[tiles + at : tiles + at + SUBL] = lower.astype(BF16)
    else:
        basis_ref, compact_ref, hess_ref = out_refs
        compact_ref[0] = upper_half[: n + 1, :n]
        compact_ref[1] = lower_half[: n + 1, :n]
        hess = jnp.where(
            lane == 0,
            row_to_col(weights_ref[:1], height),
            row_to_col(weights, height),
        )
        hess_ref[...] = hess[:n, :2]
        coef_last = at_sublane(coef_col, n0)
        for group in range(tiles // SUBL):
            at = group * SUBL
            (along,) = combine(held_ref, [coef_wide], group)
            before = column_ref[at : at + SUBL]
            column = (image_ref[at : at + SUBL] - along - before * coef_last) / norm
            for k in range(SUBL):
                lanes = pl.ds((at + k) * LANES, LANES)
                basis_ref[0:1, lanes] = before[k : k + 1]
                basis_ref[1:2, lanes] = column[k : k + 1]


def call(body, outs, args, specs, scratch=(), grid=None):
    arguments = dict(
        out_shape=[jax.ShapeDtypeStruct(shape, dtype) for shape, dtype in outs],
        in_specs=specs,
        out_specs=[vmem()] * len(outs),
        scratch_shapes=list(scratch),
    )
    if grid is not None:
        arguments.update(
            grid=grid,
            out_specs=[
                pl.BlockSpec(shape, lambda i, rank=len(shape): (0,) * rank) for shape, _ in outs
            ],
        )
    return pl.pallas_call(body, **arguments)(*args)


def on_device(stiffness_tiles, damping_tiles, tile_map, inv_mass, spectral_shift, basis, compact):
    rows_count = lax.axis_size("rows")
    sub_count = lax.axis_size("sub")
    devices = rows_count * sub_count
    half = sub_count // 2
    tile_size = stiffness_tiles.shape[-1]
    slots = stiffness_tiles.shape[2]
    held_count, local_rows = basis.shape
    tiles = local_rows // tile_size
    unknowns = local_rows * devices
    height = -(-held_count // (2 * SUBL)) * 2 * SUBL
    block = 2 * SUBL
    every = ("rows", "sub")

    def swap(value, partner):
        pairs = []
        for r in range(rows_count):
            for s in range(sub_count):
                to_r, to_s = partner(r, s)
                pairs.append((r * sub_count + s, to_r * sub_count + to_s))
        return lax.ppermute(value, every, pairs)

    def beside(r, s):
        return r ^ 1 if s % 2 == 0 else (((r + 1) ^ 1) - 1) % rows_count

    slot_map = tile_map[0, 0]
    damping = damping_tiles[0, 0]
    stiffness = stiffness_tiles[0, 0]
    shift = spectral_shift.reshape(1)
    mass = inv_mass.reshape(tiles, tile_size)
    field = ((tiles, tile_size), F32)
    vector = ((2 * tiles, tile_size), BF16)
    square = ((height, LANES), F32)

    upper_vec, vectors = call(
        start_kernel, [field, vector], (compact[:, :, -1], basis), [vmem(), vmem()]
    )
    padding = ((0, 0), (0, height - compact.shape[1]), (0, LANES - compact.shape[2]))
    halves = jnp.pad(compact, padding)
    upper_half, lower_half = halves[0], halves[1]
    gram = jnp.dot(basis, basis.T, precision=lax.Precision.HIGHEST)
    column = weights = None
    for iteration in range(ITERS):
        packed = iteration == 0
        last = iteration == ITERS - 1
        pair = jnp.stack([vectors, swap(vectors, lambda r, s: (r, s ^ 1))])
        mine = [
            swap(vectors, lambda r, s, k=k: (r, s ^ (2 * k)))[None] for k in range(1, half)
        ] + [swap(pair, lambda r, s, k=k: (beside(r, s), s ^ (2 * k))) for k in range(half)]
        mine = jnp.concatenate(mine, axis=0)
        other = swap(mine, lambda r, s: (r, s ^ 1))
        depth = tiles + SUBL if packed else tiles
        full = lambda shape: pl.BlockSpec(shape, lambda i, rank=len(shape): (0,) * rank)
        tile_spec = pl.BlockSpec((block, tile_size, tile_size), lambda i: (i, 0, 0))
        scratch = [
            pltpu.VMEM((2, 3 * sub_count * tiles, LANES), F32),
            pltpu.VMEM((2, slots, LANES), F32),
            pltpu.VMEM((slots, LANES), F32),
        ]
        args = [slot_map, slot_map[:1], pair, mine, other, damping, stiffness]
        specs = [
            smem(),
            full((1, slots)),
            full(pair.shape),
            full(mine.shape),
            full(other.shape),
            tile_spec,
            tile_spec,
        ]
        if packed:
            args.append(gram)
            specs.append(full(gram.shape))
            scratch.append(pltpu.VMEM((height, LANES), F32))
        parts = call(
            functools.partial(tile_kernel, rows_count, sub_count, packed),
            [((depth, LANES), F32)] * sub_count,
            args,
            specs,
            scratch,
            grid=(slots // block,),
        )
        parts = [parts[0]] + [
            swap(parts[k], lambda r, s, k=k: (r, s ^ k)) for k in range(1, sub_count)
        ]
        packet = (devices, SUBL, LANES) if packed else (devices, 1, LANES)
        args = [shift, *parts, upper_vec, mass, basis]
        if not packed:
            args.append(column)
        image, sent = call(
            functools.partial(inner_kernel, sub_count, packed),
            [field, (packet, F32)],
            args,
            [smem()] + [vmem()] * (len(args) - 1),
        )
        received = lax.all_to_all(sent, every, 0, 0)
        args = [shift, received, image, basis, upper_half, lower_half]
        if not packed:
            args += [gram, column, weights]
        if last:
            total = held_count + ITERS
            outs = [
                ((ITERS, local_rows), F32),
                ((2, total, total - 1), F32),
                ((total - 1, ITERS), F32),
            ]
        else:
            outs = [field, field, vector, square, square, square, ((SUBL, LANES), F32)]
        outs = call(
            functools.partial(update_kernel, unknowns, sub_count, iteration, last),
            outs,
            args,
            [smem()] + [vmem()] * (len(args) - 1),
        )
        if not last:
            column, upper_vec, vectors, upper_half, lower_half, gram, weights = outs
    return tuple(outs)


def solution(mesh):
    in_specs = (
        P("rows", "sub", None, None, None),
        P("rows", "sub", None, None, None),
        P("rows", "sub", None, None),
        P(("rows", "sub")),
        P(),
        P(None, ("rows", "sub")),
        P(),
    )
    out_specs = (P(None, ("rows", "sub")), P(), P())
    return jax.shard_map(
        on_device, mesh=mesh, in_specs=in_specs, out_specs=out_specs, check_vma=False
    )
```

time: 253 us -> 99.3 us (0.39)
  blocking collectives: 91.9 us -> 10.6 us
  waiting for transfers between devices: 70.5 us -> 20.7 us
  matrix products: 41.1 us -> 2.38 us
  Pallas kernels: 0 us -> 31.2 us
  between operations: 22.3 us -> 1.4 us
  starting transfers between devices: 10.4 us -> 21.7 us
  other arithmetic: 4.73 us -> 1.6 us
    psum x2 -> x0, blocking collectives: 79.6 us -> none  [on_device(): lax.psum((jnp.dot(held, image, precision=precise), jnp.sum(image * image)...]
    unnamed x4 -> x0, waiting for transfers between devices: 63.4 us -> none
    dot_general x36 -> x1, matrix products: 41.1 us -> 2.38 us  [on_device(): gram = jnp.dot(basis, basis.T, precision=lax.Precision.HIGHEST)]
    pallas_call x0 -> x7, Pallas kernels: none -> 31.2 us  [call(): return pl.pallas_call(body, **arguments)(*args)]
    all_gather x2 -> x0, blocking collectives: 12.3 us -> none  [on_device(): whole_part = lax.all_gather(vectors, 'sub', axis=1, tiled=True)]
    all_to_all x0 -> x1, blocking collectives: none -> 10.6 us  [on_device(): received = lax.all_to_all(sent, every, 0, 0)]
    ppermute x4 -> x16, starting transfers between devices: 10.3 us -> 19.1 us  [swap(): return lax.ppermute(value, every, pairs)]
    all_to_all x0 -> x1, waiting for transfers between devices: none -> 7.45 us  [on_device(): received = lax.all_to_all(sent, every, 0, 0)]
  transfers between devices with their start and end apart: 6 -> 17, of which waited for: 4 -> 10; matrix products, arithmetic and copies ran while one was open for 2% -> 5% of each run, Pallas kernels for 0% -> 0%
where the time goes in v1:
time: 99.3 us; the launch traced here: 98.4 us
  Pallas kernels  31.2 us (31%)
  starting transfers between devices  21.7 us (22%)
  waiting for transfers between devices  20.7 us (21%)
  blocking collectives  10.6 us (11%)
  local copies, waits for them, and re-layouts  8.9 us (9%)
  matrix products  2.38 us (2%)
  other arithmetic  1.6 us (2%)
  between operations  1.4 us (1%)
    pallas_call x7, Pallas kernels, call(): return pl.pallas_call(body, **arguments)(*args)  31.2 us
    ppermute x16, starting transfers between devices, swap(): return lax.ppermute(value, every, pairs)  19.1 us
    ppermute x16, waiting for transfers between devices, swap(): return lax.ppermute(value, every, pairs)  13.2 us
    all_to_all x1, blocking collectives, on_device(): received = lax.all_to_all(sent, every, 0, 0)  10.6 us
    all_to_all x1, waiting for transfers between devices, on_device(): received = lax.all_to_all(sent, every, 0, 0)  7.45 us
    unnamed x33, local copies, waits for them, and re-layouts  3.33 us
    pallas_call x2, local copies, waits for them, and re-layouts, call(): return pl.pallas_call(body, **arguments)(*args)  2.95 us
    all_to_all x1, starting transfers between devices, on_device(): received = lax.all_to_all(sent, every, 0, 0)  2.56 us
  transfers between devices with their start and end apart: 17, of which 10 were waited for; matrix products, arithmetic and copies ran while one was open for 5% of the time, Pallas kernels for 0%

profile of v1, /device:TPU:0, one launch (start us, length us, event | category | flops | bytes accessed | tf_op | source)
XLA Modules:
  0.0 98.4 jit_solution(11567742228549933566)
XLA Ops:
  0.6 1.4 %slice_bitcast_fusion.last_ref = f32[2,58]{1,0:T(2,128)} fusion(f32[2,58,57]{1,0,2:T(2,128)} %param.13), kind=kLoop, calls=%fused_computation.8 | loop fusion | bytes 928 | tf_op jit(solution)/shard_map/squeeze | solution.py:435
  2.0 2.6 %shard_map.94 = (f32[64,128]{1,0:T(8,128)}, bf16[128,128]{1,0:T(8,128)(2,1)}) custom-call(f32[2,58]{1,0:T(2,128)} %slice_bitcast_fusion.last_ref, f32[58,8192]{1,0:T(8,128)} %refs_2_.3), custom_call_target="tpu_custom_call" | custom-call | tf_op jit(solution)/shard_map/pallas_call | solution.py:397
  4.7 0.5 collective-permute-start
  5.2 2.5 %collective-permute-start.1 = (bf16[128,128]{1,0:T(8,128)(2,1)}, bf16[128,128]{1,0:T(8,128)(2,1)S(1)}, u32[]{:S(2)}, u32[]{:S(2)}) collective-permute-start(bf16[128,128]{1,0:T(8,128)(2,1)} %get-tuple-element.24), channel_id=1, source_target_pairs={{0,2},{1,3},{2,0},{3,1},{4,6},{5,7},{6,4},{7,5},{8,10},{9,11},{10,... | collective-permute-start | bytes 98312 | tf_op jit(solution)/shard_map/ppermute | solution.py:420
  7.6 0.8 pad_maximum_fusion.2.pair_ref
  8.5 2.4 %collective-permute-start.3 = (bf16[2,128,128]{2,1,0:T(8,128)(2,1)S(1)}, bf16[2,128,128]{2,1,0:T(8,128)(2,1)S(1)}, u32[]{:S(2)}, u32[]{:S(2)}) collective-permute-start(bf16[2,128,128]{2,1,0:T(8,128)(2,1)S(1)} %pad_maximum_fusion.2.pair_ref), channel_id=1, source_target_pairs={{0,6},{1,31},{2,4},{3,29},{4,2},{5,11},{6,0},{7,9},{8,14},{9,7},{1... | collective-permute-start | bytes 196616 | tf_op jit(solution)/shard_map/ppermute | solution.py:420
  10.9 0.5 collective-permute-start.2
  11.4 2.4 %fusion.2.rest_0_ = f32[58,58]{1,0:T(8,128)} fusion(f32[58,8192]{1,0:T(8,128)S(1)} %copy-done), kind=kOutput, calls=%fused_computation.10 | convolution fusion | flops 330694656 | bytes 1914000 | tf_op jit(solution)/shard_map/dot_general | solution.py:440
  13.8 2.1 %collective-permute-done.2 = bf16[2,128,128]{2,1,0:T(8,128)(2,1)S(1)} collective-permute-done((bf16[2,128,128]{2,1,0:T(8,128)(2,1)S(1)}, bf16[2,128,128]{2,1,0:T(8,128)(2,1)S(1)}, u32[]{:S(2)}, u32[]{:S(2)}) %collective-permute-start.2) | collective-permute-done | bytes 65568 | tf_op jit(solution)/shard_map/ppermute | solution.py:420
  15.9 3.8 %collective-permute-start.4 = (bf16[5,128,128]{2,1,0:T(8,128)(2,1)S(1)}, bf16[5,128,128]{2,1,0:T(8,128)(2,1)S(1)}, u32[]{:S(2)}, u32[]{:S(2)}) collective-permute-start(bf16[5,128,128]{2,1,0:T(8,128)(2,1)S(1)} %pad_maximum_fusion.mine_ref), channel_id=1, source_target_pairs={{0,1},{1,0},{2,3},{3,2},{4,5},{5,4},{6,7},{7,6},{8,9},{9,8},{10,11... | collective-permute-start | bytes 491528 | tf_op jit(solution)/shard_map/ppermute | solution.py:420
  19.7 0.6 slice_bitcast_fusion.1.target_ref
  20.3 0.4 collective-permute-done.4.other_ref
  20.7 0.7 copy-done.6
  21.4 8.3 %shard_map.95 = (f32[72,128]{1,0:T(8,128)}, f32[72,128]{1,0:T(8,128)}, f32[72,128]{1,0:T(8,128)}, f32[72,128]{1,0:T(8,128)}) custom-call(s32[2,128]{1,0:T(2,128)} %bitcast.37, s32[1,128]{1,0:T(1,128)} %slice_bitcast_fusion.1.target_ref, bf16[2,128,128]{2,1,0:T(8,128)(2,1)} %copy-done.5, bf16[5,128,128]{2,1,0:T(8,128)(2,1)} %copy-done.1, ...), custom_call_target="tpu_custom_call" | custom-call | tf_op jit(solution)/shard_map/pallas_call | solution.py:397
  29.7 0.4 collective-permute-start.5
  30.1 0.7 collective-permute-start.6
  30.8 0.8 collective-permute-start.7
  32.3 2.3 %collective-permute-done.6.refs_2_ = f32[72,128]{1,0:T(8,128)S(1)} collective-permute-done((f32[72,128]{1,0:T(8,128)}, f32[72,128]{1,0:T(8,128)S(1)}, u32[]{:S(2)}, u32[]{:S(2)}) %collective-permute-start.6) | collective-permute-done | bytes 36896 | tf_op jit(solution)/shard_map/ppermute | solution.py:420
  34.5 0.3 collective-permute-done.7.refs_3_
  34.8 0.3 copy-done.10
  35.2 0.3 copy-done.11
  35.4 2.7 %shard_map.96 = (f32[64,128]{1,0:T(8,128)}, f32[32,8,128]{2,1,0:T(8,128)}) custom-call(f32[1]{0:T(128)} %bitcast.21.shift_ref, f32[72,128]{1,0:T(8,128)} %get-tuple-element.25.refs_0_, f32[72,128]{1,0:T(8,128)} %copy-done.9, f32[72,128]{1,0:T(8,128)} %copy-done.10, f32[72,128]{1,0:T(8,128)} %copy-done.11, f32[64,128]{1,0:T(8,128)} %get-tuple-element.29.refs_4_, ...), custom_call_target="tpu_custom_call" | custom-call | tf_op jit(solution)/shard_map/pallas_call | solution.py:397
  38.1 2.6 %all-to-all-start = ((f32[32,8,128]{2,1,0:T(8,128)}), f32[32,8,128]{2,1,0:T(8,128)S(1)}, u32[]{:S(2)}, u32[]{:S(2)}) async-start(f32[32,8,128]{2,1,0:T(8,128)} %get-tuple-element.30), calls=%async_computation | async-start | bytes 262144 | tf_op jit(solution)/shard_map/all_to_all | solution.py:494
  40.8 0.6 fusion.1
  41.4 7.4 %all-to-all-done.refs_0_ = f32[32,8,128]{2,1,0:T(8,128)S(1)} async-done(((f32[32,8,128]{2,1,0:T(8,128)}), f32[32,8,128]{2,1,0:T(8,128)S(1)}, u32[]{:S(2)}, u32[]{:S(2)}) %all-to-all-start) | async-done | bytes 131104 | tf_op jit(solution)/shard_map/all_to_all | solution.py:494
  48.9 0.6 copy-done.3
  49.5 3.5 %shard_map.97 = (f32[64,128]{1,0:T(8,128)}, f32[64,128]{1,0:T(8,128)}, bf16[128,128]{1,0:T(8,128)(2,1)}, f32[64,128]{1,0:T(8,128)}, f32[64,128]{1,0:T(8,128)}, /*index=5*/f32[64,128]{1,0:T(8,128)}, f32[8,128]{1,0:T(8,128)}) custom-call(f32[1]{0:T(128)} %bitcast.22.shift_ref, f32[32,8,128]{2,1,0:T(8,128)} %copy-done.3, f32[64,128]{1,0:T(8,128)} %get-tuple-element.31.refs_1_, ...), custom_call_target="tpu_custom_call" | custom-call | tf_op jit(solution)/shard_map/pallas_call | solution.py:397
  53.3 1.2 %collective-permute-done.8 = bf16[128,128]{1,0:T(8,128)(2,1)S(1)} collective-permute-done((bf16[128,128]{1,0:T(8,128)(2,1)}, bf16[128,128]{1,0:T(8,128)(2,1)S(1)}, u32[]{:S(2)}, u32[]{:S(2)}) %collective-permute-start.8) | collective-permute-done | bytes 32800 | tf_op jit(solution)/shard_map/ppermute | solution.py:420
  54.5 0.8 pad_maximum_fusion.3.pair_ref
  55.2 0.9 collective-permute-start.11
  56.2 0.9 collective-permute-start.10
  57.1 1.7 %collective-permute-start.9 = (bf16[128,128]{1,0:T(8,128)(2,1)}, bf16[128,128]{1,0:T(8,128)(2,1)S(1)}, u32[]{:S(2)}, u32[]{:S(2)}) collective-permute-start(bf16[128,128]{1,0:T(8,128)(2,1)} %get-tuple-element.32), channel_id=1, source_target_pairs={{0,2},{1,3},{2,0},{3,1},{4,6},{5,7},{6,4},{7,5},{8,10},{9,11},{10,... | collective-permute-start | bytes 98312 | tf_op jit(solution)/shard_map/ppermute | solution.py:420
  58.8 2.4 %collective-permute-done.9 = bf16[128,128]{1,0:T(8,128)(2,1)S(1)} collective-permute-done((bf16[128,128]{1,0:T(8,128)(2,1)}, bf16[128,128]{1,0:T(8,128)(2,1)S(1)}, u32[]{:S(2)}, u32[]{:S(2)}) %collective-permute-start.9) | collective-permute-done | bytes 32800 | tf_op jit(solution)/shard_map/ppermute | solution.py:420
  61.3 1.8 %collective-permute-start.12 = (bf16[5,128,128]{2,1,0:T(8,128)(2,1)S(1)}, bf16[5,128,128]{2,1,0:T(8,128)(2,1)S(1)}, u32[]{:S(2)}, u32[]{:S(2)}) collective-permute-start(bf16[5,128,128]{2,1,0:T(8,128)(2,1)S(1)} %pad_maximum_fusion.1.mine_ref), channel_id=1, source_target_pairs={{0,1},{1,0},{2,3},{3,2},{4,5},{5,4},{6,7},{7,6},{8,9},{9,8},{10,11... | collective-permute-start | bytes 491528 | tf_op jit(solution)/shard_map/ppermute | solution.py:420
  63.1 1.0 %collective-permute-done.12.other_ref = bf16[5,128,128]{2,1,0:T(8,128)(2,1)S(1)} collective-permute-done((bf16[5,128,128]{2,1,0:T(8,128)(2,1)S(1)}, bf16[5,128,128]{2,1,0:T(8,128)(2,1)S(1)}, u32[]{:S(2)}, u32[]{:S(2)}) %collective-permute-start.12) | collective-permute-done | bytes 163872 | tf_op jit(solution)/shard_map/ppermute | solution.py:420
  64.1 0.7 copy-done.7
  64.8 8.3 %shard_map.98 = (f32[64,128]{1,0:T(8,128)}, f32[64,128]{1,0:T(8,128)}, f32[64,128]{1,0:T(8,128)}, f32[64,128]{1,0:T(8,128)}) custom-call(s32[2,128]{1,0:T(2,128)} %bitcast.38, s32[1,128]{1,0:T(1,128)} %slice_bitcast_fusion.1.target_ref, bf16[2,128,128]{2,1,0:T(8,128)(2,1)} %copy-done.4, bf16[5,128,128]{2,1,0:T(8,128)(2,1)} %copy-done.2, ...), custom_call_target="tpu_custom_call" | custom-call | tf_op jit(solution)/shard_map/pallas_call | solution.py:397
  73.1 0.4 collective-permute-start.13
  73.5 1.1 %collective-permute-start.14 = (f32[64,128]{1,0:T(8,128)}, f32[64,128]{1,0:T(8,128)S(1)}, u32[]{:S(2)}, u32[]{:S(2)}) collective-permute-start(f32[64,128]{1,0:T(8,128)} %get-tuple-element.35), channel_id=1, source_target_pairs={{0,2},{1,3},{2,0},{3,1},{4,6},{5,7},{6,4},{7,5},{8,10},{9,11},{10,... | collective-permute-start | bytes 98312 | tf_op jit(solution)/shard_map/ppermute | solution.py:420
  74.6 0.4 collective-permute-start.15
  75.0 2.6 %collective-permute-done.14.refs_2_ = f32[64,128]{1,0:T(8,128)S(1)} collective-permute-done((f32[64,128]{1,0:T(8,128)}, f32[64,128]{1,0:T(8,128)S(1)}, u32[]{:S(2)}, u32[]{:S(2)}) %collective-permute-start.14) | collective-permute-done | bytes 32800 | tf_op jit(solution)/shard_map/ppermute | solution.py:420
  77.6 0.9 collective-permute-done.15.refs_3_
  78.5 0.6 copy-done.14
  79.1 2.7 %shard_map.99 = (f32[64,128]{1,0:T(8,128)}, f32[32,1,128]{2,1,0:T(1,128)}) custom-call(f32[1]{0:T(128)} %bitcast.23.shift_ref, f32[64,128]{1,0:T(8,128)} %get-tuple-element.33.refs_0_, f32[64,128]{1,0:T(8,128)} %copy-done.12, f32[64,128]{1,0:T(8,128)} %copy-done.13, f32[64,128]{1,0:T(8,128)} %copy-done.14, f32[64,128]{1,0:T(8,128)} %get-tuple-element.37.refs_4_, ...), custom_call_target="tpu_custom_call" | custom-call | tf_op jit(solution)/shard_map/pallas_call | solution.py:397
  81.8 10.6 %all_to_all.10.refs_0_ = f32[32,1,128]{2,1,0:T(1,128)} all-to-all(f32[32,1,128]{2,1,0:T(1,128)} %get-tuple-element.39), channel_id=1, replica_groups=mesh['rows'=8,'sub'=4] {'rows','sub'}, dimensions={0} | all-to-all | bytes 32768 | tf_op jit(solution)/shard_map/all_to_all | solution.py:494
  92.4 3.0 %shard_map.100 = (f32[2,8192]{1,0:T(2,128)}, f32[2,60,59]{2,1,0:T(8,128)}, f32[59,2]{1,0:T(8,128)}) custom-call(f32[1]{0:T(128)} %bitcast.24.shift_ref, f32[32,1,128]{2,1,0:T(1,128)} %all_to_all.10.refs_0_, f32[64,128]{1,0:T(8,128)} %get-tuple-element.40.refs_1_, f32[58,8192]{1,0:T(8,128)} %refs_2_.3, f32[64,128]{1,0:T(8,128)} %get-tuple-element.41.refs_3_, ...), custom_call_target="tpu_custom_call" | custom-call | tf_op jit(solution)/shard_map/pallas_call | solution.py:397
  95.4 1.4 %copy.12 = f32[59,2]{0,1:T(2,128)} copy(f32[59,2]{1,0:T(8,128)} %get-tuple-element.47) | data formatting | bytes 944 | tf_op jit(solution)/shard_map/pallas_call | solution.py:397
  96.8 1.6 %copy.11 = f32[2,60,59]{1,0,2:T(2,128)} copy(f32[2,60,59]{2,1,0:T(8,128)} %get-tuple-element.46) | data formatting | bytes 56640 | tf_op jit(solution)/shard_map/pallas_call | solution.py:397
  (37 shorter events, 0.4 us)
Async XLA Ops:
  0.6 10.7 %copy-start = (f32[58,8192]{1,0:T(8,128)S(1)}, f32[58,8192]{1,0:T(8,128)}, u32[]{:S(2)}) copy-start(f32[58,8192]{1,0:T(8,128)} %refs_2_.3) | copy-start | bytes 5701636
  4.7 3.0 %collective-permute-start = (bf16[128,128]{1,0:T(8,128)(2,1)}, bf16[128,128]{1,0:T(8,128)(2,1)S(1)}, u32[]{:S(2)}, u32[]{:S(2)}) collective-permute-start(bf16[128,128]{1,0:T(8,128)(2,1)} %get-tuple-element.24), channel_id=1, source_target_pairs={{0,1},{1,0},{2,3},{3,2},{4,5},{5,4},{6,7},{7,6},{8,9},{9,8},{10,11... | collective-permute-start | bytes 98312 | tf_op jit(solution)/shard_map/ppermute | solution.py:420
  5.2 8.6 %collective-permute-start.1 = (bf16[128,128]{1,0:T(8,128)(2,1)}, bf16[128,128]{1,0:T(8,128)(2,1)S(1)}, u32[]{:S(2)}, u32[]{:S(2)}) collective-permute-start(bf16[128,128]{1,0:T(8,128)(2,1)} %get-tuple-element.24), channel_id=1, source_target_pairs={{0,2},{1,3},{2,0},{3,1},{4,6},{5,7},{6,4},{7,5},{8,10},{9,11},{10,... | collective-permute-start | bytes 98312 | tf_op jit(solution)/shard_map/ppermute | solution.py:420
  8.4 5.3 %copy-start.5 = (bf16[2,128,128]{2,1,0:T(8,128)(2,1)}, bf16[2,128,128]{2,1,0:T(8,128)(2,1)S(1)}, u32[]{:S(2)}) copy-start(bf16[2,128,128]{2,1,0:T(8,128)(2,1)S(1)} %pad_maximum_fusion.2.pair_ref) | copy-start | bytes 196612
  8.4 11.3 %copy-start.15 = (s32[1,1,2,128]{3,2,1,0:T(2,128)S(1)}, s32[1,1,2,128]{3,2,1,0:T(2,128)}, u32[]{:S(2)}) copy-start(s32[1,1,2,128]{3,2,1,0:T(2,128)} %param.9) | copy-start | bytes 3076
  8.5 5.3 %collective-permute-start.3 = (bf16[2,128,128]{2,1,0:T(8,128)(2,1)S(1)}, bf16[2,128,128]{2,1,0:T(8,128)(2,1)S(1)}, u32[]{:S(2)}, u32[]{:S(2)}) collective-permute-start(bf16[2,128,128]{2,1,0:T(8,128)(2,1)S(1)} %pad_maximum_fusion.2.pair_ref), channel_id=1, source_target_pairs={{0,6},{1,31},{2,4},{3,29},{4,2},{5,11},{6,0},{7,9},{8,14},{9,7},{1... | collective-permute-start | bytes 196616 | tf_op jit(solution)/shard_map/ppermute | solution.py:420
  10.9 5.0 %collective-permute-start.2 = (bf16[2,128,128]{2,1,0:T(8,128)(2,1)S(1)}, bf16[2,128,128]{2,1,0:T(8,128)(2,1)S(1)}, u32[]{:S(2)}, u32[]{:S(2)}) collective-permute-start(bf16[2,128,128]{2,1,0:T(8,128)(2,1)S(1)} %pad_maximum_fusion.2.pair_ref), channel_id=1, source_target_pairs={{0,4},{1,29},{2,6},{3,31},{4,0},{5,9},{6,2},{7,11},{8,12},{9,5},{1... | collective-permute-start | bytes 196616 | tf_op jit(solution)/shard_map/ppermute | solution.py:420
  15.9 4.9 %copy-start.1 = (bf16[5,128,128]{2,1,0:T(8,128)(2,1)}, bf16[5,128,128]{2,1,0:T(8,128)(2,1)S(1)}, u32[]{:S(2)}) copy-start(bf16[5,128,128]{2,1,0:T(8,128)(2,1)S(1)} %pad_maximum_fusion.mine_ref) | copy-start | bytes 491524
  15.9 4.9 %collective-permute-start.4 = (bf16[5,128,128]{2,1,0:T(8,128)(2,1)S(1)}, bf16[5,128,128]{2,1,0:T(8,128)(2,1)S(1)}, u32[]{:S(2)}, u32[]{:S(2)}) collective-permute-start(bf16[5,128,128]{2,1,0:T(8,128)(2,1)S(1)} %pad_maximum_fusion.mine_ref), channel_id=1, source_target_pairs={{0,1},{1,0},{2,3},{3,2},{4,5},{5,4},{6,7},{7,6},{8,9},{9,8},{10,11... | collective-permute-start | bytes 491528 | tf_op jit(solution)/shard_map/ppermute | solution.py:420
  20.7 0.7 copy-start.6
  29.7 11.0 %copy-start.8 = (f32[2,58,57]{1,0,2:T(2,128)S(1)}, f32[2,58,57]{1,0,2:T(2,128)}, u32[]{:S(2)}) copy-start(f32[2,58,57]{1,0,2:T(2,128)} %param.13) | copy-start | bytes 79348
  29.7 2.6 %collective-permute-start.5 = (f32[72,128]{1,0:T(8,128)}, f32[72,128]{1,0:T(8,128)S(1)}, u32[]{:S(2)}, u32[]{:S(2)}) collective-permute-start(f32[72,128]{1,0:T(8,128)} %get-tuple-element.26), channel_id=1, source_target_pairs={{0,1},{1,0},{2,3},{3,2},{4,5},{5,4},{6,7},{7,6},{8,9},{9,8},{10,11... | collective-permute-start | bytes 110600 | tf_op jit(solution)/shard_map/ppermute | solution.py:420
  30.1 4.4 %collective-permute-start.6 = (f32[72,128]{1,0:T(8,128)}, f32[72,128]{1,0:T(8,128)S(1)}, u32[]{:S(2)}, u32[]{:S(2)}) collective-permute-start(f32[72,128]{1,0:T(8,128)} %get-tuple-element.27), channel_id=1, source_target_pairs={{0,2},{1,3},{2,0},{3,1},{4,6},{5,7},{6,4},{7,5},{8,10},{9,11},{10,... | collective-permute-start | bytes 110600 | tf_op jit(solution)/shard_map/ppermute | solution.py:420
  30.8 4.0 %collective-permute-start.7 = (f32[72,128]{1,0:T(8,128)}, f32[72,128]{1,0:T(8,128)S(1)}, u32[]{:S(2)}, u32[]{:S(2)}) collective-permute-start(f32[72,128]{1,0:T(8,128)} %get-tuple-element.28), channel_id=1, source_target_pairs={{0,3},{1,2},{2,1},{3,0},{4,7},{5,6},{6,5},{7,4},{8,11},{9,10},{10,... | collective-permute-start | bytes 110600 | tf_op jit(solution)/shard_map/ppermute | solution.py:420
  32.3 2.5 %copy-start.9 = (f32[72,128]{1,0:T(8,128)}, f32[72,128]{1,0:T(8,128)S(1)}, u32[]{:S(2)}) copy-start(f32[72,128]{1,0:T(8,128)S(1)} %collective-permute-done.5.refs_1_) | copy-start | bytes 110596
  34.5 0.6 copy-start.10
  34.8 0.6 copy-start.11
  38.1 10.8 %all-to-all-start = ((f32[32,8,128]{2,1,0:T(8,128)}), f32[32,8,128]{2,1,0:T(8,128)S(1)}, u32[]{:S(2)}, u32[]{:S(2)}) async-start(f32[32,8,128]{2,1,0:T(8,128)} %get-tuple-element.30), calls=%async_computation | async-start | bytes 262144 | tf_op jit(solution)/shard_map/all_to_all | solution.py:494
  48.9 0.6 copy-start.3
  53.0 1.4 %collective-permute-start.8 = (bf16[128,128]{1,0:T(8,128)(2,1)}, bf16[128,128]{1,0:T(8,128)(2,1)S(1)}, u32[]{:S(2)}, u32[]{:S(2)}) collective-permute-start(bf16[128,128]{1,0:T(8,128)(2,1)} %get-tuple-element.32), channel_id=1, source_target_pairs={{0,1},{1,0},{2,3},{3,2},{4,5},{5,4},{6,7},{7,6},{8,9},{9,8},{10,11... | collective-permute-start | bytes 98312 | tf_op jit(solution)/shard_map/ppermute | solution.py:420
  55.2 8.9 %copy-start.4 = (bf16[2,128,128]{2,1,0:T(8,128)(2,1)}, bf16[2,128,128]{2,1,0:T(8,128)(2,1)S(1)}, u32[]{:S(2)}) copy-start(bf16[2,128,128]{2,1,0:T(8,128)(2,1)S(1)} %pad_maximum_fusion.3.pair_ref) | copy-start | bytes 196612
  55.2 6.0 %collective-permute-start.11 = (bf16[2,128,128]{2,1,0:T(8,128)(2,1)S(1)}, bf16[2,128,128]{2,1,0:T(8,128)(2,1)S(1)}, u32[]{:S(2)}, u32[]{:S(2)}) collective-permute-start(bf16[2,128,128]{2,1,0:T(8,128)(2,1)S(1)} %pad_maximum_fusion.3.pair_ref), channel_id=1, source_target_pairs={{0,6},{1,31},{2,4},{3,29},{4,2},{5,11},{6,0},{7,9},{8,14},{9,7},{1... | collective-permute-start | bytes 196616 | tf_op jit(solution)/shard_map/ppermute | solution.py:420
  56.2 5.1 %collective-permute-start.10 = (bf16[2,128,128]{2,1,0:T(8,128)(2,1)S(1)}, bf16[2,128,128]{2,1,0:T(8,128)(2,1)S(1)}, u32[]{:S(2)}, u32[]{:S(2)}) collective-permute-start(bf16[2,128,128]{2,1,0:T(8,128)(2,1)S(1)} %pad_maximum_fusion.3.pair_ref), channel_id=1, source_target_pairs={{0,4},{1,29},{2,6},{3,31},{4,0},{5,9},{6,2},{7,11},{8,12},{9,5},{1... | collective-permute-start | bytes 196616 | tf_op jit(solution)/shard_map/ppermute | solution.py:420
  57.1 4.1 %collective-permute-start.9 = (bf16[128,128]{1,0:T(8,128)(2,1)}, bf16[128,128]{1,0:T(8,128)(2,1)S(1)}, u32[]{:S(2)}, u32[]{:S(2)}) collective-permute-start(bf16[128,128]{1,0:T(8,128)(2,1)} %get-tuple-element.32), channel_id=1, source_target_pairs={{0,2},{1,3},{2,0},{3,1},{4,6},{5,7},{6,4},{7,5},{8,10},{9,11},{10,... | collective-permute-start | bytes 98312 | tf_op jit(solution)/shard_map/ppermute | solution.py:420
  61.3 2.9 %copy-start.2 = (bf16[5,128,128]{2,1,0:T(8,128)(2,1)}, bf16[5,128,128]{2,1,0:T(8,128)(2,1)S(1)}, u32[]{:S(2)}) copy-start(bf16[5,128,128]{2,1,0:T(8,128)(2,1)S(1)} %pad_maximum_fusion.1.mine_ref) | copy-start | bytes 491524
  61.3 2.8 %collective-permute-start.12 = (bf16[5,128,128]{2,1,0:T(8,128)(2,1)S(1)}, bf16[5,128,128]{2,1,0:T(8,128)(2,1)S(1)}, u32[]{:S(2)}, u32[]{:S(2)}) collective-permute-start(bf16[5,128,128]{2,1,0:T(8,128)(2,1)S(1)} %pad_maximum_fusion.1.mine_ref), channel_id=1, source_target_pairs={{0,1},{1,0},{2,3},{3,2},{4,5},{5,4},{6,7},{7,6},{8,9},{9,8},{10,11... | collective-permute-start | bytes 491528 | tf_op jit(solution)/shard_map/ppermute | solution.py:420
  64.1 0.7 copy-start.7
  73.1 1.9 %collective-permute-start.13 = (f32[64,128]{1,0:T(8,128)}, f32[64,128]{1,0:T(8,128)S(1)}, u32[]{:S(2)}, u32[]{:S(2)}) collective-permute-start(f32[64,128]{1,0:T(8,128)} %get-tuple-element.34), channel_id=1, source_target_pairs={{0,1},{1,0},{2,3},{3,2},{4,5},{5,4},{6,7},{7,6},{8,9},{9,8},{10,11... | collective-permute-start | bytes 98312 | tf_op jit(solution)/shard_map/ppermute | solution.py:420
  73.5 4.1 %collective-permute-start.14 = (f32[64,128]{1,0:T(8,128)}, f32[64,128]{1,0:T(8,128)S(1)}, u32[]{:S(2)}, u32[]{:S(2)}) collective-permute-start(f32[64,128]{1,0:T(8,128)} %get-tuple-element.35), channel_id=1, source_target_pairs={{0,2},{1,3},{2,0},{3,1},{4,6},{5,7},{6,4},{7,5},{8,10},{9,11},{10,... | collective-permute-start | bytes 98312 | tf_op jit(solution)/shard_map/ppermute | solution.py:420
  74.6 3.9 %collective-permute-start.15 = (f32[64,128]{1,0:T(8,128)}, f32[64,128]{1,0:T(8,128)S(1)}, u32[]{:S(2)}, u32[]{:S(2)}) collective-permute-start(f32[64,128]{1,0:T(8,128)} %get-tuple-element.36), channel_id=1, source_target_pairs={{0,3},{1,2},{2,1},{3,0},{4,7},{5,6},{6,5},{7,4},{8,11},{9,10},{10,... | collective-permute-start | bytes 98312 | tf_op jit(solution)/shard_map/ppermute | solution.py:420
  75.0 3.5 %copy-start.12 = (f32[64,128]{1,0:T(8,128)}, f32[64,128]{1,0:T(8,128)S(1)}, u32[]{:S(2)}) copy-start(f32[64,128]{1,0:T(8,128)S(1)} %collective-permute-done.13.refs_1_) | copy-start | bytes 98308
  77.6 0.9 copy-start.13
  78.5 0.6 copy-start.14

commit v2 on v1

--- a/solution.py
+++ b/solution.py
@@ -14,14 +14,7 @@
 BF16 = jnp.bfloat16
 VM = pltpu.VMEM
 SM = pltpu.SMEM
-
-
-def vmem():
-    return pl.BlockSpec(memory_space=VM)
-
-
-def smem():
-    return pl.BlockSpec(memory_space=SM)
+GRANT = 24 * 1024 * 1024
 
 
 def iota(shape, axis):
@@ -90,15 +83,30 @@
     return out
 
 
-def start_kernel(last_ref, held_ref, upper_ref, vec_ref):
+def start_kernel(compact_ref, basis_ref, upper_ref, vec_ref, held_ref, last_ref, sems):
     tiles = upper_ref.shape[0]
     n = held_ref.shape[0]
+    groups = tiles // SUBL
     height = -(-n // SUBL) * SUBL
+    span = SUBL * LANES
+    first = pltpu.make_async_copy(
+        compact_ref.at[compact_ref.shape[0] - 1], last_ref, sems.at[groups]
+    )
+    first.start()
+    copies = []
+    for group in range(groups):
+        lanes = pl.ds(group * span, span)
+        copies.append(
+            pltpu.make_async_copy(basis_ref.at[:, lanes], held_ref.at[:, lanes], sems.at[group])
+        )
+        copies[-1].start()
+    first.wait()
     rows = jnp.pad(last_ref[...], ((0, 0), (0, LANES - n)))
     cols = [
         jnp.broadcast_to(row_to_col(rows[i : i + 1], height), (height, LANES)) for i in range(2)
     ]
-    for group in range(tiles // SUBL):
+    for group in range(groups):
+        copies[group].wait()
         upper, lower = combine(held_ref, cols, group)
         at = group * SUBL
         upper_ref[at : at + SUBL] = upper
@@ -107,11 +115,12 @@
 
 
 def tile_kernel(
-    rows_count,
+    block,
     sub_count,
     packed,
-    map_ref,
+    source_ref,
     target_ref,
+    quarter_ref,
     pair_ref,
     mine_ref,
     other_ref,
@@ -122,91 +131,65 @@
     if packed:
         gram_ref, rest = rest[0], rest[1:]
     outs, rest = rest[:sub_count], rest[sub_count:]
-    window_ref, picked_ref, product_ref = rest[:3]
-    step = pl.program_id(0)
-    r = lax.axis_index("rows")
-    s = lax.axis_index("sub")
+    picked_ref, product_ref, buffer_ref, sems = rest[:4]
     tiles = pair_ref.shape[1] // 2
-    slots = product_ref.shape[0]
-    block = damping_ref.shape[0]
+    slots = damping_ref.shape[0]
     part_tiles = sub_count * tiles
 
-    @pl.when(step == 0)
-    def _():
-        def put(value, part, sub, scale):
-            at = pl.multiple_of((part * sub_count + sub) * tiles, tiles)
-            wide = value.astype(F32)
-            if scale is not None:
-                wide = wide * scale
-            window_ref[0, pl.ds(at, tiles)] = wide[:tiles]
-            window_ref[1, pl.ds(at, tiles)] = wide[tiles:]
-
-        put(pair_ref[0], 1, s, None)
-        put(pair_ref[1], 1, s ^ 1, None)
-        towards = jnp.where((r + s) % 2 == 0, 1, -1)
-        half = sub_count // 2
-        for source_ref, base, rel in ((mine_ref, s, towards), (other_ref, s ^ 1, -towards)):
-            for k in range(1, half):
-                put(source_ref[k - 1], 1, base ^ (2 * k), None)
-            inside = jnp.logical_and(r + rel >= 0, r + rel < rows_count)
-            scale = jnp.where(inside, 1.0, 0.0)
-            for k in range(half):
-                for e in range(2):
-                    put(
-                        source_ref[half - 1 + 2 * k + e],
-                        1 + rel,
-                        base ^ (2 * k) ^ e,
-                        scale,
-                    )
-        for t in range(slots):
-            source = jnp.clip(map_ref[1, t], 0, 3 * part_tiles - 1)
-            picked_ref[0, t : t + 1] = window_ref[0, pl.ds(source, 1)]
-            picked_ref[1, t : t + 1] = window_ref[1, pl.ds(source, 1)]
-
-    at = pl.ds(pl.multiple_of(step * block, block), block)
+    copies = []
+    for step in range(slots // block):
+        at = pl.ds(step * block, block)
+        for i, ref in enumerate((damping_ref, stiffness_ref)):
+            copies.append(
+                pltpu.make_async_copy(ref.at[at], buffer_ref.at[i, at], sems.at[i, step])
+            )
+            copies[-1].start()
+
+    window = []
+    for ref in (pair_ref, mine_ref, other_ref):
+        for i in range(ref.shape[0]):
+            window.append(jnp.concatenate([ref[i, :tiles], ref[i, tiles:]], axis=1))
+    window = jnp.concatenate(window, axis=0)
+    depth = window.shape[0]
+    chooser = jnp.where(iota((slots, depth), 1) == source_ref[...], 1.0, 0.0).astype(BF16)
+    picked_ref[...] = jnp.dot(chooser, window, preferred_element_type=F32).astype(BF16)
+
     dims = (((1,), (1,)), ((), ()))
-    result = lax.dot_general(
-        picked_ref[0, at].astype(BF16),
-        damping_ref[...].reshape(block * LANES, LANES),
-        dims,
-        preferred_element_type=F32,
-    ) + lax.dot_general(
-        picked_ref[1, at].astype(BF16),
-        stiffness_ref[...].reshape(block * LANES, LANES),
-        dims,
-        preferred_element_type=F32,
-    )
-    own = jnp.zeros((block, LANES), F32)
-    for t in range(block):
-        own = own + jnp.where(
-            iota((block, LANES), 0) == t, result[:, t * LANES : (t + 1) * LANES], 0.0
+    for step in range(slots // block):
+        at = pl.ds(step * block, block)
+        copies[2 * step].wait()
+        copies[2 * step + 1].wait()
+        both = jnp.concatenate(
+            [buffer_ref[i, at].reshape(block * LANES, LANES) for i in range(2)], axis=1
         )
-    product_ref[at] = own
-
-    @pl.when(step == pl.num_programs(0) - 1)
-    def _():
-        target = target_ref[...]
-        target = jnp.where(target >= 0, target ^ (s * tiles), -1)
-        selector = jnp.where(iota((part_tiles, slots), 0) == target, 1.0, 0.0).astype(BF16)
-        left = product_ref[...]
-        summed = jnp.zeros((part_tiles, LANES), F32)
-        for _ in range(3):
-            piece = left.astype(BF16)
-            summed = summed + jnp.dot(selector, piece, preferred_element_type=F32)
-            left = left - piece.astype(F32)
+        result = lax.dot_general(picked_ref[at], both, dims, preferred_element_type=F32)
+        own = jnp.zeros((block, LANES), F32)
+        for t in range(block):
+            own = jnp.where(
+                iota((block, LANES), 0) == t, result[:, t * LANES : (t + 1) * LANES], own
+            )
+        product_ref[at] = own
+
+    selector = jnp.where(iota((part_tiles, slots), 0) == target_ref[...], 1.0, 0.0).astype(BF16)
+    left = product_ref[...]
+    summed = jnp.zeros((part_tiles, LANES), F32)
+    for _ in range(3):
+        piece = left.astype(BF16)
+        summed = summed + jnp.dot(selector, piece, preferred_element_type=F32)
+        left = left - piece.astype(F32)
+    for k in range(sub_count):
+        outs[k][:tiles] = summed[k * tiles : (k + 1) * tiles]
+    if packed:
+        square_ref = rest[4]
+        n = gram_ref.shape[0]
+        square_ref[...] = jnp.zeros(square_ref.shape, F32)
+        square_ref[:n, :n] = gram_ref[...]
+        share = square_ref.shape[0] // sub_count
         for k in range(sub_count):
-            outs[k][:tiles] = summed[k * tiles : (k + 1) * tiles]
-        if packed:
-            square_ref = rest[3]
-            n = gram_ref.shape[0]
-            square_ref[...] = jnp.zeros(square_ref.shape, F32)
-            square_ref[:n, :n] = gram_ref[...]
-            share = square_ref.shape[0] // sub_count
-            for k in range(sub_count):
-                start = pl.multiple_of((s ^ k) * share, SUBL)
-                low = square_ref[pl.ds(start, SUBL)]
-                high = square_ref[pl.ds(start + SUBL, SUBL)]
-                outs[k][tiles:] = low + pltpu.roll(high, LANES // 2, axis=1)
+            start = pl.multiple_of((quarter_ref[0] ^ k) * share, SUBL)
+            low = square_ref[pl.ds(start, SUBL)]
+            high = square_ref[pl.ds(start + SUBL, SUBL)]
+            outs[k][tiles:] = low + pltpu.roll(high, LANES // 2, axis=1)
 
 
 def inner_kernel(sub_count, packed, shift_ref, *refs):
@@ -298,7 +281,7 @@
         self_mean = sub_sum(lane_sum(jnp.where(lane8 == spot, every, 0.0))) * inverse
     else:
         gram_ref, column_ref, weights_ref = refs[:3]
-        out_refs = refs[3:]
+        out_refs = refs[5:]
         total = packet_ref[0]
         for i in range(1, packet_ref.shape[0]):
             total = total + packet_ref[i]
@@ -332,9 +315,10 @@
     weights = jnp.where(lane[:1] == columns, beta, weights)
     coef_wide = jnp.broadcast_to(coef_col, shape)
     if not last:
-        column_ref, upper_ref, vec_ref, upper_half_out, lower_half_out, gram_out, weights_out = (
-            out_refs
-        )
+        column_ref, upper_ref, vec_ref = out_refs[:3]
+        upper_half_out, lower_half_out, gram_out, weights_out, added_ref = out_refs[3:]
+        added_ref[0, 0:1] = col_to_row(upper_new, height)
+        added_ref[0, 1:2] = col_to_row(lower_new, height)
         upper_half_out[...] = upper_half
         lower_half_out[...] = lower_half
         weights_out[...] = jnp.broadcast_to(weights, (SUBL, LANES))
@@ -360,14 +344,16 @@
             vec_ref[tiles + at : tiles + at + SUBL] = lower.astype(BF16)
     else:
         basis_ref, compact_ref, hess_ref = out_refs
-        compact_ref[0] = upper_half[: n + 1, :n]
-        compact_ref[1] = lower_half[: n + 1, :n]
-        hess = jnp.where(
-            lane == 0,
-            row_to_col(weights_ref[:1], height),
-            row_to_col(weights, height),
-        )
-        hess_ref[...] = hess[:n, :2]
+        before_ref, first_ref = refs[3:5]
+        out_refs = None
+        old, pair, width = before_ref.shape
+        compact_ref[:old, :, :width] = before_ref[...]
+        compact_ref[:old, :, width:] = jnp.zeros((old, pair, n + 1 - width), F32)
+        compact_ref[old : old + 1] = first_ref[:, :, : n + 1]
+        compact_ref[old + 1, 0:1] = col_to_row(upper_new, height)[:, : n + 1]
+        compact_ref[old + 1, 1:2] = col_to_row(lower_new, height)[:, : n + 1]
+        hess_ref[0:1] = weights_ref[:1, :n]
+        hess_ref[1:2] = weights[:, :n]
         coef_last = at_sublane(coef_col, n0)
         for group in range(tiles // SUBL):
             at = group * SUBL
@@ -380,21 +366,48 @@
                 basis_ref[1:2, lanes] = column[k : k + 1]
 
 
-def call(body, outs, args, specs, scratch=(), grid=None):
-    arguments = dict(
-        out_shape=[jax.ShapeDtypeStruct(shape, dtype) for shape, dtype in outs],
+def call(body, outs, args, scratch=(), final=False, far=()):
+    specs, values = [], []
+    for i, value in enumerate(args):
+        space = pltpu.HBM if i in far else SM if value.shape == (1,) else VM
+        specs.append(pl.BlockSpec(memory_space=space))
+        values.append(
+            value if space == SM else pltpu.with_memory_space_constraint(value, space)
+        )
+    return pl.pallas_call(
+        body,
+        out_shape=[
+            jax.ShapeDtypeStruct(shape, dtype) if final else VM(shape, dtype)
+            for shape, dtype in outs
+        ],
         in_specs=specs,
-        out_specs=[vmem()] * len(outs),
+        out_specs=[pl.BlockSpec(memory_space=VM)] * len(outs),
         scratch_shapes=list(scratch),
+        compiler_params=pltpu.CompilerParams(vmem_limit_bytes=GRANT),
+    )(*values)
+
+
+def window_rows(slot_map, rows_count, sub_count, tiles):
+    r = lax.axis_index("rows")
+    s = lax.axis_index("sub")
+    half = sub_count // 2
+    mine = 2
+    other = mine + half - 1 + sub_count
+    source = slot_map[1]
+    part = source // (sub_count * tiles) - 1
+    sub = (source // tiles) % sub_count
+    beside = (sub ^ s) & 1
+    same = sub ^ s
+    within = jnp.where(
+        same < 2, same, jnp.where(beside == 0, mine, other) + (same >> 1) - 1
     )
-    if grid is not None:
-        arguments.update(
-            grid=grid,
-            out_specs=[
-                pl.BlockSpec(shape, lambda i, rank=len(shape): (0,) * rank) for shape, _ in outs
-            ],
-        )
-    return pl.pallas_call(body, **arguments)(*args)
+    towards = jnp.where((r + s) % 2 == 0, 1, -1)
+    away = half - 1 + jnp.where(part == towards, mine + same, other + (same ^ 1))
+    slice_at = jnp.where(part == 0, within, away)
+    inside = (r + part >= 0) & (r + part < rows_count)
+    row = jnp.where(inside, slice_at * tiles + source % tiles, -1)
+    target = jnp.where(slot_map[0] >= 0, slot_map[0] ^ (s * tiles), -1)
+    return row[:, None], target[None, :]
 
 
 def on_device(stiffness_tiles, damping_tiles, tile_map, inv_mass, spectral_shift, basis, compact):
@@ -422,23 +435,29 @@
     def beside(r, s):
         return r ^ 1 if s % 2 == 0 else (((r + 1) ^ 1) - 1) % rows_count
 
-    slot_map = tile_map[0, 0]
     damping = damping_tiles[0, 0]
     stiffness = stiffness_tiles[0, 0]
     shift = spectral_shift.reshape(1)
     mass = inv_mass.reshape(tiles, tile_size)
+    quarter = lax.axis_index("sub").reshape(1)
+    source, target = window_rows(tile_map[0, 0], rows_count, sub_count, tiles)
     field = ((tiles, tile_size), F32)
     vector = ((2 * tiles, tile_size), BF16)
     square = ((height, LANES), F32)
 
-    upper_vec, vectors = call(
-        start_kernel, [field, vector], (compact[:, :, -1], basis), [vmem(), vmem()]
+    columns = compact.transpose(2, 0, 1)
+    upper_vec, vectors, basis = call(
+        start_kernel,
+        [field, vector, (basis.shape, F32)],
+        (columns, basis),
+        [VM((2, held_count), F32), pltpu.SemaphoreType.DMA((tiles // SUBL + 1,))],
+        far=(0, 1),
     )
     padding = ((0, 0), (0, height - compact.shape[1]), (0, LANES - compact.shape[2]))
     halves = jnp.pad(compact, padding)
     upper_half, lower_half = halves[0], halves[1]
     gram = jnp.dot(basis, basis.T, precision=lax.Precision.HIGHEST)
-    column = weights = None
+    column = weights = added = None
     for iteration in range(ITERS):
         packed = iteration == 0
         last = iteration == ITERS - 1
@@ -449,34 +468,22 @@
         mine = jnp.concatenate(mine, axis=0)
         other = swap(mine, lambda r, s: (r, s ^ 1))
         depth = tiles + SUBL if packed else tiles
-        full = lambda shape: pl.BlockSpec(shape, lambda i, rank=len(shape): (0,) * rank)
-        tile_spec = pl.BlockSpec((block, tile_size, tile_size), lambda i: (i, 0, 0))
         scratch = [
-            pltpu.VMEM((2, 3 * sub_count * tiles, LANES), F32),
-            pltpu.VMEM((2, slots, LANES), F32),
-            pltpu.VMEM((slots, LANES), F32),
+            VM((slots, 2 * LANES), BF16),
+            VM((slots, LANES), F32),
+            VM((2, slots, tile_size, tile_size), BF16),
+            pltpu.SemaphoreType.DMA((2, slots // block)),
         ]
-        args = [slot_map, slot_map[:1], pair, mine, other, damping, stiffness]
-        specs = [
-            smem(),
-            full((1, slots)),
-            full(pair.shape),
-            full(mine.shape),
-            full(other.shape),
-            tile_spec,
-            tile_spec,
-        ]
+        args = [source, target, quarter, pair, mine, other, damping, stiffness]
         if packed:
             args.append(gram)
-            specs.append(full(gram.shape))
-            scratch.append(pltpu.VMEM((height, LANES), F32))
+            scratch.append(VM((height, LANES), F32))
         parts = call(
-            functools.partial(tile_kernel, rows_count, sub_count, packed),
+            functools.partial(tile_kernel, block, sub_count, packed),
             [((depth, LANES), F32)] * sub_count,
             args,
-            specs,
             scratch,
-            grid=(slots // block,),
+            far=(6, 7),
         )
         parts = [parts[0]] + [
             swap(parts[k], lambda r, s, k=k: (r, s ^ k)) for k in range(1, sub_count)
@@ -486,33 +493,32 @@
         if not packed:
             args.append(column)
         image, sent = call(
-            functools.partial(inner_kernel, sub_count, packed),
-            [field, (packet, F32)],
-            args,
-            [smem()] + [vmem()] * (len(args) - 1),
+            functools.partial(inner_kernel, sub_count, packed), [field, (packet, F32)], args
         )
         received = lax.all_to_all(sent, every, 0, 0)
         args = [shift, received, image, basis, upper_half, lower_half]
         if not packed:
-            args += [gram, column, weights]
+            args += [gram, column, weights, columns, added]
+        total = held_count + ITERS
         if last:
-            total = held_count + ITERS
             outs = [
                 ((ITERS, local_rows), F32),
-                ((2, total, total - 1), F32),
-                ((total - 1, ITERS), F32),
+                ((total - 1, 2, total), F32),
+                ((ITERS, total - 1), F32),
             ]
         else:
-            outs = [field, field, vector, square, square, square, ((SUBL, LANES), F32)]
+            outs = [field, field, vector, square, square, square]
+            outs += [((SUBL, LANES), F32), ((1, 2, LANES), F32)]
         outs = call(
             functools.partial(update_kernel, unknowns, sub_count, iteration, last),
             outs,
             args,
-            [smem()] + [vmem()] * (len(args) - 1),
+            final=last,
         )
         if not last:
-            column, upper_vec, vectors, upper_half, lower_half, gram, weights = outs
-    return tuple(outs)
+            column, upper_vec, vectors, upper_half, lower_half, gram, weights, added = outs
+    new_basis, compact_out, hessenberg = outs
+    return new_basis, compact_out.transpose(1, 2, 0), hessenberg.T
 
 
 def solution(mesh):

time: 99.3 us -> 75.1 us (0.76)
  Pallas kernels: 31.2 us -> 15.3 us
  local copies, waits for them, and re-layouts: 8.9 us -> 0.25 us
  waiting for transfers between devices: 20.7 us -> 23.6 us
  other arithmetic: 1.6 us -> 0.23 us
    pallas_call x7, Pallas kernels: 31.2 us -> 15.3 us  [call(): pl.pallas_call(body, out_shape=[jax.ShapeDtypeStruct(shape, dtype) if fin...]
    unnamed x33 -> x7, local copies, waits for them, and re-layouts: 3.33 us -> 0.12 us
    pallas_call x2 -> x0, local copies, waits for them, and re-layouts: 2.95 us -> none  [call(): return pl.pallas_call(body, **arguments)(*args)]
    ppermute x16, waiting for transfers between devices: 13.2 us -> 15.6 us  [swap(): return lax.ppermute(value, every, pairs)]
    another operation x2, other arithmetic: 1.56 us -> 0.02 us  [on_device(): pair = jnp.stack([vectors, swap(vectors, lambda r, s: (r, s ^ 1))])]
    squeeze x1, local copies, waits for them, and re-layouts: 1.39 us -> 0.12 us  [window_rows(): source = slot_map[1]]
  transfers between devices with their start and end apart: 17 -> 17, of which waited for: 10 -> 12; matrix products, arithmetic and copies ran while one was open for 5% -> 3% of each run, Pallas kernels for 0% -> 0%
where the time goes in v2:
time: 75.1 us; the launch traced here: 74.8 us
  waiting for transfers between devices  23.6 us (31%)
  starting transfers between devices  21.6 us (29%)
  Pallas kernels  15.3 us (20%)
  blocking collectives  10.7 us (14%)
  matrix products  1.78 us (2%)
  between operations  1.42 us (2%)
    ppermute x16, starting transfers between devices, swap(): return lax.ppermute(value, every, pairs)  19 us
    ppermute x16, waiting for transfers between devices, swap(): return lax.ppermute(value, every, pairs)  15.6 us
    pallas_call x7, Pallas kernels, call(): pl.pallas_call(body, out_shape=[jax.ShapeDtypeStruct(shape, dtype) if fin...  15.3 us
    all_to_all x1, blocking collectives, on_device(): received = lax.all_to_all(sent, every, 0, 0)  10.7 us
    all_to_all x1, waiting for transfers between devices, on_device(): received = lax.all_to_all(sent, every, 0, 0)  8.07 us
    all_to_all x1, starting transfers between devices, on_device(): received = lax.all_to_all(sent, every, 0, 0)  2.57 us
    dot_general x1, matrix products, on_device(): gram = jnp.dot(basis, basis.T, precision=lax.Precision.HIGHEST)  1.78 us
  transfers between devices with their start and end apart: 17, of which 12 were waited for; matrix products, arithmetic and copies ran while one was open for 3% of the time, Pallas kernels for 0%

profile of v2, /device:TPU:0, one launch (start us, length us, event | category | flops | bytes accessed | tf_op | source)
XLA Modules:
  0.0 74.8 jit_solution(5247827079132130676)
XLA Ops:
  0.6 1.7 %shard_map.94 = (f32[64,128]{1,0:T(8,128)S(1)}, bf16[128,128]{1,0:T(8,128)(2,1)S(1)}, f32[58,8192]{1,0:T(8,128)S(1)}) custom-call(f32[57,2,58]{2,1,0:T(2,128)} %bitcast.28, f32[58,8192]{1,0:T(8,128)} %basis_ref.1), custom_call_target="tpu_custom_call" | custom-call | tf_op jit(solution)/shard_map/pallas_call | solution.py:377
  2.3 3.0 %collective-permute-start.1 = (bf16[128,128]{1,0:T(8,128)(2,1)S(1)}, bf16[128,128]{1,0:T(8,128)(2,1)S(1)}, u32[]{:S(2)}, u32[]{:S(2)}) collective-permute-start(bf16[128,128]{1,0:T(8,128)(2,1)S(1)} %get-tuple-element.29), channel_id=1, source_target_pairs={{0,2},{1,3},{2,0},{3,1},{4,6},{5,7},{6,4},{7,5},{8,10},{9,11},{10,... | collective-permute-start | bytes 98312 | tf_op jit(solution)/shard_map/ppermute | solution.py:433
  5.3 0.0 collective-permute-start
  5.3 1.8 %fusion.12.rest_0_ = f32[58,58]{1,0:T(8,128)S(1)} fusion(f32[58,8192]{1,0:T(8,128)S(1)} %get-tuple-element.30.refs_6_.refs_2_), kind=kOutput, calls=%fused_computation.34 | convolution fusion | flops 330694656 | bytes 1914000 | tf_op jit(solution)/shard_map/dot_general | solution.py:459
  7.1 0.0 collective-permute-done
  7.1 1.6 %collective-permute-start.3 = (bf16[2,128,128]{2,1,0:T(8,128)(2,1)S(1)}, bf16[2,128,128]{2,1,0:T(8,128)(2,1)S(1)}, u32[]{:S(2)}, u32[]{:S(2)}) collective-permute-start(bf16[2,128,128]{2,1,0:T(8,128)(2,1)S(1)} %pad_maximum_fusion.2.pair_ref), channel_id=1, source_target_pairs={{0,6},{1,31},{2,4},{3,29},{4,2},{5,11},{6,0},{7,9},{8,14},{9,7},{1... | collective-permute-start | bytes 196616 | tf_op jit(solution)/shard_map/ppermute | solution.py:433
  8.7 0.1 collective-permute-start.2
  8.8 0.0 copy-done.2
  8.8 0.1 copy.10
  8.9 0.0 collective-permute-done.1
  8.9 3.4 %collective-permute-done.3 = bf16[2,128,128]{2,1,0:T(8,128)(2,1)S(1)} collective-permute-done((bf16[2,128,128]{2,1,0:T(8,128)(2,1)S(1)}, bf16[2,128,128]{2,1,0:T(8,128)(2,1)S(1)}, u32[]{:S(2)}, u32[]{:S(2)}) %collective-permute-start.3) | collective-permute-done | bytes 65568 | tf_op jit(solution)/shard_map/ppermute | solution.py:433
  12.4 0.7 collective-permute-done.2
  13.1 4.8 %collective-permute-start.4 = (bf16[5,128,128]{2,1,0:T(8,128)(2,1)S(1)}, bf16[5,128,128]{2,1,0:T(8,128)(2,1)S(1)}, u32[]{:S(2)}, u32[]{:S(2)}) collective-permute-start(bf16[5,128,128]{2,1,0:T(8,128)(2,1)S(1)} %pad_maximum_fusion.mine_ref), channel_id=1, source_target_pairs={{0,1},{1,0},{2,3},{3,2},{4,5},{5,4},{6,7},{7,6},{8,9},{9,8},{10,11... | collective-permute-start | bytes 491528 | tf_op jit(solution)/shard_map/ppermute | solution.py:433
  17.9 0.2 fusion.5.source_ref
  18.0 0.9 %collective-permute-done.4.other_ref = bf16[5,128,128]{2,1,0:T(8,128)(2,1)S(1)} collective-permute-done((bf16[5,128,128]{2,1,0:T(8,128)(2,1)S(1)}, bf16[5,128,128]{2,1,0:T(8,128)(2,1)S(1)}, u32[]{:S(2)}, u32[]{:S(2)}) %collective-permute-start.4) | collective-permute-done | bytes 163872 | tf_op jit(solution)/shard_map/ppermute | solution.py:433
  18.9 4.9 %shard_map.95 = (f32[72,128]{1,0:T(8,128)S(1)}, f32[72,128]{1,0:T(8,128)S(1)}, f32[72,128]{1,0:T(8,128)S(1)}, f32[72,128]{1,0:T(8,128)S(1)}) custom-call(s32[128,1]{1,0:T(8,128)S(1)} %fusion.5.source_ref, s32[1,128]{1,0:T(1,128)S(1)} %get-tuple-element.57.target_ref, s32[1]{0:T(128)} %bitcast.3.quarter_ref, ...), custom_call_target="tpu_custom_call" | custom-call | tf_op jit(solution)/shard_map/pallas_call | solution.py:377
  23.8 0.0 copy-start
  23.8 0.4 collective-permute-start.5
  24.2 1.5 %collective-permute-start.6 = (f32[72,128]{1,0:T(8,128)S(1)}, f32[72,128]{1,0:T(8,128)S(1)}, u32[]{:S(2)}, u32[]{:S(2)}) collective-permute-start(f32[72,128]{1,0:T(8,128)S(1)} %get-tuple-element.33), channel_id=1, source_target_pairs={{0,2},{1,3},{2,0},{3,1},{4,6},{5,7},{6,4},{7,5},{8,10},{9,11},{10,... | collective-permute-start | bytes 110600 | tf_op jit(solution)/shard_map/ppermute | solution.py:433
  25.7 0.0 collective-permute-start.7
  26.4 0.0 collective-permute-done.5.refs_1_
  26.4 1.8 %collective-permute-done.6.refs_2_ = f32[72,128]{1,0:T(8,128)S(1)} collective-permute-done((f32[72,128]{1,0:T(8,128)S(1)}, f32[72,128]{1,0:T(8,128)S(1)}, u32[]{:S(2)}, u32[]{:S(2)}) %collective-permute-start.6) | collective-permute-done | bytes 36896 | tf_op jit(solution)/shard_map/ppermute | solution.py:433
  28.2 1.3 %collective-permute-done.7.refs_3_ = f32[72,128]{1,0:T(8,128)S(1)} collective-permute-done((f32[72,128]{1,0:T(8,128)S(1)}, f32[72,128]{1,0:T(8,128)S(1)}, u32[]{:S(2)}, u32[]{:S(2)}) %collective-permute-start.7) | collective-permute-done | bytes 36896 | tf_op jit(solution)/shard_map/ppermute | solution.py:433
  29.5 1.0 %shard_map.96 = (f32[64,128]{1,0:T(8,128)S(1)}, f32[32,8,128]{2,1,0:T(8,128)}) custom-call(f32[1]{0:T(128)} %bitcast.24.shift_ref, f32[72,128]{1,0:T(8,128)S(1)} %get-tuple-element.31.refs_0_, f32[72,128]{1,0:T(8,128)S(1)} %collective-permute-done.5.refs_1_, f32[72,128]{1,0:T(8,128)S(1)} %collective-permute-done.6.refs_2_, ...), custom_call_target="tpu_custom_call" | custom-call | tf_op jit(solution)/shard_map/pallas_call | solution.py:377
  30.4 2.6 %all-to-all-start = ((f32[32,8,128]{2,1,0:T(8,128)}), f32[32,8,128]{2,1,0:T(8,128)S(1)}, u32[]{:S(2)}, u32[]{:S(2)}) async-start(f32[32,8,128]{2,1,0:T(8,128)} %get-tuple-element.36), calls=%async_computation | async-start | bytes 262144 | tf_op jit(solution)/shard_map/all_to_all | solution.py:498
  33.0 0.1 copy.14
  33.1 8.1 %all-to-all-done.refs_0_ = f32[32,8,128]{2,1,0:T(8,128)S(1)} async-done(((f32[32,8,128]{2,1,0:T(8,128)}), f32[32,8,128]{2,1,0:T(8,128)S(1)}, u32[]{:S(2)}, u32[]{:S(2)}) %all-to-all-start) | async-done | bytes 131104 | tf_op jit(solution)/shard_map/all_to_all | solution.py:498
  41.2 1.2 %shard_map.97 = (f32[64,128]{1,0:T(8,128)S(1)}, f32[64,128]{1,0:T(8,128)S(1)}, bf16[128,128]{1,0:T(8,128)(2,1)S(1)}, f32[64,128]{1,0:T(8,128)S(1)}, f32[64,128]{...) custom-call(f32[1]{0:T(128)} %bitcast.25.shift_ref, ...), custom_call_target="tpu_custom_call" | custom-call | tf_op jit(solution)/shard_map/pallas_call | solution.py:377
  42.4 0.3 collective-permute-start.8
  42.7 1.0 %collective-permute-done.8 = bf16[128,128]{1,0:T(8,128)(2,1)S(1)} collective-permute-done((bf16[128,128]{1,0:T(8,128)(2,1)S(1)}, bf16[128,128]{1,0:T(8,128)(2,1)S(1)}, u32[]{:S(2)}, u32[]{:S(2)}) %collective-permute-start.8) | collective-permute-done | bytes 32800 | tf_op jit(solution)/shard_map/ppermute | solution.py:433
  43.7 0.9 %collective-permute-start.11 = (bf16[2,128,128]{2,1,0:T(8,128)(2,1)S(1)}, bf16[2,128,128]{2,1,0:T(8,128)(2,1)S(1)}, u32[]{:S(2)}, u32[]{:S(2)}) collective-permute-start(bf16[2,128,128]{2,1,0:T(8,128)(2,1)S(1)} %pad_maximum_fusion.3.pair_ref), channel_id=1, source_target_pairs={{0,6},{1,31},{2,4},{3,29},{4,2},{5,11},{6,0},{7,9},{8,14},{9,7},{1... | collective-permute-start | bytes 196616 | tf_op jit(solution)/shard_map/ppermute | solution.py:433
  44.6 0.9 %collective-permute-start.10 = (bf16[2,128,128]{2,1,0:T(8,128)(2,1)S(1)}, bf16[2,128,128]{2,1,0:T(8,128)(2,1)S(1)}, u32[]{:S(2)}, u32[]{:S(2)}) collective-permute-start(bf16[2,128,128]{2,1,0:T(8,128)(2,1)S(1)} %pad_maximum_fusion.3.pair_ref), channel_id=1, source_target_pairs={{0,4},{1,29},{2,6},{3,31},{4,0},{5,9},{6,2},{7,11},{8,12},{9,5},{1... | collective-permute-start | bytes 196616 | tf_op jit(solution)/shard_map/ppermute | solution.py:433
  45.6 1.7 %collective-permute-start.9 = (bf16[128,128]{1,0:T(8,128)(2,1)S(1)}, bf16[128,128]{1,0:T(8,128)(2,1)S(1)}, u32[]{:S(2)}, u32[]{:S(2)}) collective-permute-start(bf16[128,128]{1,0:T(8,128)(2,1)S(1)} %get-tuple-element.38), channel_id=1, source_target_pairs={{0,2},{1,3},{2,0},{3,1},{4,6},{5,7},{6,4},{7,5},{8,10},{9,11},{10,... | collective-permute-start | bytes 98312 | tf_op jit(solution)/shard_map/ppermute | solution.py:433
  47.2 2.2 %collective-permute-done.9 = bf16[128,128]{1,0:T(8,128)(2,1)S(1)} collective-permute-done((bf16[128,128]{1,0:T(8,128)(2,1)S(1)}, bf16[128,128]{1,0:T(8,128)(2,1)S(1)}, u32[]{:S(2)}, u32[]{:S(2)}) %collective-permute-start.9) | collective-permute-done | bytes 32800 | tf_op jit(solution)/shard_map/ppermute | solution.py:433
  49.5 0.0 collective-permute-done.11
  49.5 0.1 collective-permute-done.10
  49.6 1.9 %collective-permute-start.12 = (bf16[5,128,128]{2,1,0:T(8,128)(2,1)S(1)}, bf16[5,128,128]{2,1,0:T(8,128)(2,1)S(1)}, u32[]{:S(2)}, u32[]{:S(2)}) collective-permute-start(bf16[5,128,128]{2,1,0:T(8,128)(2,1)S(1)} %pad_maximum_fusion.1.mine_ref), channel_id=1, source_target_pairs={{0,1},{1,0},{2,3},{3,2},{4,5},{5,4},{6,7},{7,6},{8,9},{9,8},{10,11... | collective-permute-start | bytes 491528 | tf_op jit(solution)/shard_map/ppermute | solution.py:433
  51.5 1.0 %collective-permute-done.12.other_ref = bf16[5,128,128]{2,1,0:T(8,128)(2,1)S(1)} collective-permute-done((bf16[5,128,128]{2,1,0:T(8,128)(2,1)S(1)}, bf16[5,128,128]{2,1,0:T(8,128)(2,1)S(1)}, u32[]{:S(2)}, u32[]{:S(2)}) %collective-permute-start.12) | collective-permute-done | bytes 163872 | tf_op jit(solution)/shard_map/ppermute | solution.py:433
  52.5 4.9 %shard_map.98 = (f32[64,128]{1,0:T(8,128)S(1)}, f32[64,128]{1,0:T(8,128)S(1)}, f32[64,128]{1,0:T(8,128)S(1)}, f32[64,128]{1,0:T(8,128)S(1)}) custom-call(s32[128,1]{1,0:T(8,128)S(1)} %fusion.5.source_ref, s32[1,128]{1,0:T(1,128)S(1)} %get-tuple-element.57.target_ref, s32[1]{0:T(128)} %bitcast.3.quarter_ref, ...), custom_call_target="tpu_custom_call" | custom-call | tf_op jit(solution)/shard_map/pallas_call | solution.py:377
  57.4 0.4 collective-permute-start.13
  57.8 1.0 %collective-permute-start.14 = (f32[64,128]{1,0:T(8,128)S(1)}, f32[64,128]{1,0:T(8,128)S(1)}, u32[]{:S(2)}, u32[]{:S(2)}) collective-permute-start(f32[64,128]{1,0:T(8,128)S(1)} %get-tuple-element.41), channel_id=1, source_target_pairs={{0,2},{1,3},{2,0},{3,1},{4,6},{5,7},{6,4},{7,5},{8,10},{9,11},{10,... | collective-permute-start | bytes 98312 | tf_op jit(solution)/shard_map/ppermute | solution.py:433
  58.8 0.5 collective-permute-start.15
  59.3 0.0 collective-permute-done.13.refs_1_
  59.3 2.4 %collective-permute-done.14.refs_2_ = f32[64,128]{1,0:T(8,128)S(1)} collective-permute-done((f32[64,128]{1,0:T(8,128)S(1)}, f32[64,128]{1,0:T(8,128)S(1)}, u32[]{:S(2)}, u32[]{:S(2)}) %collective-permute-start.14) | collective-permute-done | bytes 32800 | tf_op jit(solution)/shard_map/ppermute | solution.py:433
  61.7 0.7 collective-permute-done.15.refs_3_
  62.4 0.4 shard_map.99
  62.9 10.7 %all_to_all.10.refs_0_ = f32[32,1,128]{2,1,0:T(1,128)S(1)} all-to-all(f32[32,1,128]{2,1,0:T(1,128)S(1)} %get-tuple-element.45), channel_id=1, replica_groups=mesh['rows'=8,'sub'=4] {'rows','sub'}, dimensions={0} | all-to-all | bytes 32768 | tf_op jit(solution)/shard_map/all_to_all | solution.py:498
  73.5 1.3 %shard_map.100 = (f32[2,8192]{1,0:T(2,128)}, f32[59,2,60]{2,1,0:T(2,128)}, f32[2,59]{1,0:T(2,128)}) custom-call(f32[1]{0:T(128)} %bitcast.27.shift_ref, f32[32,1,128]{2,1,0:T(1,128)S(1)} %all_to_all.10.refs_0_, f32[64,128]{1,0:T(8,128)S(1)} %get-tuple-element.46.refs_1_, f32[58,8192]{1,0:T(8,128)S(1)} %get-tuple-element.30.refs_6_.refs_2_, ...), custom_call_target="tpu_custom_call" | custom-call | tf_op jit(solution)/shard_map/pallas_call | solution.py:377
  (10 shorter events, 0.1 us)
Async XLA Ops:
  2.3 6.6 %collective-permute-start.1 = (bf16[128,128]{1,0:T(8,128)(2,1)S(1)}, bf16[128,128]{1,0:T(8,128)(2,1)S(1)}, u32[]{:S(2)}, u32[]{:S(2)}) collective-permute-start(bf16[128,128]{1,0:T(8,128)(2,1)S(1)} %get-tuple-element.29), channel_id=1, source_target_pairs={{0,2},{1,3},{2,0},{3,1},{4,6},{5,7},{6,4},{7,5},{8,10},{9,11},{10,... | collective-permute-start | bytes 98312 | tf_op jit(solution)/shard_map/ppermute | solution.py:433
  5.3 1.8 %collective-permute-start = (bf16[128,128]{1,0:T(8,128)(2,1)S(1)}, bf16[128,128]{1,0:T(8,128)(2,1)S(1)}, u32[]{:S(2)}, u32[]{:S(2)}) collective-permute-start(bf16[128,128]{1,0:T(8,128)(2,1)S(1)} %get-tuple-element.29), channel_id=1, source_target_pairs={{0,1},{1,0},{2,3},{3,2},{4,5},{5,4},{6,7},{7,6},{8,9},{9,8},{10,11... | collective-permute-start | bytes 98312 | tf_op jit(solution)/shard_map/ppermute | solution.py:433
  5.3 3.5 %copy-start.2 = (s32[1,1,2,128]{3,2,1,0:T(2,128)S(1)}, s32[1,1,2,128]{3,2,1,0:T(2,128)}, u32[]{:S(2)}) copy-start(s32[1,1,2,128]{3,2,1,0:T(2,128)} %param.9) | copy-start | bytes 3076
  7.1 5.2 %collective-permute-start.3 = (bf16[2,128,128]{2,1,0:T(8,128)(2,1)S(1)}, bf16[2,128,128]{2,1,0:T(8,128)(2,1)S(1)}, u32[]{:S(2)}, u32[]{:S(2)}) collective-permute-start(bf16[2,128,128]{2,1,0:T(8,128)(2,1)S(1)} %pad_maximum_fusion.2.pair_ref), channel_id=1, source_target_pairs={{0,6},{1,31},{2,4},{3,29},{4,2},{5,11},{6,0},{7,9},{8,14},{9,7},{1... | collective-permute-start | bytes 196616 | tf_op jit(solution)/shard_map/ppermute | solution.py:433
  8.7 4.4 %collective-permute-start.2 = (bf16[2,128,128]{2,1,0:T(8,128)(2,1)S(1)}, bf16[2,128,128]{2,1,0:T(8,128)(2,1)S(1)}, u32[]{:S(2)}, u32[]{:S(2)}) collective-permute-start(bf16[2,128,128]{2,1,0:T(8,128)(2,1)S(1)} %pad_maximum_fusion.2.pair_ref), channel_id=1, source_target_pairs={{0,4},{1,29},{2,6},{3,31},{4,0},{5,9},{6,2},{7,11},{8,12},{9,5},{1... | collective-permute-start | bytes 196616 | tf_op jit(solution)/shard_map/ppermute | solution.py:433
  13.1 5.8 %collective-permute-start.4 = (bf16[5,128,128]{2,1,0:T(8,128)(2,1)S(1)}, bf16[5,128,128]{2,1,0:T(8,128)(2,1)S(1)}, u32[]{:S(2)}, u32[]{:S(2)}) collective-permute-start(bf16[5,128,128]{2,1,0:T(8,128)(2,1)S(1)} %pad_maximum_fusion.mine_ref), channel_id=1, source_target_pairs={{0,1},{1,0},{2,3},{3,2},{4,5},{5,4},{6,7},{7,6},{8,9},{9,8},{10,11... | collective-permute-start | bytes 491528 | tf_op jit(solution)/shard_map/ppermute | solution.py:433
  18.9 10.6 %copy-start.1 = (f32[8192]{0:T(1024)S(1)}, f32[8192]{0:T(1024)}, u32[]{:S(2)}) copy-start(f32[8192]{0:T(1024)} %param.10) | copy-start | bytes 98308
  23.8 9.2 %copy-start = (f32[2,58,57]{1,0,2:T(2,128)S(1)}, f32[2,58,57]{1,0,2:T(2,128)}, u32[]{:S(2)}) copy-start(f32[2,58,57]{1,0,2:T(2,128)} %param.13) | copy-start | bytes 79348
  23.8 2.6 %collective-permute-start.5 = (f32[72,128]{1,0:T(8,128)S(1)}, f32[72,128]{1,0:T(8,128)S(1)}, u32[]{:S(2)}, u32[]{:S(2)}) collective-permute-start(f32[72,128]{1,0:T(8,128)S(1)} %get-tuple-element.32), channel_id=1, source_target_pairs={{0,1},{1,0},{2,3},{3,2},{4,5},{5,4},{6,7},{7,6},{8,9},{9,8},{10,11... | collective-permute-start | bytes 110600 | tf_op jit(solution)/shard_map/ppermute | solution.py:433
  24.2 4.0 %collective-permute-start.6 = (f32[72,128]{1,0:T(8,128)S(1)}, f32[72,128]{1,0:T(8,128)S(1)}, u32[]{:S(2)}, u32[]{:S(2)}) collective-permute-start(f32[72,128]{1,0:T(8,128)S(1)} %get-tuple-element.33), channel_id=1, source_target_pairs={{0,2},{1,3},{2,0},{3,1},{4,6},{5,7},{6,4},{7,5},{8,10},{9,11},{10,... | collective-permute-start | bytes 110600 | tf_op jit(solution)/shard_map/ppermute | solution.py:433
  25.7 3.7 %collective-permute-start.7 = (f32[72,128]{1,0:T(8,128)S(1)}, f32[72,128]{1,0:T(8,128)S(1)}, u32[]{:S(2)}, u32[]{:S(2)}) collective-permute-start(f32[72,128]{1,0:T(8,128)S(1)} %get-tuple-element.34), channel_id=1, source_target_pairs={{0,3},{1,2},{2,1},{3,0},{4,7},{5,6},{6,5},{7,4},{8,11},{9,10},{10,... | collective-permute-start | bytes 110600 | tf_op jit(solution)/shard_map/ppermute | solution.py:433
  30.4 10.8 %all-to-all-start = ((f32[32,8,128]{2,1,0:T(8,128)}), f32[32,8,128]{2,1,0:T(8,128)S(1)}, u32[]{:S(2)}, u32[]{:S(2)}) async-start(f32[32,8,128]{2,1,0:T(8,128)} %get-tuple-element.36), calls=%async_computation | async-start | bytes 262144 | tf_op jit(solution)/shard_map/all_to_all | solution.py:498
  42.4 1.3 %collective-permute-start.8 = (bf16[128,128]{1,0:T(8,128)(2,1)S(1)}, bf16[128,128]{1,0:T(8,128)(2,1)S(1)}, u32[]{:S(2)}, u32[]{:S(2)}) collective-permute-start(bf16[128,128]{1,0:T(8,128)(2,1)S(1)} %get-tuple-element.38), channel_id=1, source_target_pairs={{0,1},{1,0},{2,3},{3,2},{4,5},{5,4},{6,7},{7,6},{8,9},{9,8},{10,11... | collective-permute-start | bytes 98312 | tf_op jit(solution)/shard_map/ppermute | solution.py:433
  43.7 5.8 %collective-permute-start.11 = (bf16[2,128,128]{2,1,0:T(8,128)(2,1)S(1)}, bf16[2,128,128]{2,1,0:T(8,128)(2,1)S(1)}, u32[]{:S(2)}, u32[]{:S(2)}) collective-permute-start(bf16[2,128,128]{2,1,0:T(8,128)(2,1)S(1)} %pad_maximum_fusion.3.pair_ref), channel_id=1, source_target_pairs={{0,6},{1,31},{2,4},{3,29},{4,2},{5,11},{6,0},{7,9},{8,14},{9,7},{1... | collective-permute-start | bytes 196616 | tf_op jit(solution)/shard_map/ppermute | solution.py:433
  44.6 5.0 %collective-permute-start.10 = (bf16[2,128,128]{2,1,0:T(8,128)(2,1)S(1)}, bf16[2,128,128]{2,1,0:T(8,128)(2,1)S(1)}, u32[]{:S(2)}, u32[]{:S(2)}) collective-permute-start(bf16[2,128,128]{2,1,0:T(8,128)(2,1)S(1)} %pad_maximum_fusion.3.pair_ref), channel_id=1, source_target_pairs={{0,4},{1,29},{2,6},{3,31},{4,0},{5,9},{6,2},{7,11},{8,12},{9,5},{1... | collective-permute-start | bytes 196616 | tf_op jit(solution)/shard_map/ppermute | solution.py:433
  45.6 3.9 %collective-permute-start.9 = (bf16[128,128]{1,0:T(8,128)(2,1)S(1)}, bf16[128,128]{1,0:T(8,128)(2,1)S(1)}, u32[]{:S(2)}, u32[]{:S(2)}) collective-permute-start(bf16[128,128]{1,0:T(8,128)(2,1)S(1)} %get-tuple-element.38), channel_id=1, source_target_pairs={{0,2},{1,3},{2,0},{3,1},{4,6},{5,7},{6,4},{7,5},{8,10},{9,11},{10,... | collective-permute-start | bytes 98312 | tf_op jit(solution)/shard_map/ppermute | solution.py:433
  49.6 2.9 %collective-permute-start.12 = (bf16[5,128,128]{2,1,0:T(8,128)(2,1)S(1)}, bf16[5,128,128]{2,1,0:T(8,128)(2,1)S(1)}, u32[]{:S(2)}, u32[]{:S(2)}) collective-permute-start(bf16[5,128,128]{2,1,0:T(8,128)(2,1)S(1)} %pad_maximum_fusion.1.mine_ref), channel_id=1, source_target_pairs={{0,1},{1,0},{2,3},{3,2},{4,5},{5,4},{6,7},{7,6},{8,9},{9,8},{10,11... | collective-permute-start | bytes 491528 | tf_op jit(solution)/shard_map/ppermute | solution.py:433
  57.4 1.9 %collective-permute-start.13 = (f32[64,128]{1,0:T(8,128)S(1)}, f32[64,128]{1,0:T(8,128)S(1)}, u32[]{:S(2)}, u32[]{:S(2)}) collective-permute-start(f32[64,128]{1,0:T(8,128)S(1)} %get-tuple-element.40), channel_id=1, source_target_pairs={{0,1},{1,0},{2,3},{3,2},{4,5},{5,4},{6,7},{7,6},{8,9},{9,8},{10,11... | collective-permute-start | bytes 98312 | tf_op jit(solution)/shard_map/ppermute | solution.py:433
  57.8 3.9 %collective-permute-start.14 = (f32[64,128]{1,0:T(8,128)S(1)}, f32[64,128]{1,0:T(8,128)S(1)}, u32[]{:S(2)}, u32[]{:S(2)}) collective-permute-start(f32[64,128]{1,0:T(8,128)S(1)} %get-tuple-element.41), channel_id=1, source_target_pairs={{0,2},{1,3},{2,0},{3,1},{4,6},{5,7},{6,4},{7,5},{8,10},{9,11},{10,... | collective-permute-start | bytes 98312 | tf_op jit(solution)/shard_map/ppermute | solution.py:433
  58.8 3.6 %collective-permute-start.15 = (f32[64,128]{1,0:T(8,128)S(1)}, f32[64,128]{1,0:T(8,128)S(1)}, u32[]{:S(2)}, u32[]{:S(2)}) collective-permute-start(f32[64,128]{1,0:T(8,128)S(1)} %get-tuple-element.42), channel_id=1, source_target_pairs={{0,3},{1,2},{2,1},{3,0},{4,7},{5,6},{6,5},{7,4},{8,11},{9,10},{10,... | collective-permute-start | bytes 98312 | tf_op jit(solution)/shard_map/ppermute | solution.py:433

commit v3 on v2

--- a/solution.py
+++ b/solution.py
@@ -14,7 +14,8 @@
 BF16 = jnp.bfloat16
 VM = pltpu.VMEM
 SM = pltpu.SMEM
-GRANT = 24 * 1024 * 1024
+GRANT = 16 * 1024 * 1024
+JOIN_GRANT = 1024 * 1024
 
 
 def iota(shape, axis):
@@ -114,6 +115,26 @@
         vec_ref[tiles + at : tiles + at + SUBL] = lower.astype(BF16)
 
 
+def join_kernel(*refs):
+    out_ref = refs[-1]
+    at = 0
+    for ref in refs[:-2]:
+        out_ref[at : at + ref.shape[0]] = ref[...]
+        at += ref.shape[0]
+
+
+def load_kernel(pieces, source_ref, *refs):
+    target_ref, sems = refs[-2:]
+    size = target_ref.shape[0] // pieces
+    copies = []
+    for i in range(pieces):
+        at = pl.ds(i * size, size)
+        copies.append(pltpu.make_async_copy(source_ref.at[at], target_ref.at[at], sems.at[i]))
+        copies[-1].start()
+    for copy in copies:
+        copy.wait()
+
+
 def tile_kernel(
     block,
     sub_count,
@@ -125,6 +146,7 @@
     mine_ref,
     other_ref,
     damping_ref,
+    front_ref,
     stiffness_ref,
     *rest,
 ):
@@ -136,14 +158,16 @@
     slots = damping_ref.shape[0]
     part_tiles = sub_count * tiles
 
+    half = slots // 2
     copies = []
-    for step in range(slots // block):
-        at = pl.ds(step * block, block)
-        for i, ref in enumerate((damping_ref, stiffness_ref)):
-            copies.append(
-                pltpu.make_async_copy(ref.at[at], buffer_ref.at[i, at], sems.at[i, step])
+    for i in range(half // block):
+        at = pl.ds(i * block, block)
+        copies.append(
+            pltpu.make_async_copy(
+                damping_ref.at[pl.ds(half + i * block, block)], buffer_ref.at[at], sems.at[i]
             )
-            copies[-1].start()
+        )
+        copies[-1].start()
 
     window = []
     for ref in (pair_ref, mine_ref, other_ref):
@@ -157,10 +181,13 @@
     dims = (((1,), (1,)), ((), ()))
     for step in range(slots // block):
         at = pl.ds(step * block, block)
-        copies[2 * step].wait()
-        copies[2 * step + 1].wait()
+        if step * block == half:
+            for copy in copies:
+                copy.wait()
+        ref = buffer_ref if step * block >= half else front_ref
+        left = ref[pl.ds(step * block % half, block)]
         both = jnp.concatenate(
-            [buffer_ref[i, at].reshape(block * LANES, LANES) for i in range(2)], axis=1
+            [value.reshape(block * LANES, LANES) for value in (left, stiffness_ref[at])], axis=1
         )
         result = lax.dot_general(picked_ref[at], both, dims, preferred_element_type=F32)
         own = jnp.zeros((block, LANES), F32)
@@ -366,7 +393,7 @@
                 basis_ref[1:2, lanes] = column[k : k + 1]
 
 
-def call(body, outs, args, scratch=(), final=False, far=()):
+def call(body, outs, args, scratch=(), final=False, far=(), grant=GRANT, cost=None):
     specs, values = [], []
     for i, value in enumerate(args):
         space = pltpu.HBM if i in far else SM if value.shape == (1,) else VM
@@ -383,8 +410,31 @@
         in_specs=specs,
         out_specs=[pl.BlockSpec(memory_space=VM)] * len(outs),
         scratch_shapes=list(scratch),
-        compiler_params=pltpu.CompilerParams(vmem_limit_bytes=GRANT),
+        compiler_params=pltpu.CompilerParams(vmem_limit_bytes=grant),
+        cost_estimate=cost,
     )(*values)
+
+
+def load(array, count, pieces, before):
+    shape = (count,) + array.shape[1:]
+    return call(
+        functools.partial(load_kernel, pieces),
+        [(shape, array.dtype)],
+        [array] + before,
+        [pltpu.SemaphoreType.DMA((pieces,))],
+        far=(0,),
+        grant=JOIN_GRANT,
+        cost=pl.CostEstimate(
+            flops=0,
+            bytes_accessed=4 * array.size * count // array.shape[0],
+            transcendentals=0,
+        ),
+    )[0]
+
+
+def join(values, after):
+    shape = (sum(value.shape[0] for value in values),) + values[0].shape[1:]
+    return call(join_kernel, [(shape, values[0].dtype)], values + [after], grant=JOIN_GRANT)[0]
 
 
 def window_rows(slot_map, rows_count, sub_count, tiles):
@@ -456,25 +506,32 @@
     padding = ((0, 0), (0, height - compact.shape[1]), (0, LANES - compact.shape[2]))
     halves = jnp.pad(compact, padding)
     upper_half, lower_half = halves[0], halves[1]
-    gram = jnp.dot(basis, basis.T, precision=lax.Precision.HIGHEST)
+    pieces = slots // block
     column = weights = added = None
     for iteration in range(ITERS):
         packed = iteration == 0
         last = iteration == ITERS - 1
         pair = jnp.stack([vectors, swap(vectors, lambda r, s: (r, s ^ 1))])
         mine = [
-            swap(vectors, lambda r, s, k=k: (r, s ^ (2 * k)))[None] for k in range(1, half)
+            swap(vectors[None], lambda r, s, k=k: (r, s ^ (2 * k))) for k in range(1, half)
         ] + [swap(pair, lambda r, s, k=k: (beside(r, s), s ^ (2 * k))) for k in range(half)]
-        mine = jnp.concatenate(mine, axis=0)
+        before = [pair]
+        if packed:
+            _, late = lax.optimization_barrier((pair, basis))
+            gram = jnp.dot(late, late.T, precision=lax.Precision.HIGHEST)
+            before += [gram, source, target, upper_half, lower_half]
+        loaded = load(stiffness, slots, pieces, before)
+        mine = join(mine, loaded)
         other = swap(mine, lambda r, s: (r, s ^ 1))
+        loaded_half = load(damping, slots // 2, pieces // 2, [mine])
         depth = tiles + SUBL if packed else tiles
         scratch = [
             VM((slots, 2 * LANES), BF16),
             VM((slots, LANES), F32),
-            VM((2, slots, tile_size, tile_size), BF16),
-            pltpu.SemaphoreType.DMA((2, slots // block)),
+            VM((slots // 2, tile_size, tile_size), BF16),
+            pltpu.SemaphoreType.DMA((pieces // 2,)),
         ]
-        args = [source, target, quarter, pair, mine, other, damping, stiffness]
+        args = [source, target, quarter, pair, mine, other, damping, loaded_half, loaded]
         if packed:
             args.append(gram)
             scratch.append(VM((height, LANES), F32))
@@ -483,7 +540,7 @@
             [((depth, LANES), F32)] * sub_count,
             args,
             scratch,
-            far=(6, 7),
+            far=(6,),
         )
         parts = [parts[0]] + [
             swap(parts[k], lambda r, s, k=k: (r, s ^ k)) for k in range(1, sub_count)

time: 75.1 us -> 69.9 us (0.931)
  waiting for transfers between devices: 23.6 us -> 6.15 us
  blocking collectives: 10.7 us -> 22 us
  Pallas kernels: 15.3 us -> 18.5 us
  starting transfers between devices: 21.6 us -> 19.2 us
    all_to_all x1 -> x2, blocking collectives: 10.7 us -> 22 us  [on_device(): received = lax.all_to_all(sent, every, 0, 0)]
    ppermute x16, waiting for transfers between devices: 15.6 us -> 6.15 us  [swap(): return lax.ppermute(value, every, pairs)]
    all_to_all x1 -> x0, waiting for transfers between devices: 8.07 us -> none  [on_device(): received = lax.all_to_all(sent, every, 0, 0)]
    pallas_call x7 -> x13, Pallas kernels: 15.3 us -> 18.5 us  [call(): pl.pallas_call(body, out_shape=[jax.ShapeDtypeStruct(shape, dtype) if fin...]
    all_to_all x1 -> x0, starting transfers between devices: 2.57 us -> none  [on_device(): received = lax.all_to_all(sent, every, 0, 0)]
  transfers between devices with their start and end apart: 17 -> 16, of which waited for: 12 -> 6; matrix products, arithmetic and copies ran while one was open for 3% -> 3% of each run, Pallas kernels for 0% -> 11%
where the time goes in v3:
time: 69.9 us; the launch traced here: 69.6 us
  blocking collectives  22 us (31%)
  starting transfers between devices  19.2 us (27%)
  Pallas kernels  18.5 us (26%)
  waiting for transfers between devices  6.15 us (9%)
  matrix products  1.77 us (3%)
  between operations  1.52 us (2%)
    all_to_all x2, blocking collectives, on_device(): received = lax.all_to_all(sent, every, 0, 0)  22 us
    ppermute x16, starting transfers between devices, swap(): return lax.ppermute(value, every, pairs)  19.2 us
    pallas_call x13, Pallas kernels, call(): pl.pallas_call(body, out_shape=[jax.ShapeDtypeStruct(shape, dtype) if fin...  18.5 us
    ppermute x16, waiting for transfers between devices, swap(): return lax.ppermute(value, every, pairs)  6.15 us
    dot_general x1, matrix products, on_device(): gram = jnp.dot(late, late.T, precision=lax.Precision.HIGHEST)  1.77 us
  transfers between devices with their start and end apart: 16, of which 6 were waited for; matrix products, arithmetic and copies ran while one was open for 3% of the time, Pallas kernels for 11%

profile of v3, /device:TPU:0, one launch (start us, length us, event | category | flops | bytes accessed | tf_op | source)
XLA Modules:
  0.0 69.6 jit_solution(13597808410521277865)
XLA Ops:
  0.7 1.7 %shard_map.94 = (f32[64,128]{1,0:T(8,128)S(1)}, bf16[128,128]{1,0:T(8,128)(2,1)S(1)}, f32[58,8192]{1,0:T(8,128)S(1)}) custom-call(f32[57,2,58]{2,1,0:T(2,128)} %bitcast.26, f32[58,8192]{1,0:T(8,128)} %basis_ref.1), custom_call_target="tpu_custom_call" | custom-call | tf_op jit(solution)/shard_map/pallas_call | solution.py:404
  2.3 0.6 collective-permute-start
  2.9 2.6 %collective-permute-start.1 = (bf16[1,128,128]{2,1,0:T(8,128)(2,1)S(1)}, bf16[1,128,128]{2,1,0:T(8,128)(2,1)S(1)}, u32[]{:S(2)}, u32[]{:S(2)}) collective-permute-start(bf16[1,128,128]{2,1,0:T(8,128)(2,1)S(1)} %bitcast.30), channel_id=1, source_target_pairs={{0,2},{1,3},{2,0},{3,1},{4,6},{5,7},{6,4},{7,5},{8,10},{9,11},{10,... | collective-permute-start | bytes 98312 | tf_op jit(solution)/shard_map/ppermute | solution.py:483
  5.4 0.1 copy.14
  5.6 0.1 copy.10
  5.7 0.2 fusion.5.refs_2_.source_ref
  5.9 0.0 collective-permute-done
  5.9 1.7 %collective-permute-start.3 = (bf16[2,128,128]{2,1,0:T(8,128)(2,1)S(1)}, bf16[2,128,128]{2,1,0:T(8,128)(2,1)S(1)}, u32[]{:S(2)}, u32[]{:S(2)}) collective-permute-start(bf16[2,128,128]{2,1,0:T(8,128)(2,1)S(1)} %pad_maximum_fusion.refs_0_.pair_ref), channel_id=1, source_target_pairs={{0,6},{1,31},{2,4},{3,29},{4,2},{5,11},{6,0},{7,9},{8,14},{9,7},{1... | collective-permute-start | bytes 196616 | tf_op jit(solution)/shard_map/ppermute | solution.py:483
  7.6 0.5 collective-permute-start.2
  8.1 1.8 %fusion.12.refs_1_.rest_0_ = f32[58,58]{1,0:T(8,128)S(1)} fusion(f32[58,8192]{1,0:T(8,128)S(1)} %get-tuple-element.32.refs_6_.refs_2_), kind=kOutput, calls=%fused_computation.32 | convolution fusion | flops 330694656 | bytes 1914000 | tf_op jit(solution)/shard_map/dot_general | solution.py:521
  9.9 2.2 %shard_map.95.refs_3_.stiffness_ref = bf16[128,128,128]{2,1,0:T(8,128)(2,1)S(1)} custom-call(bf16[128,128,128]{2,1,0:T(8,128)(2,1)} %bitcast.38, bf16[2,128,128]{2,1,0:T(8,128)(2,1)S(1)} %pad_maximum_fusion.refs_0_.pair_ref, f32[58,58]{1,0:T(8,128)S(1)} %fusion.12.refs_1_.rest_0_, s32[128,1]{1,0:T(8,128)S(1)} %fusion.5.refs_2_.source_ref, ...), custom_call_target="tpu_custom_call" | custom-call | bytes 8388608 | tf_op jit(solution)/shard_map/pallas_call | solution.py:404
  12.1 0.0 collective-permute-done.1.refs_0_
  12.1 0.0 collective-permute-done.3.refs_2_
  12.1 0.0 collective-permute-done.2.refs_1_
  12.2 4.2 %collective-permute-start.4 = (bf16[5,128,128]{2,1,0:T(8,128)(2,1)S(1)}, bf16[5,128,128]{2,1,0:T(8,128)(2,1)S(1)}, u32[]{:S(2)}, u32[]{:S(2)}) collective-permute-start(bf16[5,128,128]{2,1,0:T(8,128)(2,1)S(1)} %shard_map.96.refs_0_.mine_ref), channel_id=1, source_target_pairs={{0,1},{1,0},{2,3},{3,2},{4,5},{5,4},{6,7},{7,6},{8,9},{9,8},{10,11... | collective-permute-start | bytes 491528 | tf_op jit(solution)/shard_map/ppermute | solution.py:483
  16.4 1.5 %shard_map.97.front_ref = bf16[64,128,128]{2,1,0:T(8,128)(2,1)S(1)} custom-call(bf16[128,128,128]{2,1,0:T(8,128)(2,1)} %bitcast.34, bf16[5,128,128]{2,1,0:T(8,128)(2,1)S(1)} %shard_map.96.refs_0_.mine_ref), custom_call_target="tpu_custom_call" | custom-call | bytes 4194304 | tf_op jit(solution)/shard_map/pallas_call | solution.py:404
  17.9 0.0 collective-permute-done.4.other_ref
  17.9 0.0 copy-start.1
  18.0 3.0 %shard_map.98 = (f32[72,128]{1,0:T(8,128)S(1)}, f32[72,128]{1,0:T(8,128)S(1)}, f32[72,128]{1,0:T(8,128)S(1)}, f32[72,128]{1,0:T(8,128)S(1)}) custom-call(s32[128,1]{1,0:T(8,128)S(1)} %fusion.5.refs_2_.source_ref, s32[1,128]{1,0:T(1,128)S(1)} %get-tuple-element.59.refs_3_.target_ref, s32[1]{0:T(128)} %bitcast.3.quarter_ref, ...), custom_call_target="tpu_custom_call" | custom-call | tf_op jit(solution)/shard_map/pallas_call | solution.py:404
  21.0 0.1 collective-permute-start.5
  21.0 1.4 %collective-permute-start.6 = (f32[72,128]{1,0:T(8,128)S(1)}, f32[72,128]{1,0:T(8,128)S(1)}, u32[]{:S(2)}, u32[]{:S(2)}) collective-permute-start(f32[72,128]{1,0:T(8,128)S(1)} %get-tuple-element.35), channel_id=1, source_target_pairs={{0,2},{1,3},{2,0},{3,1},{4,6},{5,7},{6,4},{7,5},{8,10},{9,11},{10,... | collective-permute-start | bytes 110600 | tf_op jit(solution)/shard_map/ppermute | solution.py:483
  22.5 0.4 collective-permute-start.7
  23.5 0.0 collective-permute-done.5.refs_1_
  23.6 1.5 %collective-permute-done.6.refs_2_ = f32[72,128]{1,0:T(8,128)S(1)} collective-permute-done((f32[72,128]{1,0:T(8,128)S(1)}, f32[72,128]{1,0:T(8,128)S(1)}, u32[]{:S(2)}, u32[]{:S(2)}) %collective-permute-start.6) | collective-permute-done | bytes 36896 | tf_op jit(solution)/shard_map/ppermute | solution.py:483
  25.1 0.9 %collective-permute-done.7.refs_3_ = f32[72,128]{1,0:T(8,128)S(1)} collective-permute-done((f32[72,128]{1,0:T(8,128)S(1)}, f32[72,128]{1,0:T(8,128)S(1)}, u32[]{:S(2)}, u32[]{:S(2)}) %collective-permute-start.7) | collective-permute-done | bytes 36896 | tf_op jit(solution)/shard_map/ppermute | solution.py:483
  25.9 0.3 shard_map.99
  26.3 11.5 %all_to_all.10.refs_0_ = f32[32,8,128]{2,1,0:T(8,128)S(1)} all-to-all(f32[32,8,128]{2,1,0:T(8,128)S(1)} %get-tuple-element.38), channel_id=1, replica_groups=mesh['rows'=8,'sub'=4] {'rows','sub'}, dimensions={0} | all-to-all | bytes 262144 | tf_op jit(solution)/shard_map/all_to_all | solution.py:555
  37.7 1.2 %shard_map.100 = (f32[64,128]{1,0:T(8,128)S(1)}, f32[64,128]{1,0:T(8,128)S(1)}, bf16[128,128]{1,0:T(8,128)(2,1)S(1)}, f32[64,128]{1,0:T(8,128)S(1)}, f32[64,128]...) custom-call(f32[1]{0:T(128)} %bitcast.23.shift_ref, ...), custom_call_target="tpu_custom_call" | custom-call | tf_op jit(solution)/shard_map/pallas_call | solution.py:404
  38.9 0.3 collective-permute-start.8
  39.2 1.0 %collective-permute-done.8 = bf16[128,128]{1,0:T(8,128)(2,1)S(1)} collective-permute-done((bf16[128,128]{1,0:T(8,128)(2,1)S(1)}, bf16[128,128]{1,0:T(8,128)(2,1)S(1)}, u32[]{:S(2)}, u32[]{:S(2)}) %collective-permute-start.8) | collective-permute-done | bytes 32800 | tf_op jit(solution)/shard_map/ppermute | solution.py:483
  40.2 0.9 %collective-permute-start.11 = (bf16[2,128,128]{2,1,0:T(8,128)(2,1)S(1)}, bf16[2,128,128]{2,1,0:T(8,128)(2,1)S(1)}, u32[]{:S(2)}, u32[]{:S(2)}) collective-permute-start(bf16[2,128,128]{2,1,0:T(8,128)(2,1)S(1)} %pad_maximum_fusion.1.refs_0_.pair_ref), channel_id=1, source_target_pairs={{0,6},{1,31},{2,4},{3,29},{4,2},{5,11},{6,0},{7,9},{8,14},{9,7},{1... | collective-permute-start | bytes 196616 | tf_op jit(solution)/shard_map/ppermute | solution.py:483
  41.1 0.9 %collective-permute-start.10 = (bf16[2,128,128]{2,1,0:T(8,128)(2,1)S(1)}, bf16[2,128,128]{2,1,0:T(8,128)(2,1)S(1)}, u32[]{:S(2)}, u32[]{:S(2)}) collective-permute-start(bf16[2,128,128]{2,1,0:T(8,128)(2,1)S(1)} %pad_maximum_fusion.1.refs_0_.pair_ref), channel_id=1, source_target_pairs={{0,4},{1,29},{2,6},{3,31},{4,0},{5,9},{6,2},{7,11},{8,12},{9,5},{1... | collective-permute-start | bytes 196616 | tf_op jit(solution)/shard_map/ppermute | solution.py:483
  42.1 1.7 %collective-permute-start.9 = (bf16[1,128,128]{2,1,0:T(8,128)(2,1)S(1)}, bf16[1,128,128]{2,1,0:T(8,128)(2,1)S(1)}, u32[]{:S(2)}, u32[]{:S(2)}) collective-permute-start(bf16[1,128,128]{2,1,0:T(8,128)(2,1)S(1)} %bitcast.33), channel_id=1, source_target_pairs={{0,2},{1,3},{2,0},{3,1},{4,6},{5,7},{6,4},{7,5},{8,10},{9,11},{10,... | collective-permute-start | bytes 98312 | tf_op jit(solution)/shard_map/ppermute | solution.py:483
  43.8 2.2 %shard_map.101.refs_3_.stiffness_ref = bf16[128,128,128]{2,1,0:T(8,128)(2,1)S(1)} custom-call(bf16[128,128,128]{2,1,0:T(8,128)(2,1)} %bitcast.39, bf16[2,128,128]{2,1,0:T(8,128)(2,1)S(1)} %pad_maximum_fusion.1.refs_0_.pair_ref), custom_call_target="tpu_custom_call" | custom-call | bytes 8388608 | tf_op jit(solution)/shard_map/pallas_call | solution.py:404
  46.0 0.0 collective-permute-done.9.refs_0_
  46.0 0.0 collective-permute-done.11.refs_2_
  46.0 0.1 collective-permute-done.10.refs_1_
  46.1 2.0 %collective-permute-start.12 = (bf16[5,128,128]{2,1,0:T(8,128)(2,1)S(1)}, bf16[5,128,128]{2,1,0:T(8,128)(2,1)S(1)}, u32[]{:S(2)}, u32[]{:S(2)}) collective-permute-start(bf16[5,128,128]{2,1,0:T(8,128)(2,1)S(1)} %shard_map.102.refs_0_.mine_ref), channel_id=1, source_target_pairs={{0,1},{1,0},{2,3},{3,2},{4,5},{5,4},{6,7},{7,6},{8,9},{9,8},{10,11... | collective-permute-start | bytes 491528 | tf_op jit(solution)/shard_map/ppermute | solution.py:483
  48.2 1.5 %shard_map.103.front_ref = bf16[64,128,128]{2,1,0:T(8,128)(2,1)S(1)} custom-call(bf16[128,128,128]{2,1,0:T(8,128)(2,1)} %bitcast.36, bf16[5,128,128]{2,1,0:T(8,128)(2,1)S(1)} %shard_map.102.refs_0_.mine_ref), custom_call_target="tpu_custom_call" | custom-call | bytes 4194304 | tf_op jit(solution)/shard_map/pallas_call | solution.py:404
  49.7 3.0 %shard_map.104 = (f32[64,128]{1,0:T(8,128)S(1)}, f32[64,128]{1,0:T(8,128)S(1)}, f32[64,128]{1,0:T(8,128)S(1)}, f32[64,128]{1,0:T(8,128)S(1)}) custom-call(s32[128,1]{1,0:T(8,128)S(1)} %fusion.5.refs_2_.source_ref, s32[1,128]{1,0:T(1,128)S(1)} %get-tuple-element.59.refs_3_.target_ref, s32[1]{0:T(128)} %bitcast.3.quarter_ref, ...), custom_call_target="tpu_custom_call" | custom-call | tf_op jit(solution)/shard_map/pallas_call | solution.py:404
  52.8 0.1 collective-permute-start.13
  52.8 0.9 %collective-permute-start.14 = (f32[64,128]{1,0:T(8,128)S(1)}, f32[64,128]{1,0:T(8,128)S(1)}, u32[]{:S(2)}, u32[]{:S(2)}) collective-permute-start(f32[64,128]{1,0:T(8,128)S(1)} %get-tuple-element.43), channel_id=1, source_target_pairs={{0,2},{1,3},{2,0},{3,1},{4,6},{5,7},{6,4},{7,5},{8,10},{9,11},{10,... | collective-permute-start | bytes 98312 | tf_op jit(solution)/shard_map/ppermute | solution.py:483
  53.7 1.0 %collective-permute-start.15 = (f32[64,128]{1,0:T(8,128)S(1)}, f32[64,128]{1,0:T(8,128)S(1)}, u32[]{:S(2)}, u32[]{:S(2)}) collective-permute-start(f32[64,128]{1,0:T(8,128)S(1)} %get-tuple-element.44), channel_id=1, source_target_pairs={{0,3},{1,2},{2,1},{3,0},{4,7},{5,6},{6,5},{7,4},{8,11},{9,10},{10,... | collective-permute-start | bytes 98312 | tf_op jit(solution)/shard_map/ppermute | solution.py:483
  54.7 2.3 %collective-permute-done.14.refs_2_ = f32[64,128]{1,0:T(8,128)S(1)} collective-permute-done((f32[64,128]{1,0:T(8,128)S(1)}, f32[64,128]{1,0:T(8,128)S(1)}, u32[]{:S(2)}, u32[]{:S(2)}) %collective-permute-start.14) | collective-permute-done | bytes 32800 | tf_op jit(solution)/shard_map/ppermute | solution.py:483
  56.9 0.4 collective-permute-done.15.refs_3_
  57.3 0.4 shard_map.105
  57.7 10.6 %all_to_all.11.refs_0_ = f32[32,1,128]{2,1,0:T(1,128)S(1)} all-to-all(f32[32,1,128]{2,1,0:T(1,128)S(1)} %get-tuple-element.47), channel_id=1, replica_groups=mesh['rows'=8,'sub'=4] {'rows','sub'}, dimensions={0} | all-to-all | bytes 32768 | tf_op jit(solution)/shard_map/all_to_all | solution.py:555
  68.3 1.3 %shard_map.106 = (f32[2,8192]{1,0:T(2,128)}, f32[59,2,60]{2,1,0:T(2,128)}, f32[2,59]{1,0:T(2,128)}) custom-call(f32[1]{0:T(128)} %bitcast.25.shift_ref, f32[32,1,128]{2,1,0:T(1,128)S(1)} %all_to_all.11.refs_0_, f32[64,128]{1,0:T(8,128)S(1)} %get-tuple-element.48.refs_1_, f32[58,8192]{1,0:T(8,128)S(1)} %get-tuple-element.32.refs_6_.refs_2_, ...), custom_call_target="tpu_custom_call" | custom-call | tf_op jit(solution)/shard_map/pallas_call | solution.py:404
  (13 shorter events, 0.1 us)
Async XLA Ops:
  0.6 4.8 %copy-start = (f32[2,58,57]{1,0,2:T(2,128)S(1)}, f32[2,58,57]{1,0,2:T(2,128)}, u32[]{:S(2)}) copy-start(f32[2,58,57]{1,0,2:T(2,128)} %param.13) | copy-start | bytes 79348
  0.6 4.9 %copy-start.2 = (s32[1,1,2,128]{3,2,1,0:T(2,128)S(1)}, s32[1,1,2,128]{3,2,1,0:T(2,128)}, u32[]{:S(2)}) copy-start(s32[1,1,2,128]{3,2,1,0:T(2,128)} %param.9) | copy-start | bytes 3076
  2.3 3.6 %collective-permute-start = (bf16[128,128]{1,0:T(8,128)(2,1)S(1)}, bf16[128,128]{1,0:T(8,128)(2,1)S(1)}, u32[]{:S(2)}, u32[]{:S(2)}) collective-permute-start(bf16[128,128]{1,0:T(8,128)(2,1)S(1)} %get-tuple-element.30), channel_id=1, source_target_pairs={{0,1},{1,0},{2,3},{3,2},{4,5},{5,4},{6,7},{7,6},{8,9},{9,8},{10,11... | collective-permute-start | bytes 98312 | tf_op jit(solution)/shard_map/ppermute | solution.py:483
  2.9 9.2 %collective-permute-start.1 = (bf16[1,128,128]{2,1,0:T(8,128)(2,1)S(1)}, bf16[1,128,128]{2,1,0:T(8,128)(2,1)S(1)}, u32[]{:S(2)}, u32[]{:S(2)}) collective-permute-start(bf16[1,128,128]{2,1,0:T(8,128)(2,1)S(1)} %bitcast.30), channel_id=1, source_target_pairs={{0,2},{1,3},{2,0},{3,1},{4,6},{5,7},{6,4},{7,5},{8,10},{9,11},{10,... | collective-permute-start | bytes 98312 | tf_op jit(solution)/shard_map/ppermute | solution.py:483
  5.9 6.2 %collective-permute-start.3 = (bf16[2,128,128]{2,1,0:T(8,128)(2,1)S(1)}, bf16[2,128,128]{2,1,0:T(8,128)(2,1)S(1)}, u32[]{:S(2)}, u32[]{:S(2)}) collective-permute-start(bf16[2,128,128]{2,1,0:T(8,128)(2,1)S(1)} %pad_maximum_fusion.refs_0_.pair_ref), channel_id=1, source_target_pairs={{0,6},{1,31},{2,4},{3,29},{4,2},{5,11},{6,0},{7,9},{8,14},{9,7},{1... | collective-permute-start | bytes 196616 | tf_op jit(solution)/shard_map/ppermute | solution.py:483
  7.6 4.5 %collective-permute-start.2 = (bf16[2,128,128]{2,1,0:T(8,128)(2,1)S(1)}, bf16[2,128,128]{2,1,0:T(8,128)(2,1)S(1)}, u32[]{:S(2)}, u32[]{:S(2)}) collective-permute-start(bf16[2,128,128]{2,1,0:T(8,128)(2,1)S(1)} %pad_maximum_fusion.refs_0_.pair_ref), channel_id=1, source_target_pairs={{0,4},{1,29},{2,6},{3,31},{4,0},{5,9},{6,2},{7,11},{8,12},{9,5},{1... | collective-permute-start | bytes 196616 | tf_op jit(solution)/shard_map/ppermute | solution.py:483
  12.2 5.8 %collective-permute-start.4 = (bf16[5,128,128]{2,1,0:T(8,128)(2,1)S(1)}, bf16[5,128,128]{2,1,0:T(8,128)(2,1)S(1)}, u32[]{:S(2)}, u32[]{:S(2)}) collective-permute-start(bf16[5,128,128]{2,1,0:T(8,128)(2,1)S(1)} %shard_map.96.refs_0_.mine_ref), channel_id=1, source_target_pairs={{0,1},{1,0},{2,3},{3,2},{4,5},{5,4},{6,7},{7,6},{8,9},{9,8},{10,11... | collective-permute-start | bytes 491528 | tf_op jit(solution)/shard_map/ppermute | solution.py:483
  17.9 8.0 %copy-start.1 = (f32[8192]{0:T(1024)S(1)}, f32[8192]{0:T(1024)}, u32[]{:S(2)}) copy-start(f32[8192]{0:T(1024)} %param.10) | copy-start | bytes 98308
  21.0 2.6 %collective-permute-start.5 = (f32[72,128]{1,0:T(8,128)S(1)}, f32[72,128]{1,0:T(8,128)S(1)}, u32[]{:S(2)}, u32[]{:S(2)}) collective-permute-start(f32[72,128]{1,0:T(8,128)S(1)} %get-tuple-element.34), channel_id=1, source_target_pairs={{0,1},{1,0},{2,3},{3,2},{4,5},{5,4},{6,7},{7,6},{8,9},{9,8},{10,11... | collective-permute-start | bytes 110600 | tf_op jit(solution)/shard_map/ppermute | solution.py:483
  21.0 4.0 %collective-permute-start.6 = (f32[72,128]{1,0:T(8,128)S(1)}, f32[72,128]{1,0:T(8,128)S(1)}, u32[]{:S(2)}, u32[]{:S(2)}) collective-permute-start(f32[72,128]{1,0:T(8,128)S(1)} %get-tuple-element.35), channel_id=1, source_target_pairs={{0,2},{1,3},{2,0},{3,1},{4,6},{5,7},{6,4},{7,5},{8,10},{9,11},{10,... | collective-permute-start | bytes 110600 | tf_op jit(solution)/shard_map/ppermute | solution.py:483
  22.5 3.4 %collective-permute-start.7 = (f32[72,128]{1,0:T(8,128)S(1)}, f32[72,128]{1,0:T(8,128)S(1)}, u32[]{:S(2)}, u32[]{:S(2)}) collective-permute-start(f32[72,128]{1,0:T(8,128)S(1)} %get-tuple-element.36), channel_id=1, source_target_pairs={{0,3},{1,2},{2,1},{3,0},{4,7},{5,6},{6,5},{7,4},{8,11},{9,10},{10,... | collective-permute-start | bytes 110600 | tf_op jit(solution)/shard_map/ppermute | solution.py:483
  38.9 1.3 %collective-permute-start.8 = (bf16[128,128]{1,0:T(8,128)(2,1)S(1)}, bf16[128,128]{1,0:T(8,128)(2,1)S(1)}, u32[]{:S(2)}, u32[]{:S(2)}) collective-permute-start(bf16[128,128]{1,0:T(8,128)(2,1)S(1)} %get-tuple-element.40), channel_id=1, source_target_pairs={{0,1},{1,0},{2,3},{3,2},{4,5},{5,4},{6,7},{7,6},{8,9},{9,8},{10,11... | collective-permute-start | bytes 98312 | tf_op jit(solution)/shard_map/ppermute | solution.py:483
  40.2 5.8 %collective-permute-start.11 = (bf16[2,128,128]{2,1,0:T(8,128)(2,1)S(1)}, bf16[2,128,128]{2,1,0:T(8,128)(2,1)S(1)}, u32[]{:S(2)}, u32[]{:S(2)}) collective-permute-start(bf16[2,128,128]{2,1,0:T(8,128)(2,1)S(1)} %pad_maximum_fusion.1.refs_0_.pair_ref), channel_id=1, source_target_pairs={{0,6},{1,31},{2,4},{3,29},{4,2},{5,11},{6,0},{7,9},{8,14},{9,7},{1... | collective-permute-start | bytes 196616 | tf_op jit(solution)/shard_map/ppermute | solution.py:483
  41.1 5.0 %collective-permute-start.10 = (bf16[2,128,128]{2,1,0:T(8,128)(2,1)S(1)}, bf16[2,128,128]{2,1,0:T(8,128)(2,1)S(1)}, u32[]{:S(2)}, u32[]{:S(2)}) collective-permute-start(bf16[2,128,128]{2,1,0:T(8,128)(2,1)S(1)} %pad_maximum_fusion.1.refs_0_.pair_ref), channel_id=1, source_target_pairs={{0,4},{1,29},{2,6},{3,31},{4,0},{5,9},{6,2},{7,11},{8,12},{9,5},{1... | collective-permute-start | bytes 196616 | tf_op jit(solution)/shard_map/ppermute | solution.py:483
  42.1 3.9 %collective-permute-start.9 = (bf16[1,128,128]{2,1,0:T(8,128)(2,1)S(1)}, bf16[1,128,128]{2,1,0:T(8,128)(2,1)S(1)}, u32[]{:S(2)}, u32[]{:S(2)}) collective-permute-start(bf16[1,128,128]{2,1,0:T(8,128)(2,1)S(1)} %bitcast.33), channel_id=1, source_target_pairs={{0,2},{1,3},{2,0},{3,1},{4,6},{5,7},{6,4},{7,5},{8,10},{9,11},{10,... | collective-permute-start | bytes 98312 | tf_op jit(solution)/shard_map/ppermute | solution.py:483
  46.1 3.6 %collective-permute-start.12 = (bf16[5,128,128]{2,1,0:T(8,128)(2,1)S(1)}, bf16[5,128,128]{2,1,0:T(8,128)(2,1)S(1)}, u32[]{:S(2)}, u32[]{:S(2)}) collective-permute-start(bf16[5,128,128]{2,1,0:T(8,128)(2,1)S(1)} %shard_map.102.refs_0_.mine_ref), channel_id=1, source_target_pairs={{0,1},{1,0},{2,3},{3,2},{4,5},{5,4},{6,7},{7,6},{8,9},{9,8},{10,11... | collective-permute-start | bytes 491528 | tf_op jit(solution)/shard_map/ppermute | solution.py:483
  52.8 1.9 %collective-permute-start.13 = (f32[64,128]{1,0:T(8,128)S(1)}, f32[64,128]{1,0:T(8,128)S(1)}, u32[]{:S(2)}, u32[]{:S(2)}) collective-permute-start(f32[64,128]{1,0:T(8,128)S(1)} %get-tuple-element.42), channel_id=1, source_target_pairs={{0,1},{1,0},{2,3},{3,2},{4,5},{5,4},{6,7},{7,6},{8,9},{9,8},{10,11... | collective-permute-start | bytes 98312 | tf_op jit(solution)/shard_map/ppermute | solution.py:483
  52.8 4.1 %collective-permute-start.14 = (f32[64,128]{1,0:T(8,128)S(1)}, f32[64,128]{1,0:T(8,128)S(1)}, u32[]{:S(2)}, u32[]{:S(2)}) collective-permute-start(f32[64,128]{1,0:T(8,128)S(1)} %get-tuple-element.43), channel_id=1, source_target_pairs={{0,2},{1,3},{2,0},{3,1},{4,6},{5,7},{6,4},{7,5},{8,10},{9,11},{10,... | collective-permute-start | bytes 98312 | tf_op jit(solution)/shard_map/ppermute | solution.py:483
  53.7 3.6 %collective-permute-start.15 = (f32[64,128]{1,0:T(8,128)S(1)}, f32[64,128]{1,0:T(8,128)S(1)}, u32[]{:S(2)}, u32[]{:S(2)}) collective-permute-start(f32[64,128]{1,0:T(8,128)S(1)} %get-tuple-element.44), channel_id=1, source_target_pairs={{0,3},{1,2},{2,1},{3,0},{4,7},{5,6},{6,5},{7,4},{8,11},{9,10},{10,... | collective-permute-start | bytes 98312 | tf_op jit(solution)/shard_map/ppermute | solution.py:483

commit v4 on v3

--- a/solution.py
+++ b/solution.py
@@ -482,8 +482,11 @@
                 pairs.append((r * sub_count + s, to_r * sub_count + to_s))
         return lax.ppermute(value, every, pairs)
 
-    def beside(r, s):
-        return r ^ 1 if s % 2 == 0 else (((r + 1) ^ 1) - 1) % rows_count
+    def beside(r, s, k):
+        other = r ^ 1 if s % 2 == 0 else ((r + 1) ^ 1) - 1
+        if 0 <= other < rows_count:
+            return other, s ^ (2 * k)
+        return r, s ^ 2 if sub_count > 2 else s
 
     damping = damping_tiles[0, 0]
     stiffness = stiffness_tiles[0, 0]
@@ -514,7 +517,7 @@
         pair = jnp.stack([vectors, swap(vectors, lambda r, s: (r, s ^ 1))])
         mine = [
             swap(vectors[None], lambda r, s, k=k: (r, s ^ (2 * k))) for k in range(1, half)
-        ] + [swap(pair, lambda r, s, k=k: (beside(r, s), s ^ (2 * k))) for k in range(half)]
+        ] + [swap(pair, lambda r, s, k=k: beside(r, s, k)) for k in range(half)]
         before = [pair]
         if packed:
             _, late = lax.optimization_barrier((pair, basis))

time: 69.9 us -> 66.9 us (0.957)
  starting transfers between devices: 19.2 us -> 13.3 us
  waiting for transfers between devices: 6.15 us -> 7.97 us
  blocking collectives: 22 us -> 23.1 us
    ppermute x16, starting transfers between devices: 19.2 us -> 13.3 us  [swap(): return lax.ppermute(value, every, pairs)]
    ppermute x16, waiting for transfers between devices: 6.15 us -> 7.97 us  [swap(): return lax.ppermute(value, every, pairs)]
    all_to_all x2, blocking collectives: 22 us -> 23.1 us  [on_device(): received = lax.all_to_all(sent, every, 0, 0)]
where the time goes in v4:
time: 66.9 us; the launch traced here: 66.6 us
  blocking collectives  23.1 us (35%)
  Pallas kernels  18.5 us (28%)
  starting transfers between devices  13.3 us (20%)
  waiting for transfers between devices  7.97 us (12%)
  matrix products  1.77 us (3%)
  between operations  1.53 us (2%)
    all_to_all x2, blocking collectives, on_device(): received = lax.all_to_all(sent, every, 0, 0)  23.1 us
    pallas_call x13, Pallas kernels, call(): pl.pallas_call(body, out_shape=[jax.ShapeDtypeStruct(shape, dtype) if fin...  18.5 us
    ppermute x16, starting transfers between devices, swap(): return lax.ppermute(value, every, pairs)  13.3 us
    ppermute x16, waiting for transfers between devices, swap(): return lax.ppermute(value, every, pairs)  7.97 us
    dot_general x1, matrix products, on_device(): gram = jnp.dot(late, late.T, precision=lax.Precision.HIGHEST)  1.77 us
  transfers between devices with their start and end apart: 16, of which 6 were waited for; matrix products, arithmetic and copies ran while one was open for 3% of the time, Pallas kernels for 11%

profile of v4, /device:TPU:0, one launch (start us, length us, event | category | flops | bytes accessed | tf_op | source)
XLA Modules:
  0.0 66.6 jit_solution(6283474612444905039)
XLA Ops:
  0.7 1.7 %shard_map.94 = (f32[64,128]{1,0:T(8,128)S(1)}, bf16[128,128]{1,0:T(8,128)(2,1)S(1)}, f32[58,8192]{1,0:T(8,128)S(1)}) custom-call(f32[57,2,58]{2,1,0:T(2,128)} %bitcast.26, f32[58,8192]{1,0:T(8,128)} %basis_ref.1), custom_call_target="tpu_custom_call" | custom-call | tf_op jit(solution)/shard_map/pallas_call | solution.py:404
  2.3 0.6 collective-permute-start
  2.9 2.6 %collective-permute-start.1 = (bf16[1,128,128]{2,1,0:T(8,128)(2,1)S(1)}, bf16[1,128,128]{2,1,0:T(8,128)(2,1)S(1)}, u32[]{:S(2)}, u32[]{:S(2)}) collective-permute-start(bf16[1,128,128]{2,1,0:T(8,128)(2,1)S(1)} %bitcast.30), channel_id=1, source_target_pairs={{0,2},{1,3},{2,0},{3,1},{4,6},{5,7},{6,4},{7,5},{8,10},{9,11},{10,... | collective-permute-start | bytes 98312 | tf_op jit(solution)/shard_map/ppermute | solution.py:483
  5.4 0.1 copy.14
  5.6 0.1 copy.10
  5.7 0.2 fusion.5.refs_2_.source_ref
  5.9 0.0 collective-permute-done
  5.9 1.7 %collective-permute-start.3 = (bf16[2,128,128]{2,1,0:T(8,128)(2,1)S(1)}, bf16[2,128,128]{2,1,0:T(8,128)(2,1)S(1)}, u32[]{:S(2)}, u32[]{:S(2)}) collective-permute-start(bf16[2,128,128]{2,1,0:T(8,128)(2,1)S(1)} %pad_maximum_fusion.refs_0_.pair_ref), channel_id=1, source_target_pairs={{0,6},{1,3},{2,4},{3,1},{4,2},{5,11},{6,0},{7,9},{8,14},{9,7},{10,... | collective-permute-start | bytes 196616 | tf_op jit(solution)/shard_map/ppermute | solution.py:483
  7.6 0.5 collective-permute-start.2
  8.1 1.8 %fusion.12.refs_1_.rest_0_ = f32[58,58]{1,0:T(8,128)S(1)} fusion(f32[58,8192]{1,0:T(8,128)S(1)} %get-tuple-element.32.refs_6_.refs_2_), kind=kOutput, calls=%fused_computation.32 | convolution fusion | flops 330694656 | bytes 1914000 | tf_op jit(solution)/shard_map/dot_general | solution.py:524
  9.9 2.2 %shard_map.95.refs_3_.stiffness_ref = bf16[128,128,128]{2,1,0:T(8,128)(2,1)S(1)} custom-call(bf16[128,128,128]{2,1,0:T(8,128)(2,1)} %bitcast.38, bf16[2,128,128]{2,1,0:T(8,128)(2,1)S(1)} %pad_maximum_fusion.refs_0_.pair_ref, f32[58,58]{1,0:T(8,128)S(1)} %fusion.12.refs_1_.rest_0_, s32[128,1]{1,0:T(8,128)S(1)} %fusion.5.refs_2_.source_ref, ...), custom_call_target="tpu_custom_call" | custom-call | bytes 8388608 | tf_op jit(solution)/shard_map/pallas_call | solution.py:404
  12.1 0.0 collective-permute-done.1.refs_0_
  12.1 0.0 collective-permute-done.3.refs_2_
  12.1 0.0 collective-permute-done.2.refs_1_
  12.2 0.1 collective-permute-start.4
  12.3 1.6 %shard_map.97.front_ref = bf16[64,128,128]{2,1,0:T(8,128)(2,1)S(1)} custom-call(bf16[128,128,128]{2,1,0:T(8,128)(2,1)} %bitcast.34, bf16[5,128,128]{2,1,0:T(8,128)(2,1)S(1)} %shard_map.96.refs_0_.mine_ref), custom_call_target="tpu_custom_call" | custom-call | bytes 4194304 | tf_op jit(solution)/shard_map/pallas_call | solution.py:404
  13.8 0.0 collective-permute-done.4.other_ref
  13.8 0.0 copy-start.1
  13.8 3.0 %shard_map.98 = (f32[72,128]{1,0:T(8,128)S(1)}, f32[72,128]{1,0:T(8,128)S(1)}, f32[72,128]{1,0:T(8,128)S(1)}, f32[72,128]{1,0:T(8,128)S(1)}) custom-call(s32[128,1]{1,0:T(8,128)S(1)} %fusion.5.refs_2_.source_ref, s32[1,128]{1,0:T(1,128)S(1)} %get-tuple-element.59.refs_3_.target_ref, s32[1]{0:T(128)} %bitcast.3.quarter_ref, ...), custom_call_target="tpu_custom_call" | custom-call | tf_op jit(solution)/shard_map/pallas_call | solution.py:404
  16.8 0.6 collective-permute-start.5
  17.4 1.4 %collective-permute-start.6 = (f32[72,128]{1,0:T(8,128)S(1)}, f32[72,128]{1,0:T(8,128)S(1)}, u32[]{:S(2)}, u32[]{:S(2)}) collective-permute-start(f32[72,128]{1,0:T(8,128)S(1)} %get-tuple-element.35), channel_id=1, source_target_pairs={{0,2},{1,3},{2,0},{3,1},{4,6},{5,7},{6,4},{7,5},{8,10},{9,11},{10,... | collective-permute-start | bytes 110600 | tf_op jit(solution)/shard_map/ppermute | solution.py:483
  18.8 0.1 collective-permute-start.7
  19.5 0.0 collective-permute-done.5.refs_1_
  19.5 1.9 %collective-permute-done.6.refs_2_ = f32[72,128]{1,0:T(8,128)S(1)} collective-permute-done((f32[72,128]{1,0:T(8,128)S(1)}, f32[72,128]{1,0:T(8,128)S(1)}, u32[]{:S(2)}, u32[]{:S(2)}) %collective-permute-start.6) | collective-permute-done | bytes 36896 | tf_op jit(solution)/shard_map/ppermute | solution.py:483
  21.4 1.2 %collective-permute-done.7.refs_3_ = f32[72,128]{1,0:T(8,128)S(1)} collective-permute-done((f32[72,128]{1,0:T(8,128)S(1)}, f32[72,128]{1,0:T(8,128)S(1)}, u32[]{:S(2)}, u32[]{:S(2)}) %collective-permute-start.7) | collective-permute-done | bytes 36896 | tf_op jit(solution)/shard_map/ppermute | solution.py:483
  22.5 0.3 shard_map.99
  22.8 13.3 %all_to_all.10.refs_0_ = f32[32,8,128]{2,1,0:T(8,128)S(1)} all-to-all(f32[32,8,128]{2,1,0:T(8,128)S(1)} %get-tuple-element.38), channel_id=1, replica_groups=mesh['rows'=8,'sub'=4] {'rows','sub'}, dimensions={0} | all-to-all | bytes 262144 | tf_op jit(solution)/shard_map/all_to_all | solution.py:558
  36.1 1.2 %shard_map.100 = (f32[64,128]{1,0:T(8,128)S(1)}, f32[64,128]{1,0:T(8,128)S(1)}, bf16[128,128]{1,0:T(8,128)(2,1)S(1)}, f32[64,128]{1,0:T(8,128)S(1)}, f32[64,128]...) custom-call(f32[1]{0:T(128)} %bitcast.23.shift_ref, ...), custom_call_target="tpu_custom_call" | custom-call | tf_op jit(solution)/shard_map/pallas_call | solution.py:404
  37.3 0.3 collective-permute-start.8
  37.6 1.0 %collective-permute-done.8 = bf16[128,128]{1,0:T(8,128)(2,1)S(1)} collective-permute-done((bf16[128,128]{1,0:T(8,128)(2,1)S(1)}, bf16[128,128]{1,0:T(8,128)(2,1)S(1)}, u32[]{:S(2)}, u32[]{:S(2)}) %collective-permute-start.8) | collective-permute-done | bytes 32800 | tf_op jit(solution)/shard_map/ppermute | solution.py:483
  38.6 0.9 %collective-permute-start.11 = (bf16[2,128,128]{2,1,0:T(8,128)(2,1)S(1)}, bf16[2,128,128]{2,1,0:T(8,128)(2,1)S(1)}, u32[]{:S(2)}, u32[]{:S(2)}) collective-permute-start(bf16[2,128,128]{2,1,0:T(8,128)(2,1)S(1)} %pad_maximum_fusion.1.refs_0_.pair_ref), channel_id=1, source_target_pairs={{0,6},{1,3},{2,4},{3,1},{4,2},{5,11},{6,0},{7,9},{8,14},{9,7},{10,... | collective-permute-start | bytes 196616 | tf_op jit(solution)/shard_map/ppermute | solution.py:483
  39.5 0.9 %collective-permute-start.10 = (bf16[2,128,128]{2,1,0:T(8,128)(2,1)S(1)}, bf16[2,128,128]{2,1,0:T(8,128)(2,1)S(1)}, u32[]{:S(2)}, u32[]{:S(2)}) collective-permute-start(bf16[2,128,128]{2,1,0:T(8,128)(2,1)S(1)} %pad_maximum_fusion.1.refs_0_.pair_ref), channel_id=1, source_target_pairs={{0,4},{1,3},{2,6},{3,1},{4,0},{5,9},{6,2},{7,11},{8,12},{9,5},{10,... | collective-permute-start | bytes 196616 | tf_op jit(solution)/shard_map/ppermute | solution.py:483
  40.5 1.7 %collective-permute-start.9 = (bf16[1,128,128]{2,1,0:T(8,128)(2,1)S(1)}, bf16[1,128,128]{2,1,0:T(8,128)(2,1)S(1)}, u32[]{:S(2)}, u32[]{:S(2)}) collective-permute-start(bf16[1,128,128]{2,1,0:T(8,128)(2,1)S(1)} %bitcast.33), channel_id=1, source_target_pairs={{0,2},{1,3},{2,0},{3,1},{4,6},{5,7},{6,4},{7,5},{8,10},{9,11},{10,... | collective-permute-start | bytes 98312 | tf_op jit(solution)/shard_map/ppermute | solution.py:483
  42.1 2.2 %shard_map.101.refs_3_.stiffness_ref = bf16[128,128,128]{2,1,0:T(8,128)(2,1)S(1)} custom-call(bf16[128,128,128]{2,1,0:T(8,128)(2,1)} %bitcast.39, bf16[2,128,128]{2,1,0:T(8,128)(2,1)S(1)} %pad_maximum_fusion.1.refs_0_.pair_ref), custom_call_target="tpu_custom_call" | custom-call | bytes 8388608 | tf_op jit(solution)/shard_map/pallas_call | solution.py:404
  44.4 0.6 collective-permute-done.9.refs_0_
  45.0 0.0 collective-permute-done.11.refs_2_
  45.0 0.1 collective-permute-start.12
  45.1 1.6 %shard_map.103.front_ref = bf16[64,128,128]{2,1,0:T(8,128)(2,1)S(1)} custom-call(bf16[128,128,128]{2,1,0:T(8,128)(2,1)} %bitcast.36, bf16[5,128,128]{2,1,0:T(8,128)(2,1)S(1)} %shard_map.102.refs_0_.mine_ref), custom_call_target="tpu_custom_call" | custom-call | bytes 4194304 | tf_op jit(solution)/shard_map/pallas_call | solution.py:404
  46.6 0.0 collective-permute-done.12.other_ref
  46.7 3.0 %shard_map.104 = (f32[64,128]{1,0:T(8,128)S(1)}, f32[64,128]{1,0:T(8,128)S(1)}, f32[64,128]{1,0:T(8,128)S(1)}, f32[64,128]{1,0:T(8,128)S(1)}) custom-call(s32[128,1]{1,0:T(8,128)S(1)} %fusion.5.refs_2_.source_ref, s32[1,128]{1,0:T(1,128)S(1)} %get-tuple-element.59.refs_3_.target_ref, s32[1]{0:T(128)} %bitcast.3.quarter_ref, ...), custom_call_target="tpu_custom_call" | custom-call | tf_op jit(solution)/shard_map/pallas_call | solution.py:404
  49.7 0.6 collective-permute-start.13
  50.2 1.1 %collective-permute-start.14 = (f32[64,128]{1,0:T(8,128)S(1)}, f32[64,128]{1,0:T(8,128)S(1)}, u32[]{:S(2)}, u32[]{:S(2)}) collective-permute-start(f32[64,128]{1,0:T(8,128)S(1)} %get-tuple-element.43), channel_id=1, source_target_pairs={{0,2},{1,3},{2,0},{3,1},{4,6},{5,7},{6,4},{7,5},{8,10},{9,11},{10,... | collective-permute-start | bytes 98312 | tf_op jit(solution)/shard_map/ppermute | solution.py:483
  51.3 0.3 collective-permute-start.15
  51.7 2.5 %collective-permute-done.14.refs_2_ = f32[64,128]{1,0:T(8,128)S(1)} collective-permute-done((f32[64,128]{1,0:T(8,128)S(1)}, f32[64,128]{1,0:T(8,128)S(1)}, u32[]{:S(2)}, u32[]{:S(2)}) %collective-permute-start.14) | collective-permute-done | bytes 32800 | tf_op jit(solution)/shard_map/ppermute | solution.py:483
  54.1 0.8 %collective-permute-done.15.refs_3_ = f32[64,128]{1,0:T(8,128)S(1)} collective-permute-done((f32[64,128]{1,0:T(8,128)S(1)}, f32[64,128]{1,0:T(8,128)S(1)}, u32[]{:S(2)}, u32[]{:S(2)}) %collective-permute-start.15) | collective-permute-done | bytes 32800 | tf_op jit(solution)/shard_map/ppermute | solution.py:483
  55.0 0.4 shard_map.105
  55.4 9.9 %all_to_all.11.refs_0_ = f32[32,1,128]{2,1,0:T(1,128)S(1)} all-to-all(f32[32,1,128]{2,1,0:T(1,128)S(1)} %get-tuple-element.47), channel_id=1, replica_groups=mesh['rows'=8,'sub'=4] {'rows','sub'}, dimensions={0} | all-to-all | bytes 32768 | tf_op jit(solution)/shard_map/all_to_all | solution.py:558
  65.2 1.3 %shard_map.106 = (f32[2,8192]{1,0:T(2,128)}, f32[59,2,60]{2,1,0:T(2,128)}, f32[2,59]{1,0:T(2,128)}) custom-call(f32[1]{0:T(128)} %bitcast.25.shift_ref, f32[32,1,128]{2,1,0:T(1,128)S(1)} %all_to_all.11.refs_0_, f32[64,128]{1,0:T(8,128)S(1)} %get-tuple-element.48.refs_1_, f32[58,8192]{1,0:T(8,128)S(1)} %get-tuple-element.32.refs_6_.refs_2_, ...), custom_call_target="tpu_custom_call" | custom-call | tf_op jit(solution)/shard_map/pallas_call | solution.py:404
  (13 shorter events, 0.1 us)
Async XLA Ops:
  0.6 4.8 %copy-start = (f32[2,58,57]{1,0,2:T(2,128)S(1)}, f32[2,58,57]{1,0,2:T(2,128)}, u32[]{:S(2)}) copy-start(f32[2,58,57]{1,0,2:T(2,128)} %param.13) | copy-start | bytes 79348
  0.6 4.9 %copy-start.2 = (s32[1,1,2,128]{3,2,1,0:T(2,128)S(1)}, s32[1,1,2,128]{3,2,1,0:T(2,128)}, u32[]{:S(2)}) copy-start(s32[1,1,2,128]{3,2,1,0:T(2,128)} %param.9) | copy-start | bytes 3076
  2.3 3.6 %collective-permute-start = (bf16[128,128]{1,0:T(8,128)(2,1)S(1)}, bf16[128,128]{1,0:T(8,128)(2,1)S(1)}, u32[]{:S(2)}, u32[]{:S(2)}) collective-permute-start(bf16[128,128]{1,0:T(8,128)(2,1)S(1)} %get-tuple-element.30), channel_id=1, source_target_pairs={{0,1},{1,0},{2,3},{3,2},{4,5},{5,4},{6,7},{7,6},{8,9},{9,8},{10,11... | collective-permute-start | bytes 98312 | tf_op jit(solution)/shard_map/ppermute | solution.py:483
  2.9 9.2 %collective-permute-start.1 = (bf16[1,128,128]{2,1,0:T(8,128)(2,1)S(1)}, bf16[1,128,128]{2,1,0:T(8,128)(2,1)S(1)}, u32[]{:S(2)}, u32[]{:S(2)}) collective-permute-start(bf16[1,128,128]{2,1,0:T(8,128)(2,1)S(1)} %bitcast.30), channel_id=1, source_target_pairs={{0,2},{1,3},{2,0},{3,1},{4,6},{5,7},{6,4},{7,5},{8,10},{9,11},{10,... | collective-permute-start | bytes 98312 | tf_op jit(solution)/shard_map/ppermute | solution.py:483
  5.9 6.2 %collective-permute-start.3 = (bf16[2,128,128]{2,1,0:T(8,128)(2,1)S(1)}, bf16[2,128,128]{2,1,0:T(8,128)(2,1)S(1)}, u32[]{:S(2)}, u32[]{:S(2)}) collective-permute-start(bf16[2,128,128]{2,1,0:T(8,128)(2,1)S(1)} %pad_maximum_fusion.refs_0_.pair_ref), channel_id=1, source_target_pairs={{0,6},{1,3},{2,4},{3,1},{4,2},{5,11},{6,0},{7,9},{8,14},{9,7},{10,... | collective-permute-start | bytes 196616 | tf_op jit(solution)/shard_map/ppermute | solution.py:483
  7.6 4.5 %collective-permute-start.2 = (bf16[2,128,128]{2,1,0:T(8,128)(2,1)S(1)}, bf16[2,128,128]{2,1,0:T(8,128)(2,1)S(1)}, u32[]{:S(2)}, u32[]{:S(2)}) collective-permute-start(bf16[2,128,128]{2,1,0:T(8,128)(2,1)S(1)} %pad_maximum_fusion.refs_0_.pair_ref), channel_id=1, source_target_pairs={{0,4},{1,3},{2,6},{3,1},{4,0},{5,9},{6,2},{7,11},{8,12},{9,5},{10,... | collective-permute-start | bytes 196616 | tf_op jit(solution)/shard_map/ppermute | solution.py:483
  12.2 1.6 %collective-permute-start.4 = (bf16[5,128,128]{2,1,0:T(8,128)(2,1)S(1)}, bf16[5,128,128]{2,1,0:T(8,128)(2,1)S(1)}, u32[]{:S(2)}, u32[]{:S(2)}) collective-permute-start(bf16[5,128,128]{2,1,0:T(8,128)(2,1)S(1)} %shard_map.96.refs_0_.mine_ref), channel_id=1, source_target_pairs={{0,1},{1,0},{2,3},{3,2},{4,5},{5,4},{6,7},{7,6},{8,9},{9,8},{10,11... | collective-permute-start | bytes 491528 | tf_op jit(solution)/shard_map/ppermute | solution.py:483
  13.8 8.7 %copy-start.1 = (f32[8192]{0:T(1024)S(1)}, f32[8192]{0:T(1024)}, u32[]{:S(2)}) copy-start(f32[8192]{0:T(1024)} %param.10) | copy-start | bytes 98308
  16.8 2.6 %collective-permute-start.5 = (f32[72,128]{1,0:T(8,128)S(1)}, f32[72,128]{1,0:T(8,128)S(1)}, u32[]{:S(2)}, u32[]{:S(2)}) collective-permute-start(f32[72,128]{1,0:T(8,128)S(1)} %get-tuple-element.34), channel_id=1, source_target_pairs={{0,1},{1,0},{2,3},{3,2},{4,5},{5,4},{6,7},{7,6},{8,9},{9,8},{10,11... | collective-permute-start | bytes 110600 | tf_op jit(solution)/shard_map/ppermute | solution.py:483
  17.4 4.0 %collective-permute-start.6 = (f32[72,128]{1,0:T(8,128)S(1)}, f32[72,128]{1,0:T(8,128)S(1)}, u32[]{:S(2)}, u32[]{:S(2)}) collective-permute-start(f32[72,128]{1,0:T(8,128)S(1)} %get-tuple-element.35), channel_id=1, source_target_pairs={{0,2},{1,3},{2,0},{3,1},{4,6},{5,7},{6,4},{7,5},{8,10},{9,11},{10,... | collective-permute-start | bytes 110600 | tf_op jit(solution)/shard_map/ppermute | solution.py:483
  18.8 3.8 %collective-permute-start.7 = (f32[72,128]{1,0:T(8,128)S(1)}, f32[72,128]{1,0:T(8,128)S(1)}, u32[]{:S(2)}, u32[]{:S(2)}) collective-permute-start(f32[72,128]{1,0:T(8,128)S(1)} %get-tuple-element.36), channel_id=1, source_target_pairs={{0,3},{1,2},{2,1},{3,0},{4,7},{5,6},{6,5},{7,4},{8,11},{9,10},{10,... | collective-permute-start | bytes 110600 | tf_op jit(solution)/shard_map/ppermute | solution.py:483
  37.3 1.3 %collective-permute-start.8 = (bf16[128,128]{1,0:T(8,128)(2,1)S(1)}, bf16[128,128]{1,0:T(8,128)(2,1)S(1)}, u32[]{:S(2)}, u32[]{:S(2)}) collective-permute-start(bf16[128,128]{1,0:T(8,128)(2,1)S(1)} %get-tuple-element.40), channel_id=1, source_target_pairs={{0,1},{1,0},{2,3},{3,2},{4,5},{5,4},{6,7},{7,6},{8,9},{9,8},{10,11... | collective-permute-start | bytes 98312 | tf_op jit(solution)/shard_map/ppermute | solution.py:483
  38.6 6.4 %collective-permute-start.11 = (bf16[2,128,128]{2,1,0:T(8,128)(2,1)S(1)}, bf16[2,128,128]{2,1,0:T(8,128)(2,1)S(1)}, u32[]{:S(2)}, u32[]{:S(2)}) collective-permute-start(bf16[2,128,128]{2,1,0:T(8,128)(2,1)S(1)} %pad_maximum_fusion.1.refs_0_.pair_ref), channel_id=1, source_target_pairs={{0,6},{1,3},{2,4},{3,1},{4,2},{5,11},{6,0},{7,9},{8,14},{9,7},{10,... | collective-permute-start | bytes 196616 | tf_op jit(solution)/shard_map/ppermute | solution.py:483
  39.5 5.5 %collective-permute-start.10 = (bf16[2,128,128]{2,1,0:T(8,128)(2,1)S(1)}, bf16[2,128,128]{2,1,0:T(8,128)(2,1)S(1)}, u32[]{:S(2)}, u32[]{:S(2)}) collective-permute-start(bf16[2,128,128]{2,1,0:T(8,128)(2,1)S(1)} %pad_maximum_fusion.1.refs_0_.pair_ref), channel_id=1, source_target_pairs={{0,4},{1,3},{2,6},{3,1},{4,0},{5,9},{6,2},{7,11},{8,12},{9,5},{10,... | collective-permute-start | bytes 196616 | tf_op jit(solution)/shard_map/ppermute | solution.py:483
  40.5 4.5 %collective-permute-start.9 = (bf16[1,128,128]{2,1,0:T(8,128)(2,1)S(1)}, bf16[1,128,128]{2,1,0:T(8,128)(2,1)S(1)}, u32[]{:S(2)}, u32[]{:S(2)}) collective-permute-start(bf16[1,128,128]{2,1,0:T(8,128)(2,1)S(1)} %bitcast.33), channel_id=1, source_target_pairs={{0,2},{1,3},{2,0},{3,1},{4,6},{5,7},{6,4},{7,5},{8,10},{9,11},{10,... | collective-permute-start | bytes 98312 | tf_op jit(solution)/shard_map/ppermute | solution.py:483
  45.0 1.6 %collective-permute-start.12 = (bf16[5,128,128]{2,1,0:T(8,128)(2,1)S(1)}, bf16[5,128,128]{2,1,0:T(8,128)(2,1)S(1)}, u32[]{:S(2)}, u32[]{:S(2)}) collective-permute-start(bf16[5,128,128]{2,1,0:T(8,128)(2,1)S(1)} %shard_map.102.refs_0_.mine_ref), channel_id=1, source_target_pairs={{0,1},{1,0},{2,3},{3,2},{4,5},{5,4},{6,7},{7,6},{8,9},{9,8},{10,11... | collective-permute-start | bytes 491528 | tf_op jit(solution)/shard_map/ppermute | solution.py:483
  49.7 2.0 %collective-permute-start.13 = (f32[64,128]{1,0:T(8,128)S(1)}, f32[64,128]{1,0:T(8,128)S(1)}, u32[]{:S(2)}, u32[]{:S(2)}) collective-permute-start(f32[64,128]{1,0:T(8,128)S(1)} %get-tuple-element.42), channel_id=1, source_target_pairs={{0,1},{1,0},{2,3},{3,2},{4,5},{5,4},{6,7},{7,6},{8,9},{9,8},{10,11... | collective-permute-start | bytes 98312 | tf_op jit(solution)/shard_map/ppermute | solution.py:483
  50.2 3.9 %collective-permute-start.14 = (f32[64,128]{1,0:T(8,128)S(1)}, f32[64,128]{1,0:T(8,128)S(1)}, u32[]{:S(2)}, u32[]{:S(2)}) collective-permute-start(f32[64,128]{1,0:T(8,128)S(1)} %get-tuple-element.43), channel_id=1, source_target_pairs={{0,2},{1,3},{2,0},{3,1},{4,6},{5,7},{6,4},{7,5},{8,10},{9,11},{10,... | collective-permute-start | bytes 98312 | tf_op jit(solution)/shard_map/ppermute | solution.py:483
  51.3 3.7 %collective-permute-start.15 = (f32[64,128]{1,0:T(8,128)S(1)}, f32[64,128]{1,0:T(8,128)S(1)}, u32[]{:S(2)}, u32[]{:S(2)}) collective-permute-start(f32[64,128]{1,0:T(8,128)S(1)} %get-tuple-element.44), channel_id=1, source_target_pairs={{0,3},{1,2},{2,1},{3,0},{4,7},{5,6},{6,5},{7,4},{8,11},{9,10},{10,... | collective-permute-start | bytes 98312 | tf_op jit(solution)/shard_map/ppermute | solution.py:483

commit v5 on v4

--- a/solution.py
+++ b/solution.py
@@ -16,6 +16,7 @@
 SM = pltpu.SMEM
 GRANT = 16 * 1024 * 1024
 JOIN_GRANT = 1024 * 1024
+LOAD_GRANT = 8 * 1024 * 1024
 
 
 def iota(shape, axis):
@@ -123,20 +124,41 @@
         at += ref.shape[0]
 
 
-def load_kernel(pieces, source_ref, *refs):
-    target_ref, sems = refs[-2:]
-    size = target_ref.shape[0] // pieces
+def start_copies(source_ref, start, target_ref, sems, piece):
     copies = []
-    for i in range(pieces):
-        at = pl.ds(i * size, size)
-        copies.append(pltpu.make_async_copy(source_ref.at[at], target_ref.at[at], sems.at[i]))
+    for i in range(target_ref.shape[0] // piece):
+        copies.append(
+            pltpu.make_async_copy(
+                source_ref.at[pl.ds(start + i * piece, piece)],
+                target_ref.at[pl.ds(i * piece, piece)],
+                sems.at[i],
+            )
+        )
         copies[-1].start()
-    for copy in copies:
-        copy.wait()
+    return copies
+
+
+def load_kernel(jobs, unused, *refs):
+    sources, refs = refs[: len(jobs)], refs[len(jobs) + unused :]
+    targets, refs = refs[: len(jobs)], refs[len(jobs) :]
+    started = []
+    for (start, turned, piece), source, target in zip(jobs, sources, targets):
+        landing = target
+        if turned:
+            landing, refs = refs[0], refs[1:]
+        started.append((start_copies(source, start, landing, refs[0], piece), landing))
+        refs = refs[1:]
+    for (_, turned, piece), target, (copies, landing) in zip(jobs, targets, started):
+        for i, copy in enumerate(copies):
+            copy.wait()
+            if turned:
+                for slot in range(i * piece, (i + 1) * piece):
+                    target[slot] = landing[slot].T
 
 
 def tile_kernel(
     block,
+    loads,
     sub_count,
     packed,
     source_ref,
@@ -145,29 +167,20 @@
     pair_ref,
     mine_ref,
     other_ref,
-    damping_ref,
-    front_ref,
     stiffness_ref,
     *rest,
 ):
+    loaded, rest = rest[:loads], rest[loads:]
     if packed:
         gram_ref, rest = rest[0], rest[1:]
     outs, rest = rest[:sub_count], rest[sub_count:]
-    picked_ref, product_ref, buffer_ref, sems = rest[:4]
+    picked_ref, product_ref = rest[:2]
     tiles = pair_ref.shape[1] // 2
-    slots = damping_ref.shape[0]
+    slots = stiffness_ref.shape[0]
+    places = []
+    for ref in loaded:
+        places += [(ref, i) for i in range(ref.shape[0])]
     part_tiles = sub_count * tiles
-
-    half = slots // 2
-    copies = []
-    for i in range(half // block):
-        at = pl.ds(i * block, block)
-        copies.append(
-            pltpu.make_async_copy(
-                damping_ref.at[pl.ds(half + i * block, block)], buffer_ref.at[at], sems.at[i]
-            )
-        )
-        copies[-1].start()
 
     window = []
     for ref in (pair_ref, mine_ref, other_ref):
@@ -178,24 +191,27 @@
     chooser = jnp.where(iota((slots, depth), 1) == source_ref[...], 1.0, 0.0).astype(BF16)
     picked_ref[...] = jnp.dot(chooser, window, preferred_element_type=F32).astype(BF16)
 
-    dims = (((1,), (1,)), ((), ()))
     for step in range(slots // block):
-        at = pl.ds(step * block, block)
-        if step * block == half:
-            for copy in copies:
-                copy.wait()
-        ref = buffer_ref if step * block >= half else front_ref
-        left = ref[pl.ds(step * block % half, block)]
-        both = jnp.concatenate(
-            [value.reshape(block * LANES, LANES) for value in (left, stiffness_ref[at])], axis=1
-        )
-        result = lax.dot_general(picked_ref[at], both, dims, preferred_element_type=F32)
+        first = step * block
+        picked = picked_ref[pl.ds(first, block)]
         own = jnp.zeros((block, LANES), F32)
-        for t in range(block):
-            own = jnp.where(
-                iota((block, LANES), 0) == t, result[:, t * LANES : (t + 1) * LANES], own
+        for t in range(0, block, 2):
+            left, right = [], []
+            for slot in (first + t, first + t + 1):
+                ref, i = places[slot]
+                left.append(ref[i].T)
+                right.append(stiffness_ref[slot])
+            both = jnp.concatenate(
+                [jnp.concatenate(left, axis=1), jnp.concatenate(right, axis=1)], axis=0
             )
-        product_ref[at] = own
+            result = jnp.dot(picked, both, preferred_element_type=F32)
+            for e in range(2):
+                own = jnp.where(
+                    iota((block, LANES), 0) == t + e,
+                    result[:, e * LANES : (e + 1) * LANES],
+                    own,
+                )
+        product_ref[pl.ds(first, block)] = own
 
     selector = jnp.where(iota((part_tiles, slots), 0) == target_ref[...], 1.0, 0.0).astype(BF16)
     left = product_ref[...]
@@ -207,7 +223,7 @@
     for k in range(sub_count):
         outs[k][:tiles] = summed[k * tiles : (k + 1) * tiles]
     if packed:
-        square_ref = rest[4]
+        square_ref = rest[2]
         n = gram_ref.shape[0]
         square_ref[...] = jnp.zeros(square_ref.shape, F32)
         square_ref[:n, :n] = gram_ref[...]
@@ -415,21 +431,28 @@
     )(*values)
 
 
-def load(array, count, pieces, before):
-    shape = (count,) + array.shape[1:]
+def load(jobs, before):
+    outs, scratch, size = [], [], 0
+    for array, start, count, turned, piece in jobs:
+        assert count % piece == 0
+        shape = (count,) + array.shape[1:]
+        outs.append((shape, array.dtype))
+        scratch += [VM(shape, array.dtype)] * turned
+        scratch.append(pltpu.SemaphoreType.DMA((count // piece,)))
+        size += 4 * array.size * count // array.shape[0]
     return call(
-        functools.partial(load_kernel, pieces),
-        [(shape, array.dtype)],
-        [array] + before,
-        [pltpu.SemaphoreType.DMA((pieces,))],
-        far=(0,),
-        grant=JOIN_GRANT,
-        cost=pl.CostEstimate(
-            flops=0,
-            bytes_accessed=4 * array.size * count // array.shape[0],
-            transcendentals=0,
+        functools.partial(
+            load_kernel,
+            [(start, turned, piece) for _, start, _, turned, piece in jobs],
+            len(before),
         ),
-    )[0]
+        outs,
+        [job[0] for job in jobs] + before,
+        scratch,
+        far=tuple(range(len(jobs))),
+        grant=LOAD_GRANT,
+        cost=pl.CostEstimate(flops=0, bytes_accessed=size, transcendentals=0),
+    )
 
 
 def join(values, after):
@@ -509,7 +532,7 @@
     padding = ((0, 0), (0, height - compact.shape[1]), (0, LANES - compact.shape[2]))
     halves = jnp.pad(compact, padding)
     upper_half, lower_half = halves[0], halves[1]
-    pieces = slots // block
+    cut = (slots * 5 // 8, slots * 3 // 8)
     column = weights = added = None
     for iteration in range(ITERS):
         packed = iteration == 0
@@ -523,27 +546,26 @@
             _, late = lax.optimization_barrier((pair, basis))
             gram = jnp.dot(late, late.T, precision=lax.Precision.HIGHEST)
             before += [gram, source, target, upper_half, lower_half]
-        loaded = load(stiffness, slots, pieces, before)
-        mine = join(mine, loaded)
+        stiffness_loaded, early = load(
+            [(stiffness, 0, slots, True, 2 * block), (damping, 0, cut[0], False, block)], before
+        )
+        mine = join(mine, early)
         other = swap(mine, lambda r, s: (r, s ^ 1))
-        loaded_half = load(damping, slots // 2, pieces // 2, [mine])
+        (middle,) = load([(damping, cut[0], cut[1], False, block)], [mine])
         depth = tiles + SUBL if packed else tiles
         scratch = [
             VM((slots, 2 * LANES), BF16),
             VM((slots, LANES), F32),
-            VM((slots // 2, tile_size, tile_size), BF16),
-            pltpu.SemaphoreType.DMA((pieces // 2,)),
         ]
-        args = [source, target, quarter, pair, mine, other, damping, loaded_half, loaded]
+        args = [source, target, quarter, pair, mine, other, stiffness_loaded, early, middle]
         if packed:
             args.append(gram)
             scratch.append(VM((height, LANES), F32))
         parts = call(
-            functools.partial(tile_kernel, block, sub_count, packed),
+            functools.partial(tile_kernel, block, 2, sub_count, packed),
             [((depth, LANES), F32)] * sub_count,
             args,
             scratch,
-            far=(6,),
         )
         parts = [parts[0]] + [
             swap(parts[k], lambda r, s, k=k: (r, s ^ k)) for k in range(1, sub_count)

time: 66.9 us -> 64.6 us (0.966)
  waiting for transfers between devices: 7.97 us -> 6.96 us
  Pallas kernels: 18.5 us -> 17.5 us
    ppermute x16, waiting for transfers between devices: 7.97 us -> 6.96 us  [swap(): return lax.ppermute(value, every, pairs)]
    pallas_call x13, Pallas kernels: 18.5 us -> 17.5 us  [call(): pl.pallas_call(body, out_shape=[jax.ShapeDtypeStruct(shape, dtype) if fin...]
  transfers between devices with their start and end apart: 16 -> 16, of which waited for: 6 -> 5; matrix products, arithmetic and copies ran while one was open for 3% -> 3% of each run, Pallas kernels for 11% -> 14%
where the time goes in v5:
time: 64.6 us; the launch traced here: 64.4 us
  blocking collectives  22.9 us (35%)
  Pallas kernels  17.5 us (27%)
  starting transfers between devices  13.3 us (21%)
  waiting for transfers between devices  6.96 us (11%)
  matrix products  1.77 us (3%)
  between operations  1.55 us (2%)
    all_to_all x2, blocking collectives, on_device(): received = lax.all_to_all(sent, every, 0, 0)  22.9 us
    pallas_call x13, Pallas kernels, call(): pl.pallas_call(body, out_shape=[jax.ShapeDtypeStruct(shape, dtype) if fin...  17.5 us
    ppermute x16, starting transfers between devices, swap(): return lax.ppermute(value, every, pairs)  13.3 us
    ppermute x16, waiting for transfers between devices, swap(): return lax.ppermute(value, every, pairs)  6.96 us
    dot_general x1, matrix products, on_device(): gram = jnp.dot(late, late.T, precision=lax.Precision.HIGHEST)  1.77 us
  transfers between devices with their start and end apart: 16, of which 5 were waited for; matrix products, arithmetic and copies ran while one was open for 3% of the time, Pallas kernels for 14%

profile of v5, /device:TPU:0, one launch (start us, length us, event | category | flops | bytes accessed | tf_op | source)
XLA Modules:
  0.0 64.4 jit_solution(11696377984622061677)
XLA Ops:
  0.7 1.7 %shard_map.94 = (f32[64,128]{1,0:T(8,128)S(1)}, bf16[128,128]{1,0:T(8,128)(2,1)S(1)}, f32[58,8192]{1,0:T(8,128)S(1)}) custom-call(f32[57,2,58]{2,1,0:T(2,128)} %bitcast.26, f32[58,8192]{1,0:T(8,128)} %basis_ref.1), custom_call_target="tpu_custom_call" | custom-call | tf_op jit(solution)/shard_map/pallas_call | solution.py:420
  2.3 0.6 collective-permute-start
  2.9 2.6 %collective-permute-start.1 = (bf16[1,128,128]{2,1,0:T(8,128)(2,1)S(1)}, bf16[1,128,128]{2,1,0:T(8,128)(2,1)S(1)}, u32[]{:S(2)}, u32[]{:S(2)}) collective-permute-start(bf16[1,128,128]{2,1,0:T(8,128)(2,1)S(1)} %bitcast.30), channel_id=1, source_target_pairs={{0,2},{1,3},{2,0},{3,1},{4,6},{5,7},{6,4},{7,5},{8,10},{9,11},{10,... | collective-permute-start | bytes 98312 | tf_op jit(solution)/shard_map/ppermute | solution.py:506
  5.4 0.1 copy.14
  5.6 0.1 copy.10
  5.7 0.2 fusion.5.refs_4_.source_ref
  5.9 0.0 collective-permute-done
  5.9 1.7 %collective-permute-start.3 = (bf16[2,128,128]{2,1,0:T(8,128)(2,1)S(1)}, bf16[2,128,128]{2,1,0:T(8,128)(2,1)S(1)}, u32[]{:S(2)}, u32[]{:S(2)}) collective-permute-start(bf16[2,128,128]{2,1,0:T(8,128)(2,1)S(1)} %pad_maximum_fusion.refs_2_.pair_ref), channel_id=1, source_target_pairs={{0,6},{1,3},{2,4},{3,1},{4,2},{5,11},{6,0},{7,9},{8,14},{9,7},{10,... | collective-permute-start | bytes 196616 | tf_op jit(solution)/shard_map/ppermute | solution.py:506
  7.6 0.5 collective-permute-start.2
  8.1 1.8 %fusion.12.refs_3_.rest_2_ = f32[58,58]{1,0:T(8,128)S(1)} fusion(f32[58,8192]{1,0:T(8,128)S(1)} %get-tuple-element.36.refs_6_.refs_2_), kind=kOutput, calls=%fused_computation.32 | convolution fusion | flops 330694656 | bytes 1914000 | tf_op jit(solution)/shard_map/dot_general | solution.py:547
  9.9 3.2 %shard_map.95 = (bf16[128,128,128]{2,1,0:T(8,128)(2,1)S(1)}, bf16[80,128,128]{2,1,0:T(8,128)(2,1)S(1)}) custom-call(bf16[128,128,128]{2,1,0:T(8,128)(2,1)} %bitcast.38, bf16[128,128,128]{2,1,0:T(8,128)(2,1)} %bitcast.34, bf16[2,128,128]{2,1,0:T(8,128)(2,1)S(1)} %pad_maximum_fusion.refs_2_.pair_ref, f32[58,58]{1,0:T(8,128)S(1)} %fusion.12.refs_3_.rest_2_, ...), custom_call_target="tpu_custom_call" | custom-call | bytes 13631488 | tf_op jit(solution)/shard_map/pallas_call | solution.py:420
  13.1 0.0 collective-permute-done.1.refs_0_
  13.1 0.0 collective-permute-done.3.refs_2_
  13.1 0.0 collective-permute-done.2.refs_1_
  13.2 0.1 collective-permute-start.4
  13.3 1.4 %shard_map.97.rest_1_ = bf16[48,128,128]{2,1,0:T(8,128)(2,1)S(1)} custom-call(bf16[128,128,128]{2,1,0:T(8,128)(2,1)} %bitcast.35, bf16[5,128,128]{2,1,0:T(8,128)(2,1)S(1)} %shard_map.96.refs_1_.mine_ref), custom_call_target="tpu_custom_call" | custom-call | bytes 3145728 | tf_op jit(solution)/shard_map/pallas_call | solution.py:420
  14.7 0.0 collective-permute-done.4.other_ref
  14.7 0.0 copy-start.1
  14.7 1.7 %shard_map.98 = (f32[72,128]{1,0:T(8,128)S(1)}, f32[72,128]{1,0:T(8,128)S(1)}, f32[72,128]{1,0:T(8,128)S(1)}, f32[72,128]{1,0:T(8,128)S(1)}) custom-call(s32[128,1]{1,0:T(8,128)S(1)} %fusion.5.refs_4_.source_ref, s32[1,128]{1,0:T(1,128)S(1)} %get-tuple-element.67.refs_5_.target_ref, s32[1]{0:T(128)} %bitcast.3.quarter_ref, ...), custom_call_target="tpu_custom_call" | custom-call | tf_op jit(solution)/shard_map/pallas_call | solution.py:420
  16.4 0.6 collective-permute-start.5
  16.9 1.4 %collective-permute-start.6 = (f32[72,128]{1,0:T(8,128)S(1)}, f32[72,128]{1,0:T(8,128)S(1)}, u32[]{:S(2)}, u32[]{:S(2)}) collective-permute-start(f32[72,128]{1,0:T(8,128)S(1)} %get-tuple-element.41), channel_id=1, source_target_pairs={{0,2},{1,3},{2,0},{3,1},{4,6},{5,7},{6,4},{7,5},{8,10},{9,11},{10,... | collective-permute-start | bytes 110600 | tf_op jit(solution)/shard_map/ppermute | solution.py:506
  18.3 0.1 collective-permute-start.7
  19.0 0.0 collective-permute-done.5.refs_1_
  19.0 1.9 %collective-permute-done.6.refs_2_ = f32[72,128]{1,0:T(8,128)S(1)} collective-permute-done((f32[72,128]{1,0:T(8,128)S(1)}, f32[72,128]{1,0:T(8,128)S(1)}, u32[]{:S(2)}, u32[]{:S(2)}) %collective-permute-start.6) | collective-permute-done | bytes 36896 | tf_op jit(solution)/shard_map/ppermute | solution.py:506
  20.9 1.2 %collective-permute-done.7.refs_3_ = f32[72,128]{1,0:T(8,128)S(1)} collective-permute-done((f32[72,128]{1,0:T(8,128)S(1)}, f32[72,128]{1,0:T(8,128)S(1)}, u32[]{:S(2)}, u32[]{:S(2)}) %collective-permute-start.7) | collective-permute-done | bytes 36896 | tf_op jit(solution)/shard_map/ppermute | solution.py:506
  22.0 0.3 shard_map.99
  22.4 13.1 %all_to_all.10.refs_0_ = f32[32,8,128]{2,1,0:T(8,128)S(1)} all-to-all(f32[32,8,128]{2,1,0:T(8,128)S(1)} %get-tuple-element.44), channel_id=1, replica_groups=mesh['rows'=8,'sub'=4] {'rows','sub'}, dimensions={0} | all-to-all | bytes 262144 | tf_op jit(solution)/shard_map/all_to_all | solution.py:580
  35.4 1.2 %shard_map.100 = (f32[64,128]{1,0:T(8,128)S(1)}, f32[64,128]{1,0:T(8,128)S(1)}, bf16[128,128]{1,0:T(8,128)(2,1)S(1)}, f32[64,128]{1,0:T(8,128)S(1)}, f32[64,128]...) custom-call(f32[1]{0:T(128)} %bitcast.23.shift_ref, ...), custom_call_target="tpu_custom_call" | custom-call | tf_op jit(solution)/shard_map/pallas_call | solution.py:420
  36.6 0.3 collective-permute-start.8
  36.9 1.0 %collective-permute-done.8 = bf16[128,128]{1,0:T(8,128)(2,1)S(1)} collective-permute-done((bf16[128,128]{1,0:T(8,128)(2,1)S(1)}, bf16[128,128]{1,0:T(8,128)(2,1)S(1)}, u32[]{:S(2)}, u32[]{:S(2)}) %collective-permute-start.8) | collective-permute-done | bytes 32800 | tf_op jit(solution)/shard_map/ppermute | solution.py:506
  37.9 0.9 %collective-permute-start.11 = (bf16[2,128,128]{2,1,0:T(8,128)(2,1)S(1)}, bf16[2,128,128]{2,1,0:T(8,128)(2,1)S(1)}, u32[]{:S(2)}, u32[]{:S(2)}) collective-permute-start(bf16[2,128,128]{2,1,0:T(8,128)(2,1)S(1)} %pad_maximum_fusion.1.refs_2_.pair_ref), channel_id=1, source_target_pairs={{0,6},{1,3},{2,4},{3,1},{4,2},{5,11},{6,0},{7,9},{8,14},{9,7},{10,... | collective-permute-start | bytes 196616 | tf_op jit(solution)/shard_map/ppermute | solution.py:506
  38.8 0.9 %collective-permute-start.10 = (bf16[2,128,128]{2,1,0:T(8,128)(2,1)S(1)}, bf16[2,128,128]{2,1,0:T(8,128)(2,1)S(1)}, u32[]{:S(2)}, u32[]{:S(2)}) collective-permute-start(bf16[2,128,128]{2,1,0:T(8,128)(2,1)S(1)} %pad_maximum_fusion.1.refs_2_.pair_ref), channel_id=1, source_target_pairs={{0,4},{1,3},{2,6},{3,1},{4,0},{5,9},{6,2},{7,11},{8,12},{9,5},{10,... | collective-permute-start | bytes 196616 | tf_op jit(solution)/shard_map/ppermute | solution.py:506
  39.8 1.7 %collective-permute-start.9 = (bf16[1,128,128]{2,1,0:T(8,128)(2,1)S(1)}, bf16[1,128,128]{2,1,0:T(8,128)(2,1)S(1)}, u32[]{:S(2)}, u32[]{:S(2)}) collective-permute-start(bf16[1,128,128]{2,1,0:T(8,128)(2,1)S(1)} %bitcast.33), channel_id=1, source_target_pairs={{0,2},{1,3},{2,0},{3,1},{4,6},{5,7},{6,4},{7,5},{8,10},{9,11},{10,... | collective-permute-start | bytes 98312 | tf_op jit(solution)/shard_map/ppermute | solution.py:506
  41.5 3.2 %shard_map.101 = (bf16[128,128,128]{2,1,0:T(8,128)(2,1)S(1)}, bf16[80,128,128]{2,1,0:T(8,128)(2,1)S(1)}) custom-call(bf16[128,128,128]{2,1,0:T(8,128)(2,1)} %bitcast.39, bf16[128,128,128]{2,1,0:T(8,128)(2,1)} %bitcast.36, bf16[2,128,128]{2,1,0:T(8,128)(2,1)S(1)} %pad_maximum_fusion.1.refs_2_.pair_ref), custom_call_target="tpu_custom_call" | custom-call | bytes 13631488 | tf_op jit(solution)/shard_map/pallas_call | solution.py:420
  44.7 0.0 collective-permute-done.10.refs_1_
  44.7 0.1 collective-permute-start.12
  44.8 1.4 %shard_map.103.rest_1_ = bf16[48,128,128]{2,1,0:T(8,128)(2,1)S(1)} custom-call(bf16[128,128,128]{2,1,0:T(8,128)(2,1)} %bitcast.37, bf16[5,128,128]{2,1,0:T(8,128)(2,1)S(1)} %shard_map.102.refs_1_.mine_ref), custom_call_target="tpu_custom_call" | custom-call | bytes 3145728 | tf_op jit(solution)/shard_map/pallas_call | solution.py:420
  46.2 0.0 collective-permute-done.12.other_ref
  46.2 1.7 %shard_map.104 = (f32[64,128]{1,0:T(8,128)S(1)}, f32[64,128]{1,0:T(8,128)S(1)}, f32[64,128]{1,0:T(8,128)S(1)}, f32[64,128]{1,0:T(8,128)S(1)}) custom-call(s32[128,1]{1,0:T(8,128)S(1)} %fusion.5.refs_4_.source_ref, s32[1,128]{1,0:T(1,128)S(1)} %get-tuple-element.67.refs_5_.target_ref, s32[1]{0:T(128)} %bitcast.3.quarter_ref, ...), custom_call_target="tpu_custom_call" | custom-call | tf_op jit(solution)/shard_map/pallas_call | solution.py:420
  47.9 0.6 collective-permute-start.13
  48.4 0.7 %collective-permute-start.14 = (f32[64,128]{1,0:T(8,128)S(1)}, f32[64,128]{1,0:T(8,128)S(1)}, u32[]{:S(2)}, u32[]{:S(2)}) collective-permute-start(f32[64,128]{1,0:T(8,128)S(1)} %get-tuple-element.51), channel_id=1, source_target_pairs={{0,2},{1,3},{2,0},{3,1},{4,6},{5,7},{6,4},{7,5},{8,10},{9,11},{10,... | collective-permute-start | bytes 98312 | tf_op jit(solution)/shard_map/ppermute | solution.py:506
  49.1 0.8 %collective-permute-start.15 = (f32[64,128]{1,0:T(8,128)S(1)}, f32[64,128]{1,0:T(8,128)S(1)}, u32[]{:S(2)}, u32[]{:S(2)}) collective-permute-start(f32[64,128]{1,0:T(8,128)S(1)} %get-tuple-element.52), channel_id=1, source_target_pairs={{0,3},{1,2},{2,1},{3,0},{4,7},{5,6},{6,5},{7,4},{8,11},{9,10},{10,... | collective-permute-start | bytes 98312 | tf_op jit(solution)/shard_map/ppermute | solution.py:506
  49.9 0.0 collective-permute-done.13.refs_1_
  49.9 2.7 %collective-permute-done.14.refs_2_ = f32[64,128]{1,0:T(8,128)S(1)} collective-permute-done((f32[64,128]{1,0:T(8,128)S(1)}, f32[64,128]{1,0:T(8,128)S(1)}, u32[]{:S(2)}, u32[]{:S(2)}) %collective-permute-start.14) | collective-permute-done | bytes 32800 | tf_op jit(solution)/shard_map/ppermute | solution.py:506
  52.6 0.2 collective-permute-done.15.refs_3_
  52.8 0.4 shard_map.105
  53.2 9.8 %all_to_all.11.refs_0_ = f32[32,1,128]{2,1,0:T(1,128)S(1)} all-to-all(f32[32,1,128]{2,1,0:T(1,128)S(1)} %get-tuple-element.55), channel_id=1, replica_groups=mesh['rows'=8,'sub'=4] {'rows','sub'}, dimensions={0} | all-to-all | bytes 32768 | tf_op jit(solution)/shard_map/all_to_all | solution.py:580
  63.0 1.3 %shard_map.106 = (f32[2,8192]{1,0:T(2,128)}, f32[59,2,60]{2,1,0:T(2,128)}, f32[2,59]{1,0:T(2,128)}) custom-call(f32[1]{0:T(128)} %bitcast.25.shift_ref, f32[32,1,128]{2,1,0:T(1,128)S(1)} %all_to_all.11.refs_0_, f32[64,128]{1,0:T(8,128)S(1)} %get-tuple-element.56.refs_1_, f32[58,8192]{1,0:T(8,128)S(1)} %get-tuple-element.36.refs_6_.refs_2_, ...), custom_call_target="tpu_custom_call" | custom-call | tf_op jit(solution)/shard_map/pallas_call | solution.py:420
  (13 shorter events, 0.1 us)
Async XLA Ops:
  0.6 4.8 %copy-start = (f32[2,58,57]{1,0,2:T(2,128)S(1)}, f32[2,58,57]{1,0,2:T(2,128)}, u32[]{:S(2)}) copy-start(f32[2,58,57]{1,0,2:T(2,128)} %param.13) | copy-start | bytes 79348
  0.6 4.9 %copy-start.2 = (s32[1,1,2,128]{3,2,1,0:T(2,128)S(1)}, s32[1,1,2,128]{3,2,1,0:T(2,128)}, u32[]{:S(2)}) copy-start(s32[1,1,2,128]{3,2,1,0:T(2,128)} %param.9) | copy-start | bytes 3076
  2.3 3.6 %collective-permute-start = (bf16[128,128]{1,0:T(8,128)(2,1)S(1)}, bf16[128,128]{1,0:T(8,128)(2,1)S(1)}, u32[]{:S(2)}, u32[]{:S(2)}) collective-permute-start(bf16[128,128]{1,0:T(8,128)(2,1)S(1)} %get-tuple-element.34), channel_id=1, source_target_pairs={{0,1},{1,0},{2,3},{3,2},{4,5},{5,4},{6,7},{7,6},{8,9},{9,8},{10,11... | collective-permute-start | bytes 98312 | tf_op jit(solution)/shard_map/ppermute | solution.py:506
  2.9 10.2 %collective-permute-start.1 = (bf16[1,128,128]{2,1,0:T(8,128)(2,1)S(1)}, bf16[1,128,128]{2,1,0:T(8,128)(2,1)S(1)}, u32[]{:S(2)}, u32[]{:S(2)}) collective-permute-start(bf16[1,128,128]{2,1,0:T(8,128)(2,1)S(1)} %bitcast.30), channel_id=1, source_target_pairs={{0,2},{1,3},{2,0},{3,1},{4,6},{5,7},{6,4},{7,5},{8,10},{9,11},{10,... | collective-permute-start | bytes 98312 | tf_op jit(solution)/shard_map/ppermute | solution.py:506
  5.9 7.2 %collective-permute-start.3 = (bf16[2,128,128]{2,1,0:T(8,128)(2,1)S(1)}, bf16[2,128,128]{2,1,0:T(8,128)(2,1)S(1)}, u32[]{:S(2)}, u32[]{:S(2)}) collective-permute-start(bf16[2,128,128]{2,1,0:T(8,128)(2,1)S(1)} %pad_maximum_fusion.refs_2_.pair_ref), channel_id=1, source_target_pairs={{0,6},{1,3},{2,4},{3,1},{4,2},{5,11},{6,0},{7,9},{8,14},{9,7},{10,... | collective-permute-start | bytes 196616 | tf_op jit(solution)/shard_map/ppermute | solution.py:506
  7.6 5.5 %collective-permute-start.2 = (bf16[2,128,128]{2,1,0:T(8,128)(2,1)S(1)}, bf16[2,128,128]{2,1,0:T(8,128)(2,1)S(1)}, u32[]{:S(2)}, u32[]{:S(2)}) collective-permute-start(bf16[2,128,128]{2,1,0:T(8,128)(2,1)S(1)} %pad_maximum_fusion.refs_2_.pair_ref), channel_id=1, source_target_pairs={{0,4},{1,3},{2,6},{3,1},{4,0},{5,9},{6,2},{7,11},{8,12},{9,5},{10,... | collective-permute-start | bytes 196616 | tf_op jit(solution)/shard_map/ppermute | solution.py:506
  13.2 1.5 %collective-permute-start.4 = (bf16[5,128,128]{2,1,0:T(8,128)(2,1)S(1)}, bf16[5,128,128]{2,1,0:T(8,128)(2,1)S(1)}, u32[]{:S(2)}, u32[]{:S(2)}) collective-permute-start(bf16[5,128,128]{2,1,0:T(8,128)(2,1)S(1)} %shard_map.96.refs_1_.mine_ref), channel_id=1, source_target_pairs={{0,1},{1,0},{2,3},{3,2},{4,5},{5,4},{6,7},{7,6},{8,9},{9,8},{10,11... | collective-permute-start | bytes 491528 | tf_op jit(solution)/shard_map/ppermute | solution.py:506
  14.7 7.4 %copy-start.1 = (f32[8192]{0:T(1024)S(1)}, f32[8192]{0:T(1024)}, u32[]{:S(2)}) copy-start(f32[8192]{0:T(1024)} %param.10) | copy-start | bytes 98308
  16.4 2.6 %collective-permute-start.5 = (f32[72,128]{1,0:T(8,128)S(1)}, f32[72,128]{1,0:T(8,128)S(1)}, u32[]{:S(2)}, u32[]{:S(2)}) collective-permute-start(f32[72,128]{1,0:T(8,128)S(1)} %get-tuple-element.40), channel_id=1, source_target_pairs={{0,1},{1,0},{2,3},{3,2},{4,5},{5,4},{6,7},{7,6},{8,9},{9,8},{10,11... | collective-permute-start | bytes 110600 | tf_op jit(solution)/shard_map/ppermute | solution.py:506
  16.9 4.0 %collective-permute-start.6 = (f32[72,128]{1,0:T(8,128)S(1)}, f32[72,128]{1,0:T(8,128)S(1)}, u32[]{:S(2)}, u32[]{:S(2)}) collective-permute-start(f32[72,128]{1,0:T(8,128)S(1)} %get-tuple-element.41), channel_id=1, source_target_pairs={{0,2},{1,3},{2,0},{3,1},{4,6},{5,7},{6,4},{7,5},{8,10},{9,11},{10,... | collective-permute-start | bytes 110600 | tf_op jit(solution)/shard_map/ppermute | solution.py:506
  18.3 3.8 %collective-permute-start.7 = (f32[72,128]{1,0:T(8,128)S(1)}, f32[72,128]{1,0:T(8,128)S(1)}, u32[]{:S(2)}, u32[]{:S(2)}) collective-permute-start(f32[72,128]{1,0:T(8,128)S(1)} %get-tuple-element.42), channel_id=1, source_target_pairs={{0,3},{1,2},{2,1},{3,0},{4,7},{5,6},{6,5},{7,4},{8,11},{9,10},{10,... | collective-permute-start | bytes 110600 | tf_op jit(solution)/shard_map/ppermute | solution.py:506
  36.6 1.3 %collective-permute-start.8 = (bf16[128,128]{1,0:T(8,128)(2,1)S(1)}, bf16[128,128]{1,0:T(8,128)(2,1)S(1)}, u32[]{:S(2)}, u32[]{:S(2)}) collective-permute-start(bf16[128,128]{1,0:T(8,128)(2,1)S(1)} %get-tuple-element.46), channel_id=1, source_target_pairs={{0,1},{1,0},{2,3},{3,2},{4,5},{5,4},{6,7},{7,6},{8,9},{9,8},{10,11... | collective-permute-start | bytes 98312 | tf_op jit(solution)/shard_map/ppermute | solution.py:506
  37.9 6.8 %collective-permute-start.11 = (bf16[2,128,128]{2,1,0:T(8,128)(2,1)S(1)}, bf16[2,128,128]{2,1,0:T(8,128)(2,1)S(1)}, u32[]{:S(2)}, u32[]{:S(2)}) collective-permute-start(bf16[2,128,128]{2,1,0:T(8,128)(2,1)S(1)} %pad_maximum_fusion.1.refs_2_.pair_ref), channel_id=1, source_target_pairs={{0,6},{1,3},{2,4},{3,1},{4,2},{5,11},{6,0},{7,9},{8,14},{9,7},{10,... | collective-permute-start | bytes 196616 | tf_op jit(solution)/shard_map/ppermute | solution.py:506
  38.8 5.9 %collective-permute-start.10 = (bf16[2,128,128]{2,1,0:T(8,128)(2,1)S(1)}, bf16[2,128,128]{2,1,0:T(8,128)(2,1)S(1)}, u32[]{:S(2)}, u32[]{:S(2)}) collective-permute-start(bf16[2,128,128]{2,1,0:T(8,128)(2,1)S(1)} %pad_maximum_fusion.1.refs_2_.pair_ref), channel_id=1, source_target_pairs={{0,4},{1,3},{2,6},{3,1},{4,0},{5,9},{6,2},{7,11},{8,12},{9,5},{10,... | collective-permute-start | bytes 196616 | tf_op jit(solution)/shard_map/ppermute | solution.py:506
  39.8 4.9 %collective-permute-start.9 = (bf16[1,128,128]{2,1,0:T(8,128)(2,1)S(1)}, bf16[1,128,128]{2,1,0:T(8,128)(2,1)S(1)}, u32[]{:S(2)}, u32[]{:S(2)}) collective-permute-start(bf16[1,128,128]{2,1,0:T(8,128)(2,1)S(1)} %bitcast.33), channel_id=1, source_target_pairs={{0,2},{1,3},{2,0},{3,1},{4,6},{5,7},{6,4},{7,5},{8,10},{9,11},{10,... | collective-permute-start | bytes 98312 | tf_op jit(solution)/shard_map/ppermute | solution.py:506
  44.7 1.5 %collective-permute-start.12 = (bf16[5,128,128]{2,1,0:T(8,128)(2,1)S(1)}, bf16[5,128,128]{2,1,0:T(8,128)(2,1)S(1)}, u32[]{:S(2)}, u32[]{:S(2)}) collective-permute-start(bf16[5,128,128]{2,1,0:T(8,128)(2,1)S(1)} %shard_map.102.refs_1_.mine_ref), channel_id=1, source_target_pairs={{0,1},{1,0},{2,3},{3,2},{4,5},{5,4},{6,7},{7,6},{8,9},{9,8},{10,11... | collective-permute-start | bytes 491528 | tf_op jit(solution)/shard_map/ppermute | solution.py:506
  47.9 2.0 %collective-permute-start.13 = (f32[64,128]{1,0:T(8,128)S(1)}, f32[64,128]{1,0:T(8,128)S(1)}, u32[]{:S(2)}, u32[]{:S(2)}) collective-permute-start(f32[64,128]{1,0:T(8,128)S(1)} %get-tuple-element.50), channel_id=1, source_target_pairs={{0,1},{1,0},{2,3},{3,2},{4,5},{5,4},{6,7},{7,6},{8,9},{9,8},{10,11... | collective-permute-start | bytes 98312 | tf_op jit(solution)/shard_map/ppermute | solution.py:506
  48.4 4.2 %collective-permute-start.14 = (f32[64,128]{1,0:T(8,128)S(1)}, f32[64,128]{1,0:T(8,128)S(1)}, u32[]{:S(2)}, u32[]{:S(2)}) collective-permute-start(f32[64,128]{1,0:T(8,128)S(1)} %get-tuple-element.51), channel_id=1, source_target_pairs={{0,2},{1,3},{2,0},{3,1},{4,6},{5,7},{6,4},{7,5},{8,10},{9,11},{10,... | collective-permute-start | bytes 98312 | tf_op jit(solution)/shard_map/ppermute | solution.py:506
  49.1 3.7 %collective-permute-start.15 = (f32[64,128]{1,0:T(8,128)S(1)}, f32[64,128]{1,0:T(8,128)S(1)}, u32[]{:S(2)}, u32[]{:S(2)}) collective-permute-start(f32[64,128]{1,0:T(8,128)S(1)} %get-tuple-element.52), channel_id=1, source_target_pairs={{0,3},{1,2},{2,1},{3,0},{4,7},{5,6},{6,5},{7,4},{8,11},{9,10},{10,... | collective-permute-start | bytes 98312 | tf_op jit(solution)/shard_map/ppermute | solution.py:506
